TPU v7x, 32 devices: a whole 2x2x4 slice. The times are simulated.
32 devices in a mesh: dp: 16 (over z, y, core), mp: 2 (over x).
Axes of the slice: x: 2, y: 2, z: 4, core: 2. Of those that a mesh axis runs over, the one named last changes fastest.
Arguments:
- tokens: bfloat16 [32, 1024, 1024], P('dp', 'mp'), may hold values from -6 to 6
- cotangent: bfloat16 [32, 1024, 1024], P('dp', 'mp'), may hold values from -6 to 6
- buckets: int32 [32], P('dp'), may hold values from 0 to 7
- counts: int32 [8], replicated, may hold values from 1000 to 3999
- lead_table: bfloat16 [8, 1024], replicated, may hold values from -3 to 3
- norm1_gain: bfloat16 [1024], replicated, may hold values from 0.25 to 1.75
- norm1_shift: bfloat16 [1024], replicated, may hold values from -1 to 1
- w_qkv: bfloat16 [1024, 3, 1024], P(None, None, 'mp'), may hold values from -0.1875 to 0.1875
- qv_bias: bfloat16 [2, 1024], P(None, 'mp'), may hold values from -0.59765625 to 0.59765625
- w_out: bfloat16 [1024, 1024], P('mp'), may hold values from -1.5 to 1.5
- out_bias: bfloat16 [1024], replicated, may hold values from -1 to 1
- norm2_gain: bfloat16 [1024], replicated, may hold values from 0.25 to 1.75
- norm2_shift: bfloat16 [1024], replicated, may hold values from -1 to 1
- w_fc1: bfloat16 [1024, 4096], P(None, 'mp'), may hold values from -0.1875 to 0.1875
- fc1_bias: bfloat16 [4096], P('mp'), may hold values from -1.5 to 1.5
- w_fc2: bfloat16 [4096, 1024], P('mp'), may hold values from -0.09375 to 0.09375
- fc2_bias: bfloat16 [1024], replicated, may hold values from -1 to 1
Outputs:
- block_output: bfloat16 [32, 1024, 1024], P('dp', 'mp')
- input_grad: float32 [32, 1024, 1024], P('dp', 'mp')
- lead_grad: float32 [8, 1024], replicated
- norm1_gain_grad: float32 [1024], replicated
- norm1_shift_grad: float32 [1024], replicated
- qkv_grad: float32 [1024, 3, 1024], P(None, None, 'mp')
- qv_bias_grad: float32 [2, 1024], P(None, 'mp')
- out_grad: float32 [1024, 1024], P('mp')
- out_bias_grad: float32 [1024], replicated
- norm2_gain_grad: float32 [1024], replicated
- norm2_shift_grad: float32 [1024], replicated
- fc1_grad: float32 [1024, 4096], P(None, 'mp')
- fc1_bias_grad: float32 [4096], P('mp')
- fc2_grad: float32 [4096, 1024], P('mp')
- fc2_bias_grad: float32 [1024], replicated
All inputs are finite; a program needn't handle non-finite values.
Results may differ from a plain program's by a relative error of at most 0.02.
Values may be sent and summed in bfloat16 or wider, within the bound.
No kernel may reach another device: no remote copies, remote signals or barrier semaphores. Data moves between devices by JAX's collectives and lax.ppermute only.
A program may use at most 320 MiB of HBM per device.

v0:
```python
import jax
import jax.numpy as jnp
from jax import lax
from jax.sharding import PartitionSpec as P

HD = 64


EPS = 1e-05


def norm_forward(values, norm_gain, norm_shift):
    center = values - jnp.mean(values, axis=-1, keepdims=True)
    inverse = lax.rsqrt(jnp.mean(center * center, axis=-1, keepdims=True) + EPS)
    scaled = center * inverse
    return (scaled * norm_gain + norm_shift, scaled, inverse)


def norm_backward(grad_out, scaled, inverse, norm_gain):
    grad_scaled = grad_out * norm_gain
    grad_mean = jnp.mean(grad_scaled, axis=-1, keepdims=True)
    cross_mean = jnp.mean(grad_scaled * scaled, axis=-1, keepdims=True)
    grad_in = inverse * (grad_scaled - grad_mean - scaled * cross_mean)
    gain_grad = jnp.sum(grad_out * scaled, axis=(0, 1))
    shift_grad = jnp.sum(grad_out, axis=(0, 1))
    return (grad_in, gain_grad, shift_grad)


def gelu_slope(pre_act):
    normal_cdf = 0.5 * (1.0 + lax.erf(pre_act * 0.7071067811865476))
    return normal_cdf + pre_act * jnp.exp(-0.5 * pre_act * pre_act) * 0.3989422804014327


def attention_forward(query_all, key_all, value_all, block_rows):
    block_count = query_all.shape[0] // block_rows
    query_blocks = query_all.reshape((block_count, block_rows) + query_all.shape[1:])

    def one_block(query_block):
        scores = (
            jnp.einsum("qshd,kshd->shqk", query_block, key_all, preferred_element_type=jnp.float32)
            * 0.125
        )
        row_max = jnp.max(scores, axis=-1, keepdims=True)
        powers = jnp.exp(scores - row_max)
        exp_total = jnp.sum(powers, axis=-1, keepdims=True)
        attn_weights = (powers / exp_total).astype(jnp.bfloat16)
        attended = jnp.einsum(
            "shqk,kshd->qshd", attn_weights, value_all, preferred_element_type=jnp.float32
        )
        return (attended.astype(jnp.bfloat16), (row_max + jnp.log(exp_total))[..., 0])

    attended, log_total = lax.map(one_block, query_blocks)
    return (attended.reshape(query_all.shape), log_total)


def attention_backward(query_all, key_all, value_all, grad_attended, log_total, block_rows):
    block_count = query_all.shape[0] // block_rows
    query_blocks = query_all.reshape((block_count, block_rows) + query_all.shape[1:])
    grad_blocks = grad_attended.reshape((block_count, block_rows) + query_all.shape[1:])

    def one_block(running, sliced):
        key_grad, value_grad = running
        query_block, grad_block, log_block = sliced
        scores = (
            jnp.einsum("qshd,kshd->shqk", query_block, key_all, preferred_element_type=jnp.float32)
            * 0.125
        )
        attn_weights = jnp.exp(scores - log_block[..., None])
        weight_low = attn_weights.astype(jnp.bfloat16)
        grad_weights = jnp.einsum(
            "qshd,kshd->shqk", grad_block, value_all, preferred_element_type=jnp.float32
        )
        inner = jnp.sum(attn_weights * grad_weights, axis=-1, keepdims=True)
        grad_scores = (attn_weights * (grad_weights - inner)).astype(jnp.bfloat16)
        query_grad = (
            jnp.einsum("shqk,kshd->qshd", grad_scores, key_all, preferred_element_type=jnp.float32)
            * 0.125
        )
        key_grad = (
            key_grad
            + jnp.einsum(
                "shqk,qshd->kshd", grad_scores, query_block, preferred_element_type=jnp.float32
            )
            * 0.125
        )
        value_grad = value_grad + jnp.einsum(
            "shqk,qshd->kshd", weight_low, grad_block, preferred_element_type=jnp.float32
        )
        return ((key_grad, value_grad), query_grad.astype(jnp.bfloat16))

    zero_grad = jnp.zeros(key_all.shape, jnp.float32)
    (key_grad, value_grad), query_grad = lax.scan(
        one_block, (zero_grad, zero_grad), (query_blocks, grad_blocks, log_total)
    )
    return (
        query_grad.reshape(query_all.shape),
        key_grad.astype(jnp.bfloat16),
        value_grad.astype(jnp.bfloat16),
    )


def body(
    tokens,
    cotangent,
    buckets,
    counts,
    lead_table,
    norm1_gain,
    norm1_shift,
    w_qkv,
    qv_bias,
    w_out,
    out_bias,
    norm2_gain,
    norm2_shift,
    w_fc1,
    fc1_bias,
    w_fc2,
    fc2_bias,
):
    samples_here = tokens.shape[0]
    local_rows = tokens.shape[1]
    local_width = w_qkv.shape[2]
    local_heads = local_width // HD
    seq_len = local_rows * lax.axis_size("mp")
    block_rows = min(512, seq_len)
    head_shape = (seq_len, samples_here, local_heads, HD)
    count_f = counts.astype(jnp.float32)
    onehot = (buckets[:, None] == jnp.arange(counts.shape[0], dtype=jnp.int32)[None, :]).astype(
        jnp.float32
    )
    loss_weight = jnp.mean(count_f) / jnp.sum(onehot * count_f[None, :], axis=1)
    lead_rows = jnp.dot(
        onehot,
        lead_table.astype(jnp.float32),
        precision=lax.Precision.HIGHEST,
        preferred_element_type=jnp.float32,
    )
    shifted = jnp.swapaxes(tokens, 0, 1).astype(jnp.float32) + lead_rows[None]
    normed_one, scaled_one, inverse_one = norm_forward(
        shifted, norm1_gain.astype(jnp.float32), norm1_shift.astype(jnp.float32)
    )
    normed_one = normed_one.astype(jnp.bfloat16)
    normed_full = lax.all_gather(normed_one, "mp", axis=0, tiled=True)
    project = jnp.einsum("tsd,dcf->tscf", normed_full, w_qkv, preferred_element_type=jnp.float32)
    bias_f = qv_bias.astype(jnp.float32)
    query_all = (project[:, :, 0] + bias_f[0]).astype(jnp.bfloat16).reshape(head_shape)
    key_all = project[:, :, 1].astype(jnp.bfloat16).reshape(head_shape)
    value_all = (project[:, :, 2] + bias_f[1]).astype(jnp.bfloat16).reshape(head_shape)
    attended, log_total = attention_forward(query_all, key_all, value_all, block_rows)
    attended_flat = attended.reshape(seq_len, samples_here, local_width)
    picked = attended_flat
    branch = lax.psum_scatter(
        jnp.einsum("tsf,fd->tsd", picked, w_out, preferred_element_type=jnp.float32),
        "mp",
        scatter_dimension=0,
        tiled=True,
    )
    middle = shifted + branch + out_bias.astype(jnp.float32)
    gain_two = norm2_gain.astype(jnp.float32)
    normed_two, scaled_two, inverse_two = norm_forward(
        middle, gain_two, norm2_shift.astype(jnp.float32)
    )
    normed_two = normed_two.astype(jnp.bfloat16)
    grad_top = jnp.swapaxes(cotangent, 0, 1).astype(jnp.float32) * loss_weight[None, :, None]
    grad_low = grad_top.astype(jnp.bfloat16)
    fc1_full, fc1_bias_full, fc2_full = (
        lax.all_gather(w_fc1, "mp", axis=1, tiled=True),
        lax.all_gather(fc1_bias, "mp", axis=0, tiled=True),
        lax.all_gather(w_fc2, "mp", axis=0, tiled=True),
    )
    pre_act = jnp.einsum(
        "tsd,df->tsf", normed_two, fc1_full, preferred_element_type=jnp.float32
    ) + fc1_bias_full.astype(jnp.float32)
    hidden = jax.nn.gelu(pre_act, approximate=False).astype(jnp.bfloat16)
    mlp_branch = jnp.einsum("tsf,fd->tsd", hidden, fc2_full, preferred_element_type=jnp.float32)
    output = middle + mlp_branch + fc2_bias.astype(jnp.float32)
    grad_hidden = jnp.einsum("tsd,fd->tsf", grad_low, fc2_full, preferred_element_type=jnp.float32)
    grad_pre = (grad_hidden * gelu_slope(pre_act)).astype(jnp.bfloat16)
    grad_normed_two = jnp.einsum(
        "tsf,df->tsd", grad_pre, fc1_full, preferred_element_type=jnp.float32
    )
    fc1_part = jnp.einsum("tsd,tsf->df", normed_two, grad_pre, preferred_element_type=jnp.float32)
    fc1_bias_part = jnp.sum(grad_pre.astype(jnp.float32), axis=(0, 1))
    fc2_part = jnp.einsum("tsf,tsd->fd", hidden, grad_low, preferred_element_type=jnp.float32)
    fc1_grad, fc1_bias_grad, fc2_grad = (
        lax.psum_scatter(
            fc1_part.astype(jnp.bfloat16), "mp", scatter_dimension=1, tiled=True
        ).astype(jnp.float32),
        lax.psum_scatter(
            fc1_bias_part.astype(jnp.bfloat16), "mp", scatter_dimension=0, tiled=True
        ).astype(jnp.float32),
        lax.psum_scatter(
            fc2_part.astype(jnp.bfloat16), "mp", scatter_dimension=0, tiled=True
        ).astype(jnp.float32),
    )
    fc2_bias_grad = jnp.sum(grad_top, axis=(0, 1))
    grad_from_norm, gain_two_grad, shift_two_grad = norm_backward(
        grad_normed_two, scaled_two, inverse_two, gain_two
    )
    grad_middle = grad_top + grad_from_norm
    out_bias_grad = jnp.sum(grad_middle, axis=(0, 1))
    grad_branch = grad_middle.astype(jnp.bfloat16)
    grad_branch_full = lax.all_gather(grad_branch, "mp", axis=0, tiled=True)
    out_grad = jnp.einsum(
        "tsf,tsd->fd", attended_flat, grad_branch_full, preferred_element_type=jnp.float32
    )
    grad_attended = jnp.einsum(
        "tsd,fd->tsf", grad_branch_full, w_out, preferred_element_type=jnp.float32
    ).astype(jnp.bfloat16)
    query_grad, key_grad, value_grad = attention_backward(
        query_all, key_all, value_all, grad_attended.reshape(head_shape), log_total, block_rows
    )
    grad_project = jnp.stack([query_grad, key_grad, value_grad], axis=2).reshape(
        seq_len, samples_here, 3, local_width
    )
    qkv_grad = jnp.einsum(
        "tsd,tscf->dcf", normed_full, grad_project, preferred_element_type=jnp.float32
    )
    query_bias_grad = jnp.sum(query_grad.astype(jnp.float32), axis=(0, 1)).reshape(local_width)
    value_bias_grad = jnp.sum(value_grad.astype(jnp.float32), axis=(0, 1)).reshape(local_width)
    qv_bias_grad = jnp.stack([query_bias_grad, value_bias_grad])
    picked = grad_project
    grad_normed_one = lax.psum_scatter(
        jnp.einsum("tscf,dcf->tsd", picked, w_qkv, preferred_element_type=jnp.float32).astype(
            jnp.bfloat16
        ),
        "mp",
        scatter_dimension=0,
        tiled=True,
    ).astype(jnp.float32)
    grad_in_one, gain_one_grad, shift_one_grad = norm_backward(
        grad_normed_one, scaled_one, inverse_one, norm1_gain.astype(jnp.float32)
    )
    grad_shifted = grad_middle + grad_in_one
    lead_grad = jnp.dot(
        onehot.T,
        jnp.sum(grad_shifted, axis=0),
        precision=lax.Precision.HIGHEST,
        preferred_element_type=jnp.float32,
    )
    small_grads = jnp.stack(
        [gain_one_grad, shift_one_grad, out_bias_grad, gain_two_grad, shift_two_grad, fc2_bias_grad]
    )
    lead_grad, small_grads = lax.psum((lead_grad, small_grads), ("dp", "mp"))
    qkv_grad, qv_bias_grad, out_grad, fc1_grad, fc1_bias_grad, fc2_grad = (
        lax.psum(qkv_grad.astype(jnp.bfloat16), "dp").astype(jnp.float32),
        lax.psum(qv_bias_grad.astype(jnp.bfloat16), "dp").astype(jnp.float32),
        lax.psum(out_grad.astype(jnp.bfloat16), "dp").astype(jnp.float32),
        lax.psum(fc1_grad.astype(jnp.bfloat16), "dp").astype(jnp.float32),
        lax.psum(fc1_bias_grad.astype(jnp.bfloat16), "dp").astype(jnp.float32),
        lax.psum(fc2_grad.astype(jnp.bfloat16), "dp").astype(jnp.float32),
    )
    block_output = jnp.swapaxes(output, 0, 1).astype(jnp.bfloat16)
    input_grad = jnp.swapaxes(grad_shifted, 0, 1)
    return (
        block_output,
        input_grad,
        lead_grad,
        small_grads[0],
        small_grads[1],
        qkv_grad,
        qv_bias_grad,
        out_grad,
        small_grads[2],
        small_grads[3],
        small_grads[4],
        fc1_grad,
        fc1_bias_grad,
        fc2_grad,
        small_grads[5],
    )


def solution(mesh):
    in_specs = (
        P("dp", "mp", None),
        P("dp", "mp", None),
        P("dp"),
        P(),
        P(),
        P(),
        P(),
        P(None, None, "mp"),
        P(None, "mp"),
        P("mp", None),
        P(),
        P(),
        P(),
        P(None, "mp"),
        P("mp"),
        P("mp", None),
        P(),
    )
    out_specs = (
        P("dp", "mp", None),
        P("dp", "mp", None),
        P(),
        P(),
        P(),
        P(None, None, "mp"),
        P(None, "mp"),
        P("mp", None),
        P(),
        P(),
        P(),
        P(None, "mp"),
        P("mp"),
        P("mp", None),
        P(),
    )
    return jax.shard_map(body, mesh=mesh, in_specs=in_specs, out_specs=out_specs, check_vma=False)
```

profile of v0, /device:TPU:0, one launch (start us, length us, event | category | flops | bytes accessed | tf_op | source)
XLA Modules:
  0.0 1236.8 jit_solution(1615556166740631826)
XLA Ops:
  17.5 59.3 %all-gather.5.cloned.1.call-done = bf16[1024,2,1024]{2,0,1:T(8,128)(2,1)} async-done(((bf16[512,2,1024]{2,0,1:T(8,128)(2,1)}), bf16[1024,2,1024]{2,0,1:T(8,128)(2,1)}) %all-gather.5.cloned.1.call-update) | async-done | bytes 4194320 | tf_op jit(solution)/shard_map/all_gather | solution.py:144
  76.9 9.9 fusion.66
  88.4 4.2 fusion.98
  92.7 6.6 squeeze.38
  99.2 3.9 add_convert_fusion.2
  106.8 94.0 %while.27 = (s32[]{:T(128)}, bf16[2,512,2,8,64]{1,4,3,2,0:T(8,128)(2,1)}, f32[2,2,8,512]{3,2,1,0:T(8,128)S(1)}, bf16[2,512,2,8,64]{1,4,3,2,0:T(8,128)(2,1)}, bf1...) while((s32[]{:T(128)}, bf16[2,512,2,8,64]{1,4,3,2,0:T(8,128)(2,1)}, ...), condition=%wide.region_5.0_spmd, body=%wide.region_2.5_spmd.sunk | while | flops 2223497216 | bytes 132382896 | solution.py:52
  106.9 17.5 %multiply_reduce_fusion.9 = (f32[2,8,512]{2,1,0:T(8,128)S(1)}, f32[2,8,512,1024]{3,2,1,0:T(8,128)}) fusion(bf16[1024,2,8,64]{0,3,2,1:T(8,128)(2,1)} %get-tuple-element.363, bf16[2,512,2,8,64]{1,4,3,2,0:T(8,128)(2,1)} %get-tuple-element.362, s32[]{:T(128)S(6)} %copy.108), kind=kOutput, calls=%fused_computation.2.clone.1 | convolution fusion | flops 1090510848 | bytes 36732932 | tf_op jit(solution)/shard_map/while/body/eval_jaxpr/qshd,kshd->shqk/dot_general | solution.py:40
  124.5 14.7 %fusion.135 = f32[2,8,512]{2,1,0:T(8,128)S(1)} fusion(f32[2,8,512,1024]{3,2,1,0:T(8,128)} %get-tuple-element.332, f32[2,8,512]{2,1,0:T(8,128)S(1)} %get-tuple-element.333), kind=kLoop, calls=%fused_computation.3.clone.1 | loop fusion | flops 25157632 | bytes 33619968 | tf_op jit(solution)/shard_map/while/body/eval_jaxpr/reduce_sum | solution.py:45
  139.2 13.3 %fusion.136 = bf16[2,512,2,8,64]{1,4,3,2,0:T(8,128)(2,1)S(1)} fusion(bf16[2,512,2,8,64]{1,4,3,2,0:T(8,128)(2,1)S(1)} %copy-done.14, s32[]{:T(128)S(6)} %copy.108, bf16[1024,2,8,64]{0,3,2,1:T(8,128)(2,1)S(1)} %copy-done.3, f32[2,8,512,1024]{3,2,1,0:T(8,128)} %get-tuple-element.332, f32[2,8,512]{2,1,0:T(8,128)S(1)} %fusion.135, ...), kind=kOutput, calls=%fused_computation.7.clone.1 | convolution fusion | flops 1107820544 | bytes 36765700 | tf_op jit(solution)/shard_map/while/body/eval_jaxpr/shqk,kshd->qshd/dot_general | solution.py:47
  153.8 17.5 %multiply_reduce_fusion.9 = (f32[2,8,512]{2,1,0:T(8,128)S(1)}, f32[2,8,512,1024]{3,2,1,0:T(8,128)}) fusion(bf16[1024,2,8,64]{0,3,2,1:T(8,128)(2,1)} %get-tuple-element.363, bf16[2,512,2,8,64]{1,4,3,2,0:T(8,128)(2,1)} %get-tuple-element.362, s32[]{:T(128)S(6)} %copy.108), kind=kOutput, calls=%fused_computation.2.clone.1 | convolution fusion | flops 1090510848 | bytes 36732932 | tf_op jit(solution)/shard_map/while/body/eval_jaxpr/qshd,kshd->shqk/dot_general | solution.py:40
  171.4 14.7 %fusion.135 = f32[2,8,512]{2,1,0:T(8,128)S(1)} fusion(f32[2,8,512,1024]{3,2,1,0:T(8,128)} %get-tuple-element.332, f32[2,8,512]{2,1,0:T(8,128)S(1)} %get-tuple-element.333), kind=kLoop, calls=%fused_computation.3.clone.1 | loop fusion | flops 25157632 | bytes 33619968 | tf_op jit(solution)/shard_map/while/body/eval_jaxpr/reduce_sum | solution.py:45
  186.1 13.3 %fusion.136 = bf16[2,512,2,8,64]{1,4,3,2,0:T(8,128)(2,1)S(1)} fusion(bf16[2,512,2,8,64]{1,4,3,2,0:T(8,128)(2,1)S(1)} %copy-done.14, s32[]{:T(128)S(6)} %copy.108, bf16[1024,2,8,64]{0,3,2,1:T(8,128)(2,1)S(1)} %copy-done.3, f32[2,8,512,1024]{3,2,1,0:T(8,128)} %get-tuple-element.332, f32[2,8,512]{2,1,0:T(8,128)S(1)} %fusion.135, ...), kind=kOutput, calls=%fused_computation.7.clone.1 | convolution fusion | flops 1107820544 | bytes 36765700 | tf_op jit(solution)/shard_map/while/body/eval_jaxpr/shqk,kshd->qshd/dot_general | solution.py:47
  200.8 5.1 copy.73
  205.9 4.4 reshape_reshape.8
  210.3 7.6 fusion.84
  219.5 4.3 all_gather.17
  225.3 92.0 %reduce-scatter.5.cloned.1.call-done = f32[512,2,1024]{2,0,1:T(8,128)} async-done(((f32[1024,2,1024]{2,0,1:T(8,128)}), f32[512,2,1024]{2,0,1:T(8,128)}) %reduce-scatter.5.cloned.1.call-update) | async-done | bytes 4194320 | tf_op jit(solution)/shard_map/reduce_scatter | solution.py:153
  317.4 3.6 fusion.96
  323.6 99.5 %all-gather.7.cloned.1.call-done = bf16[1024,4096]{1,0:T(8,128)(2,1)} async-done(((bf16[1024,2048]{1,0:T(8,128)(2,1)}), bf16[1024,4096]{1,0:T(8,128)(2,1)}) %all-gather.7.cloned.1.call-update) | async-done | bytes 8388624 | tf_op jit(solution)/shard_map/all_gather | solution.py:168
  423.0 24.7 %fusion.73 = (u8[512,4096]{1,0:T(8,128)(4,1)}, u8[512,4096]{1,0:T(8,128)(4,1)}, f32[512,2,4096]{2,0,1:T(8,128)}) fusion(f32[4096]{0:T(1024)S(1)} %convert_element_type.169, bf16[1024,4096]{1,0:T(8,128)(2,1)} %all-gather.7.cloned.1.call-done, f32[512,2,1024]{2,0,1:T(8,128)} %copy-done.7, f32[1024]{0:T(1024)S(1)} %convert_element_type.167, ...), kind=kOutput, calls=%fused_computation.120 | convolution fusion | flops 8649703424 | bytes 33587200 | tf_op jit(solution)/shard_map/tsd,df->tsf/dot_general | solution.py:172
  447.8 80.8 %all-gather.9.cloned.1.call-done = bf16[4096,1024]{1,0:T(8,128)(2,1)} async-done(((bf16[2048,1024]{1,0:T(8,128)(2,1)}), bf16[4096,1024]{1,0:T(8,128)(2,1)}) %all-gather.9.cloned.1.call-update) | async-done | bytes 8388624 | tf_op jit(solution)/shard_map/all_gather | solution.py:170
  528.6 19.9 %fusion.100 = (bf16[4096]{0:T(1024)(128)(2,1)}, bf16[512,2,4096]{2,0,1:T(8,128)(2,1)}) fusion(f32[512,2,4096]{2,0,1:T(8,128)} %get-tuple-element.239, f32[4096]{0:T(1024)S(1)} %convert_element_type.169, bf16[4096,1024]{1,0:T(8,128)(2,1)} %all-gather.9.cloned.1.call-done, bf16[2,512,1024]{2,1,0:T(8,128)(2,1)} %param.22, f32[2]{0:T(128)S(1)} %broadcast_divide_fusion), kind=kOutput, calls=%fused_computation.159 | convolution fusion | flops 8643407872 | bytes 35676168 | tf_op jit(solution)/shard_map/tsd,fd->tsf/dot_general | solution.py:178
  548.5 15.8 %multiply_reduce_fusion.2 = (f32[1024]{0:T(1024)}, f32[512,2]{0,1:T(2,128)S(1)}, f32[512,2]{0,1:T(2,128)S(1)}, f32[1024]{0:T(1024)}, f32[512,2,1024]{2,0,1:T(8,128)S(1)}) fusion(f32[512,2,1024]{2,0,1:T(8,128)S(1)} %copy-done.8, f32[512,2]{0,1:T(2,128)S(1)} %add_rsqrt_fusion, f32[512,2]{0,1:T(2,128)S(1)} %broadcast_multiply_fusion.4, ...), kind=kOutput, calls=%fused_computation.107 | convolution fusion | flops 8599367680 | bytes 25194496 | tf_op jit(solution)/shard_map/tsf,df->tsd/dot_general | solution.py:180
  564.3 3.7 fusion.95
  568.1 41.2 %fusion.36 = bf16[512,2,4096]{2,0,1:T(8,128)(2,1)S(1)} fusion(f32[512,2,4096]{2,0,1:T(8,128)} %get-tuple-element.239, f32[4096]{0:T(1024)S(1)} %convert_element_type.169, u8[512,4096]{1,0:T(8,128)(4,1)} %get-tuple-element.169, u8[512,4096]{1,0:T(8,128)(4,1)} %get-tuple-element.168), kind=kLoop, calls=%fused_computation.46 | loop fusion | flops 297795584 | bytes 29376512 | tf_op jit(solution)/shard_map/convert_element_type | solution.py:175
  609.3 3.4 copy-done.10
  612.7 11.7 bitcast_convert_fusion
  624.6 15.6 %bitcast_convert_fusion.1 = bf16[1024,4096]{1,0:T(8,128)(2,1)} fusion(bf16[512,2,4096]{2,0,1:T(8,128)(2,1)} %get-tuple-element.242, f32[512,2,1024]{2,0,1:T(8,128)} %copy-done.7, f32[1024]{0:T(1024)S(1)} %convert_element_type.167, f32[1024]{0:T(1024)S(1)} %convert_element_type.166, f32[512,2]{0,1:T(2,128)S(1)} %add_rsqrt_fusion, ...), kind=kOutput, calls=%fused_computation.59 | convolution fusion | flops 8599371776 | bytes 20987904 | tf_op jit(solution)/shard_map/tsd,tsf->df/dot_general | solution.py:183
  640.2 6.3 convolution_convert_fusion
  646.6 6.1 reshape.141
  652.7 5.6 copy.76
  659.9 220.8 %while.28 = (s32[]{:T(128)}, f32[1024,2,8,64]{0,3,2,1:T(8,128)}, f32[1024,2,8,64]{0,3,2,1:T(8,128)}, bf16[2,512,2,8,64]{1,4,3,2,0:T(8,128)(2,1)}, bf16[2,512,2,8...) while((s32[]{:T(128)}, f32[1024,2,8,64]{0,3,2,1:T(8,128)}, ...), condition=%wide.region_15.16_spmd.clone, body=%wide.region_13.15_spmd.clone.sunk | while | flops 5475655680 | bytes 322142432 | solution.py:92
  660.3 18.1 %fusion.146 = f32[2,8,512,1024]{3,2,1,0:T(8,128)} fusion(bf16[1024,2,8,64]{0,3,2,1:T(8,128)(2,1)} %get-tuple-element.393, bf16[2,512,2,8,64]{1,4,3,2,0:T(8,128)(2,1)} %get-tuple-element.392, s32[]{:T(128)S(6)} %copy.118), kind=kOutput, calls=%fused_computation.30.clone.1 | convolution fusion | flops 1073741824 | bytes 36700164 | tf_op jit(solution)/shard_map/while/body/eval_jaxpr/qshd,kshd->shqk/dot_general | solution.py:65
  678.4 16.9 %bitcast_add_fusion.8 = f32[1024,2,8,64]{0,3,2,1:T(8,128)} fusion(f32[1024,2,8,64]{0,3,2,1:T(8,128)} %get-tuple-element.379, f32[2,8,512,1024]{3,2,1,0:T(8,128)} %fusion.146, f32[2,8,512]{2,1,0:T(8,128)S(1)} %dynamic-slice_bitcast_fusion.2, pred[]{:T(512)S(6)} %compare.3, bf16[2,512,2,8,64]{1,4,3,2,0:T(8,128)(2,1)} %get-tuple-element.395, s32[]{:T(128)S(6)} %copy.118), kind=kOutput, calls=%fused_computation.21.clone.1 | convolution fusion | flops 1101004800 | bytes 43024388 | tf_op jit(solution)/shard_map/while/body/eval_jaxpr/shqk,qshd->kshd/dot_general | solution.py:86
  695.3 24.5 %multiply_reduce_fusion.10 = (f32[2,8,512]{2,1,0:T(8,128)S(1)}, f32[2,8,512,1024]{3,2,1,0:T(8,128)}) fusion(f32[2,8,512,1024]{3,2,1,0:T(8,128)} %fusion.146, f32[2,8,512]{2,1,0:T(8,128)S(1)} %dynamic-slice_bitcast_fusion.2, bf16[1024,2,8,64]{0,3,2,1:T(8,128)(2,1)} %get-tuple-element.396, bf16[2,512,2,8,64]{1,4,3,2,0:T(8,128)(2,1)} %get-tuple-element.395, ...), kind=kOutput, calls=%fused_computation.15.clone.1 | convolution fusion | flops 1107288064 | bytes 70320128 | tf_op jit(solution)/shard_map/while/body/eval_jaxpr/qshd,kshd->shqk/dot_general | solution.py:70
  719.7 28.4 %multiply_convert_fusion.3 = bf16[2,8,512,1024]{3,2,1,0:T(8,128)(2,1)} fusion(f32[2,8,512,1024]{3,2,1,0:T(8,128)} %get-tuple-element.343, f32[2,8,512,1024]{3,2,1,0:T(8,128)} %fusion.146, f32[2,8,512]{2,1,0:T(8,128)S(1)} %get-tuple-element.344, f32[2,8,512]{2,1,0:T(8,128)S(1)} %dynamic-slice_bitcast_fusion.2), kind=kLoop, calls=%fused_computation.14.clone.1 | loop fusion | flops 41943040 | bytes 83951616 | tf_op jit(solution)/shard_map/while/body/eval_jaxpr/convert_element_type | solution.py:74
  748.2 10.6 fusion.147
  758.7 9.6 bitcast_add_fusion.7
  770.4 18.3 %fusion.146 = f32[2,8,512,1024]{3,2,1,0:T(8,128)} fusion(bf16[1024,2,8,64]{0,3,2,1:T(8,128)(2,1)} %get-tuple-element.393, bf16[2,512,2,8,64]{1,4,3,2,0:T(8,128)(2,1)} %get-tuple-element.392, s32[]{:T(128)S(6)} %copy.118), kind=kOutput, calls=%fused_computation.30.clone.1 | convolution fusion | flops 1073741824 | bytes 36700164 | tf_op jit(solution)/shard_map/while/body/eval_jaxpr/qshd,kshd->shqk/dot_general | solution.py:65
  788.7 18.1 %bitcast_add_fusion.8 = f32[1024,2,8,64]{0,3,2,1:T(8,128)} fusion(f32[1024,2,8,64]{0,3,2,1:T(8,128)} %get-tuple-element.379, f32[2,8,512,1024]{3,2,1,0:T(8,128)} %fusion.146, f32[2,8,512]{2,1,0:T(8,128)S(1)} %dynamic-slice_bitcast_fusion.2, pred[]{:T(512)S(6)} %compare.3, bf16[2,512,2,8,64]{1,4,3,2,0:T(8,128)(2,1)} %get-tuple-element.395, s32[]{:T(128)S(6)} %copy.118), kind=kOutput, calls=%fused_computation.21.clone.1 | convolution fusion | flops 1101004800 | bytes 43024388 | tf_op jit(solution)/shard_map/while/body/eval_jaxpr/shqk,qshd->kshd/dot_general | solution.py:86
  806.8 24.2 %multiply_reduce_fusion.10 = (f32[2,8,512]{2,1,0:T(8,128)S(1)}, f32[2,8,512,1024]{3,2,1,0:T(8,128)}) fusion(f32[2,8,512,1024]{3,2,1,0:T(8,128)} %fusion.146, f32[2,8,512]{2,1,0:T(8,128)S(1)} %dynamic-slice_bitcast_fusion.2, bf16[1024,2,8,64]{0,3,2,1:T(8,128)(2,1)} %get-tuple-element.396, bf16[2,512,2,8,64]{1,4,3,2,0:T(8,128)(2,1)} %get-tuple-element.395, ...), kind=kOutput, calls=%fused_computation.15.clone.1 | convolution fusion | flops 1107288064 | bytes 70320128 | tf_op jit(solution)/shard_map/while/body/eval_jaxpr/qshd,kshd->shqk/dot_general | solution.py:70
  831.0 27.8 %multiply_convert_fusion.3 = bf16[2,8,512,1024]{3,2,1,0:T(8,128)(2,1)} fusion(f32[2,8,512,1024]{3,2,1,0:T(8,128)} %get-tuple-element.343, f32[2,8,512,1024]{3,2,1,0:T(8,128)} %fusion.146, f32[2,8,512]{2,1,0:T(8,128)S(1)} %get-tuple-element.344, f32[2,8,512]{2,1,0:T(8,128)S(1)} %dynamic-slice_bitcast_fusion.2), kind=kLoop, calls=%fused_computation.14.clone.1 | loop fusion | flops 41943040 | bytes 83951616 | tf_op jit(solution)/shard_map/while/body/eval_jaxpr/convert_element_type | solution.py:74
  858.8 10.3 fusion.147
  869.2 9.4 bitcast_add_fusion.7
  880.7 3.8 convert_element_type.180
  884.6 3.9 copy.79
  888.5 5.6 copy.96
  894.2 6.5 reshape.142
  900.6 3.7 fusion.94
  904.4 3.9 copy.80
  908.3 10.1 bitcast_convert_fusion.2
  918.5 6.3 bitcast_convert_fusion.5
  924.8 8.5 bitcast_convert_fusion.3
  937.8 5.2 all-reduce
  943.1 15.8 %fusion.80 = bf16[2,512,1024]{2,1,0:T(8,128)(2,1)} fusion(f32[1024]{0:T(1024)S(1)} %convert_element_type.171, f32[512,2,1024]{2,0,1:T(8,128)} %copy-done.7, bf16[512,2,4096]{2,0,1:T(8,128)(2,1)} %copy-done.10, bf16[4096,1024]{1,0:T(8,128)(2,1)} %all-gather.9.cloned.1.call-done), kind=kOutput, calls=%fused_computation.127 | convolution fusion | flops 8593080320 | bytes 23072768 | tf_op jit(solution)/shard_map/tsf,fd->tsd/dot_general | solution.py:176
  961.0 33.7 %all-reduce.2 = (bf16[2,512]{1,0:T(2,128)(2,1)S(1)}, bf16[2048]{0:T(1024)(128)(2,1)S(1)}) all-reduce(bf16[2,512]{1,0:T(2,128)(2,1)S(1)} %pad_maximum_fusion.5, bf16[2048]{0:T(1024)(128)(2,1)S(1)} %dynamic-slice.1), channel_id=1, replica_groups=mesh['dp'=16,'mp'=2] {'dp'}, use_global_device_ids=true, to_apply=%region_31.32 | all-reduce | flops 3072 | bytes 12288 | tf_op jit(solution)/shard_map/psum | solution.py:248
  995.9 3.4 fusion.58
  999.5 5.5 fusion.63
  1005.4 39.2 %all-reduce.1 = (f32[8,1024]{1,0:T(8,128)}, f32[6,1024]{1,0:T(8,128)S(1)}) all-reduce(f32[8,1024]{1,0:T(8,128)S(1)} %fusion.86, f32[6,1024]{1,0:T(8,128)S(1)} %stack.46), channel_id=1, replica_groups=mesh['dp'=16,'mp'=2] {'dp','mp'}, use_global_device_ids=true, to_apply=%region_20.21 | all-reduce | flops 14336 | bytes 114688 | tf_op jit(solution)/shard_map/psum | solution.py:245
  1045.2 169.3 %all-reduce.6.cloned.1.call-done = (bf16[1024,3,512]{2,0,1:T(8,128)(2,1)}, bf16[512,1024]{1,0:T(8,128)(2,1)}, bf16[1024,2048]{1,0:T(8,128)(2,1)}, bf16[2048,1024]{1,0:T(8,128)(2,1)}) async-done(((bf16[1024,3,512]{2,0,1:T(8,128)(2,1)}, bf16[512,1024]{1,0:T(8,128)(2,1)}, bf16[1024,2048]{1,0:T(8,128)(2,1)}, bf16[2048,1024]{1,0:T(8,128)(2,1)}), (bf16[1024,3,512]{2,0,1:T(8,128)(2,1)}, ...) | async-done | bytes 12582928 | tf_op jit(solution)/shard_map/psum | solution.py:247
  1214.6 2.9 convert_element_type.190
  1217.5 3.6 convert_element_type.185
  1221.1 4.4 convert_element_type.192
  1225.6 4.4 convert_element_type.195
  (181 shorter events, 37.1 us)
Async XLA Ops:
  7.2 69.7 %copy-start = (bf16[1024,3,512]{2,0,1:T(8,128)(2,1)S(1)}, bf16[1024,3,512]{2,0,1:T(8,128)(2,1)}, u32[]{:S(2)}) copy-start(bf16[1024,3,512]{2,0,1:T(8,128)(2,1)} %param.28) | copy-start | bytes 9437188
  7.2 69.7 %all-gather.5.cloned.1.call-start = ((), (), s32[]{:S(2)}) async-start(), calls=%async_computation.4 | async-start | bytes 6291456 | tf_op jit(solution)/shard_map/all_gather | solution.py:144
  7.2 7.8 copy-start.5
  8.1 6.3 copy-start.29
  9.9 4.5 copy-start.24
  11.9 2.4 copy-start.27
  12.0 5.4 copy-start.39
  14.4 0.6 copy-start.31
  17.3 300.1 %reduce-scatter.5.cloned.1.call-start = ((), (), s32[]{:S(2)}) async-start(), calls=%async_computation.5 | async-start | bytes 12582912 | tf_op jit(solution)/shard_map/reduce_scatter | solution.py:153
  99.2 3.9 copy-start.9
  124.5 14.7 %copy-start.3 = (bf16[1024,2,8,64]{0,3,2,1:T(8,128)(2,1)S(1)}, bf16[1024,2,8,64]{0,3,2,1:T(8,128)(2,1)}, u32[]{:S(2)}) copy-start(bf16[1024,2,8,64]{0,3,2,1:T(8,128)(2,1)} %get-tuple-element.364) | copy-start | bytes 6291460 | tf_op jit(solution)/shard_map/while
  124.5 14.7 %copy-start.14 = (bf16[2,512,2,8,64]{1,4,3,2,0:T(8,128)(2,1)S(1)}, bf16[2,512,2,8,64]{1,4,3,2,0:T(8,128)(2,1)}, u32[]{:S(2)}) copy-start(bf16[2,512,2,8,64]{1,4,3,2,0:T(8,128)(2,1)} %get-tuple-element.353) | copy-start | bytes 6291460 | tf_op jit(solution)/shard_map/while
  152.5 1.3 copy-start.15
  171.4 14.7 %copy-start.3 = (bf16[1024,2,8,64]{0,3,2,1:T(8,128)(2,1)S(1)}, bf16[1024,2,8,64]{0,3,2,1:T(8,128)(2,1)}, u32[]{:S(2)}) copy-start(bf16[1024,2,8,64]{0,3,2,1:T(8,128)(2,1)} %get-tuple-element.364) | copy-start | bytes 6291460 | tf_op jit(solution)/shard_map/while
  171.4 14.7 %copy-start.14 = (bf16[2,512,2,8,64]{1,4,3,2,0:T(8,128)(2,1)S(1)}, bf16[2,512,2,8,64]{1,4,3,2,0:T(8,128)(2,1)}, u32[]{:S(2)}) copy-start(bf16[2,512,2,8,64]{1,4,3,2,0:T(8,128)(2,1)} %get-tuple-element.353) | copy-start | bytes 6291460 | tf_op jit(solution)/shard_map/while
  199.4 1.3 copy-start.15
  200.8 9.5 copy-start.22
  218.0 1.4 copy-start.45
  218.0 1.5 copy-start.40
  218.0 1.5 copy-start.41
  218.0 1.5 copy-start.42
  218.0 1.5 copy-start.36
  218.0 7.1 copy-start.46
  218.0 99.3 %copy-start.25 = (f32[2,1024]{1,0:T(2,128)S(1)}, f32[2,1024]{1,0:T(2,128)}, u32[]{:S(2)}) copy-start(f32[2,1024]{1,0:T(2,128)} %copy-done.24) | copy-start | bytes 24580
  218.0 205.0 %all-gather.7.cloned.1.call-start = ((), (), s32[]{:S(2)}) async-start(), calls=%async_computation.6 | async-start | bytes 12582912 | tf_op jit(solution)/shard_map/all_gather | solution.py:168
  218.8 309.8 %all-gather.9.cloned.1.call-start = ((), (), s32[]{:S(2)}) async-start(), calls=%async_computation.7 | async-start | bytes 12582912 | tf_op jit(solution)/shard_map/all_gather | solution.py:170
  219.4 420.9 %all-gather.11.cloned.1.call-start = ((), (), s32[]{:S(2)}) async-start(), calls=%async_computation.8 | async-start | bytes 6291456 | tf_op jit(solution)/shard_map/all_gather | solution.py:204
  225.3 384.0 %copy-start.37 = (f32[2]{0:T(128)}, f32[2]{0:T(128)S(1)}, u32[]{:S(2)}) copy-start(f32[2]{0:T(128)S(1)} %broadcast_divide_fusion) | copy-start | bytes 28
  321.0 2.0 copy-start.7
  528.6 19.9 %copy-start.8 = (f32[512,2,1024]{2,0,1:T(8,128)S(1)}, f32[512,2,1024]{2,0,1:T(8,128)}, u32[]{:S(2)}) copy-start(f32[512,2,1024]{2,0,1:T(8,128)} %copy-done.7) | copy-start | bytes 12582916
  548.5 15.8 %copy-start.11 = (bf16[2,512,1024]{2,1,0:T(8,128)(2,1)S(1)}, bf16[2,512,1024]{2,1,0:T(8,128)(2,1)}, u32[]{:S(2)}) copy-start(bf16[2,512,1024]{2,1,0:T(8,128)(2,1)} %param.22) | copy-start | bytes 6291460
  568.0 365.3 %reduce-scatter.11.cloned.1.call-start = ((), (), s32[]{:S(2)}) async-start(), calls=%async_computation.11 | async-start | bytes 12582912 | tf_op jit(solution)/shard_map/reduce_scatter | solution.py:193
  568.0 44.7 %copy-start.12 = (bf16[2,512,1024]{2,1,0:T(8,128)(2,1)S(1)}, bf16[2,512,1024]{2,1,0:T(8,128)(2,1)}, u32[]{:S(2)}) copy-start(bf16[2,512,1024]{2,1,0:T(8,128)(2,1)} %param.22) | copy-start | bytes 6291460
  609.3 3.4 copy-start.10
  624.5 308.8 %reduce-scatter.9.cloned.1.call-start = ((), (), s32[]{:S(2)}) async-start(), calls=%async_computation.10 | async-start | bytes 12582912 | tf_op jit(solution)/shard_map/reduce_scatter | solution.py:187
  640.2 355.7 %reduce-scatter.7.cloned.1.call-start = ((), (), s32[]{:S(2)}) async-start(), calls=%async_computation.9 | async-start | bytes 6291456 | tf_op jit(solution)/shard_map/reduce_scatter | solution.py:224
  652.7 7.2 copy-start.23
  748.2 10.6 copy-start.1
  748.2 10.6 copy-start.4
  768.4 2.0 copy-start.2
  858.8 10.4 copy-start.1
  858.8 10.4 copy-start.4
  878.6 2.0 copy-start.2
  918.4 296.2 %all-reduce.6.cloned.1.call-start = ((), (), s32[]{:S(2)}) async-start(), calls=%async_computation.12 | async-start | bytes 25165824 | tf_op jit(solution)/shard_map/psum | solution.py:247
  918.5 6.3 copy-start.19
  918.5 6.3 copy-start.20
  918.5 6.3 copy-start.21
  918.5 6.3 copy-start.44
  933.3 0.7 copy-start.43
  933.3 0.7 copy-start.48
  933.3 1.9 copy-start.38
  933.3 4.5 copy-start.33
  943.0 52.9 %copy-start.26 = (f32[2,1024]{1,0:T(2,128)S(1)}, f32[2,1024]{1,0:T(2,128)}, u32[]{:S(2)}) copy-start(f32[2,1024]{1,0:T(2,128)} %copy-done.24) | copy-start | bytes 24580
  943.0 52.9 %copy-start.28 = (f32[512,2]{0,1:T(2,128)S(1)}, f32[512,2]{0,1:T(2,128)}, u32[]{:S(2)}) copy-start(f32[512,2]{0,1:T(2,128)} %copy-done.27) | copy-start | bytes 12292
  943.0 52.9 %copy-start.30 = (f32[1024]{0:T(1024)S(1)}, f32[1024]{0:T(1024)}, u32[]{:S(2)}) copy-start(f32[1024]{0:T(1024)} %copy-done.29) | copy-start | bytes 12292
  943.1 52.9 %copy-start.32 = (f32[512,2]{0,1:T(2,128)S(1)}, f32[512,2]{0,1:T(2,128)}, u32[]{:S(2)}) copy-start(f32[512,2]{0,1:T(2,128)} %copy-done.31) | copy-start | bytes 12292
  995.9 3.5 copy-start.6
  995.9 3.6 copy-start.13
  999.5 5.5 copy-start.34
  999.5 5.5 copy-start.35
  999.5 5.6 copy-start.47
  1214.6 2.9 copy-start.18
  1217.5 3.6 copy-start.17
  1221.1 4.5 copy-start.16
Sparse Core Ops, SparseCore 0:
  17.4 59.4 all-gather.4
  218.1 99.2 reduce-scatter.4
  319.0 104.0 all-gather.6
  424.5 103.9 all-gather.8
  568.1 56.7 all-gather.10
  627.2 99.2 reduce-scatter.10
  728.7 99.2 reduce-scatter.8
  918.5 55.0 reduce-scatter.6
  978.8 235.7 all-reduce.5
where the time goes:
time: 1250 us; the launch traced here: 1240 us
  waiting for transfers between devices  502 us (40%)
  matrix products  375 us (30%)
  other arithmetic  188 us (15%)
  blocking collectives  82.4 us (7%)
  local copies, waits for them, and re-layouts  72 us (6%)
  between operations  16 us (1%)
    psum x1, waiting for transfers between devices, body(): lax.psum(qkv_grad.astype(jnp.bfloat16), 'dp').astype(jnp.float32)  169 us
    all_gather x1, waiting for transfers between devices, body(): lax.all_gather(w_fc1, 'mp', axis=1, tiled=True)  99.5 us
    reduce_scatter x1, waiting for transfers between devices, body(): lax.psum_scatter(jnp.einsum('tsf,fd->tsd', picked, w_out, preferred_eleme...  92 us
    all_gather x1, waiting for transfers between devices, body(): lax.all_gather(w_fc2, 'mp', axis=0, tiled=True)  80.8 us
    dot_general x4, matrix products, one_block(): jnp.einsum('qshd,kshd->shqk', query_block, key_all, preferred_element_typ...  71.4 us
    all_gather x1, waiting for transfers between devices, body(): normed_full = lax.all_gather(normed_one, 'mp', axis=0, tiled=True)  59.3 us
    convert_element_type x2, other arithmetic, one_block(): grad_scores = (attn_weights * (grad_weights - inner)).astype(jnp.bfloat16)  56.3 us
    dot_general x2, matrix products, one_block(): jnp.einsum('qshd,kshd->shqk', grad_block, value_all, preferred_element_ty...  48.6 us
  transfers between devices with their start and end apart: 9, of which 5 were waited for; matrix products, arithmetic and copies ran while one was open for 34% of the time, Pallas kernels for 0%

commit v1 on v0

--- a/solution.py
+++ b/solution.py
@@ -1,6 +1,10 @@
+import functools
+
 import jax
 import jax.numpy as jnp
 from jax import lax
+from jax.experimental import pallas as pl
+from jax.experimental.pallas import tpu as pltpu
 from jax.sharding import PartitionSpec as P
 
 HD = 64
@@ -272,6 +276,435 @@
     )
 
 
+F32 = jnp.float32
+BF16 = jnp.bfloat16
+NN = (((1,), (0,)), ((), ()))
+NT = (((1,), (1,)), ((), ()))
+TN = (((0,), (0,)), ((), ()))
+
+
+def dot(left, right, dims):
+    return lax.dot_general(left, right, dims, preferred_element_type=F32)
+
+
+def attention_forward_kernel(qkv_ref, out_ref, power_ref, inverse_ref):
+    outs = []
+    for head in range(2):
+        lanes = slice(HD * head, HD * head + HD)
+        query = qkv_ref[0, :, lanes] * BF16(0.125)
+        scores = dot(qkv_ref[1, :, lanes], query, NT)
+        powers = jnp.exp(scores - jnp.max(scores, axis=0, keepdims=True))
+        inverse = 1.0 / jnp.sum(powers, axis=0, keepdims=True)
+        power_low = powers.astype(BF16)
+        power_ref[head] = power_low
+        inverse_ref[0, head : head + 1, :] = inverse
+        outs.append(dot(qkv_ref[2, :, lanes], power_low, TN) * inverse)
+    out_ref[...] = jnp.concatenate(outs, axis=0).T.astype(BF16)
+
+
+def attention_backward_kernel(block, qkv_ref, power_ref, inverse_ref, out_ref, grad_ref, dqkv_ref, sums_ref):
+    rows_all = qkv_ref.shape[1]
+    out_t = out_ref[...].astype(F32).T
+    grad_t = grad_ref[...].astype(F32).T
+    for head in range(2):
+        lanes = slice(HD * head, HD * head + HD)
+        inverse = inverse_ref[0, head : head + 1, :]
+        grad_head = grad_t[lanes]
+        inner = jnp.sum(grad_head * out_t[lanes], axis=0, keepdims=True) * inverse
+        grad_scaled = grad_head * inverse
+        grad_low_t = grad_scaled.astype(BF16)
+        grad_low = grad_scaled.T.astype(BF16)
+        query = qkv_ref[0, :, lanes] * BF16(0.125)
+        key = qkv_ref[1, :, lanes]
+        value = qkv_ref[2, :, lanes]
+        key_t = key.T
+        key_grad = value_grad = None
+        query_grads = []
+        for start in range(0, rows_all, block):
+            rows = slice(start, start + block)
+            power = power_ref[head, :, rows]
+            grad_power = dot(value, grad_low_t[:, rows], NN) - inner[:, rows]
+            grad_scores = (power.astype(F32) * grad_power).astype(BF16)
+            key_part = dot(grad_scores, query[rows], NN)
+            value_part = dot(power, grad_low[rows], NN)
+            key_grad = key_part if key_grad is None else key_grad + key_part
+            value_grad = value_part if value_grad is None else value_grad + value_part
+            query_grads.append(dot(key_t, grad_scores, NN))
+        sums_ref[0, :, lanes] = jnp.concatenate(query_grads, axis=1).T * 0.125
+        sums_ref[1, :, lanes] = key_grad
+        sums_ref[2, :, lanes] = value_grad
+    dqkv_ref[...] = sums_ref[...].astype(BF16)
+
+
+def attend(qkv):
+    _, rows, width = qkv.shape
+    pairs = width // (2 * HD)
+    work = 2 * pairs * rows * rows
+    return pl.pallas_call(
+        attention_forward_kernel,
+        out_shape=(
+            jax.ShapeDtypeStruct((rows, width), BF16),
+            jax.ShapeDtypeStruct((2 * pairs, rows, rows), BF16),
+            jax.ShapeDtypeStruct((pairs, 2, rows), F32),
+        ),
+        grid=(pairs,),
+        in_specs=[pl.BlockSpec((3, rows, 2 * HD), lambda j: (0, 0, j))],
+        out_specs=(
+            pl.BlockSpec((rows, 2 * HD), lambda j: (0, j)),
+            pl.BlockSpec((2, rows, rows), lambda j: (j, 0, 0)),
+            pl.BlockSpec((1, 2, rows), lambda j: (j, 0, 0)),
+        ),
+        compiler_params=pltpu.CompilerParams(vmem_limit_bytes=48 << 20),
+        cost_estimate=pl.CostEstimate(
+            flops=work * HD * 4 * 4, transcendentals=work, bytes_accessed=work * 2 + 8 * rows * width
+        ),
+        name="attention_forward",
+    )(qkv)
+
+
+def attend_back(qkv, powers, inverse, attended, grad_attended):
+    _, rows, width = qkv.shape
+    pairs = width // (2 * HD)
+    work = 2 * pairs * rows * rows
+    return pl.pallas_call(
+        functools.partial(attention_backward_kernel, min(512, rows)),
+        out_shape=jax.ShapeDtypeStruct((3, rows, width), BF16),
+        grid=(pairs,),
+        in_specs=[
+            pl.BlockSpec((3, rows, 2 * HD), lambda j: (0, 0, j)),
+            pl.BlockSpec((2, rows, rows), lambda j: (j, 0, 0)),
+            pl.BlockSpec((1, 2, rows), lambda j: (j, 0, 0)),
+            pl.BlockSpec((rows, 2 * HD), lambda j: (0, j)),
+            pl.BlockSpec((rows, 2 * HD), lambda j: (0, j)),
+        ],
+        out_specs=pl.BlockSpec((3, rows, 2 * HD), lambda j: (0, 0, j)),
+        scratch_shapes=[pltpu.VMEM((3, rows, 2 * HD), F32)],
+        compiler_params=pltpu.CompilerParams(vmem_limit_bytes=48 << 20),
+        cost_estimate=pl.CostEstimate(
+            flops=work * HD * 8 * 4, transcendentals=0, bytes_accessed=work * 2 + 16 * rows * width
+        ),
+        name="attention_backward",
+    )(qkv, powers, inverse, attended, grad_attended)
+
+
+def hidden_kernel(normed_ref, weight_ref, bias_ref, hidden_ref, slope_ref):
+    rows_all = normed_ref.shape[0]
+    block = min(256, rows_all)
+    for start in range(0, rows_all, block):
+        rows = slice(start, start + block)
+        pre_act = dot(normed_ref[rows], weight_ref[...], NN) + bias_ref[...]
+        cdf = 0.5 * (1.0 + lax.erf(pre_act * 0.7071067811865476))
+        hidden_ref[rows] = (pre_act * cdf).astype(BF16)
+        density = jnp.exp(-0.5 * pre_act * pre_act) * 0.3989422804014327
+        slope_ref[rows] = (cdf + pre_act * density).astype(BF16)
+
+
+def hidden_layer(normed, weight, bias):
+    rows, width = normed.shape
+    units = weight.shape[1]
+    tile = min(512, units)
+    return pl.pallas_call(
+        hidden_kernel,
+        out_shape=(jax.ShapeDtypeStruct((rows, units), BF16),) * 2,
+        grid=(units // tile,),
+        in_specs=[
+            pl.BlockSpec((rows, width), lambda j: (0, 0)),
+            pl.BlockSpec((width, tile), lambda j: (0, j)),
+            pl.BlockSpec((1, tile), lambda j: (0, j)),
+        ],
+        out_specs=(pl.BlockSpec((rows, tile), lambda j: (0, j)),) * 2,
+        compiler_params=pltpu.CompilerParams(vmem_limit_bytes=32 << 20),
+        cost_estimate=pl.CostEstimate(
+            flops=2 * rows * width * units,
+            transcendentals=2 * rows * units,
+            bytes_accessed=2 * (rows * width + width * units + 2 * rows * units),
+        ),
+        name="hidden_layer",
+    )(normed, weight, bias)
+
+
+def after(value, *firsts):
+    return lax.optimization_barrier((value, *firsts))[0]
+
+
+def fast_body(
+    tokens,
+    cotangent,
+    buckets,
+    counts,
+    lead_table,
+    norm1_gain,
+    norm1_shift,
+    w_qkv,
+    qv_bias,
+    w_out,
+    out_bias,
+    norm2_gain,
+    norm2_shift,
+    w_fc1,
+    fc1_bias,
+    w_fc2,
+    fc2_bias,
+):
+    replicas = lax.axis_size("dp")
+    levels = replicas.bit_length() - 1
+    dp_at, mp_at = lax.axis_index("dp"), lax.axis_index("mp")
+    bits = [(dp_at >> level) & 1 for level in range(levels)]
+
+    def over_x(value):
+        return lax.ppermute(value, "mp", [(0, 1), (1, 0)])
+
+    def over(level, value):
+        return lax.ppermute(value, "dp", [(i, i ^ (1 << level)) for i in range(replicas)])
+
+    def joined(bit, mine, theirs, axis=0):
+        return jnp.where(
+            bit == 0,
+            jnp.concatenate([mine, theirs], axis),
+            jnp.concatenate([theirs, mine], axis),
+        )
+
+    def part(value, index, count, axis=0):
+        size = value.shape[axis] // count
+        return lax.dynamic_slice_in_dim(value, index * size, size, axis)
+
+    half_rows, width = tokens.shape[1:]
+    heads_width = w_qkv.shape[2]
+    units = w_fc1.shape[1]
+
+    small = jnp.concatenate([qv_bias.reshape(-1), fc1_bias])
+    small_rows = -(-small.shape[0] // width)
+    small_rows_padded = -(-small_rows // 16) * 16
+    small = jnp.pad(small, (0, small_rows_padded * width - small.shape[0])).reshape(-1, width)
+    token_send = jnp.concatenate([part(tokens, 1 - mp_at, 2)[0], small])
+    token_recv = over_x(token_send)
+    far_small = token_recv[half_rows:].reshape(-1)
+    far_qv_bias = far_small[: 2 * heads_width].reshape(2, heads_width)
+    far_fc1_bias = far_small[2 * heads_width : 2 * heads_width + units]
+    token_rows = jnp.concatenate([part(tokens, mp_at, 2)[0], token_recv[:half_rows]])
+
+    def fetch(weight, *firsts):
+        piece = over_x(after(part(weight, bits[0], 2), *firsts))
+        return joined(bits[0], piece, over(0, piece)), piece
+
+    def fetch_shared(weight, *firsts):
+        piece = over_x(after(part(weight, bits[0] * 2 + bits[1], 4), *firsts))
+        piece_y = over(1, piece)
+        half = joined(bits[1], piece, piece_y)
+        return joined(bits[0], half, over(0, half)), piece
+
+    own_qkv = jnp.transpose(w_qkv, (1, 0, 2))
+    far_qkv, qkv_piece = fetch(own_qkv.reshape(-1, heads_width), token_recv)
+    far_qkv = far_qkv.reshape(own_qkv.shape)
+    far_fc1, fc1_piece = fetch_shared(w_fc1, qkv_piece)
+    far_out, out_piece = fetch(w_out, qkv_piece)
+    cot_recv = over_x(after(part(cotangent, 1 - mp_at, 2)[0], fc1_piece))
+    far_fc2, fc2_piece = fetch_shared(w_fc2, cot_recv)
+    cot_rows = jnp.concatenate([part(cotangent, mp_at, 2)[0], cot_recv])
+
+    bucket = lax.dynamic_index_in_dim(buckets, mp_at, 0, keepdims=False)
+    count_f = counts.astype(F32)
+    loss_weight = jnp.mean(count_f) / lax.dynamic_index_in_dim(count_f, bucket, 0, keepdims=False)
+    lead_row = lax.dynamic_index_in_dim(lead_table, bucket, 0).astype(F32)
+
+    def normalise(values):
+        center = values - jnp.mean(values, axis=-1, keepdims=True)
+        inverse = lax.rsqrt(jnp.mean(center * center, axis=-1, keepdims=True) + EPS)
+        return center * inverse, inverse
+
+    def normalise_back(grad_out, scaled, inverse, gain):
+        grad_scaled = grad_out * gain
+        grad_mean = jnp.mean(grad_scaled, axis=-1, keepdims=True)
+        cross_mean = jnp.mean(grad_scaled * scaled, axis=-1, keepdims=True)
+        grad_in = inverse * (grad_scaled - grad_mean - scaled * cross_mean)
+        return grad_in, jnp.sum(grad_out * scaled, axis=0), jnp.sum(grad_out, axis=0)
+
+    shifted = token_rows.astype(F32) + lead_row
+    gain_one = norm1_gain.astype(F32)
+    scaled_one, inverse_one = normalise(shifted)
+    normed_one = (scaled_one * gain_one + norm1_shift.astype(F32)).astype(BF16)
+
+    def project(weight, bias):
+        bias_f = bias.astype(F32)
+        bias_three = jnp.stack([bias_f[0], jnp.zeros_like(bias_f[0]), bias_f[1]])
+        heads = jnp.einsum("td,cdf->ctf", normed_one, weight, preferred_element_type=F32)
+        return (heads + bias_three[:, None, :]).astype(BF16)
+
+    own_heads = project(own_qkv, qv_bias)
+    own_attended, own_powers, own_inverse = attend(own_heads)
+    far_heads = project(far_qkv, far_qv_bias)
+    far_attended, far_powers, far_inverse = attend(far_heads)
+    branch = dot(own_attended, w_out, NN) + dot(far_attended, far_out, NN)
+    middle = shifted + branch + out_bias.astype(F32)
+    gain_two = norm2_gain.astype(F32)
+    scaled_two, inverse_two = normalise(middle)
+    normed_two = (scaled_two * gain_two + norm2_shift.astype(F32)).astype(BF16)
+
+    own_hidden, own_slope = hidden_layer(normed_two, w_fc1, fc1_bias.astype(F32)[None])
+    far_hidden, far_slope = hidden_layer(normed_two, far_fc1, far_fc1_bias.astype(F32)[None])
+    grad_top = cot_rows.astype(F32) * loss_weight
+    grad_low = grad_top.astype(BF16)
+
+    def reduce_core(keep, send):
+        return [(k, over(0, s)) for k, s in zip(keep, send)]
+
+    def total(pair):
+        return sum(p.astype(F32) for p in pair)
+
+    def scatter(parts):
+        for level in range(1, levels):
+            bit = bits[level]
+            send = total([part(p, 1 - bit, 2, p.ndim - 2) for p in parts]).astype(BF16)
+            parts = [part(p, bit, 2, p.ndim - 2) for p in parts] + [over(level, send)]
+            parts = [total(parts).astype(BF16)]
+        return parts[0]
+
+    def gather(mine):
+        for level in range(levels - 1, 0, -1):
+            mine = joined(bits[level], mine, over(level, mine), mine.ndim - 2)
+        return mine
+
+    def reduce_x_first(own_pair, far_pair):
+        recv = over_x(total(far_pair).astype(BF16))
+        return scatter([*own_pair, recv])
+
+    def reduce_y_first(own_pair, far_pair):
+        both = [jnp.stack([o, f]) for o, f in zip(own_pair, far_pair)]
+        bit = bits[1]
+        send = total([part(b, 1 - bit, 2, b.ndim - 2) for b in both]).astype(BF16)
+        recv = over(1, send)
+        kept = [part(b, bit, 2, b.ndim - 2) for b in both] + [recv]
+        recv_x = over_x(total([k[1] for k in kept]).astype(BF16))
+        mine = total([k[0] for k in kept] + [recv_x]).astype(BF16)
+        for level in range(2, levels):
+            bit = bits[level]
+            send = part(mine, 1 - bit, 2, mine.ndim - 2)
+            mine = total([part(mine, bit, 2, mine.ndim - 2), over(level, send)]).astype(BF16)
+        return mine
+
+    low_keep, low_send = part(grad_low, bits[0], 2, 1), part(grad_low, 1 - bits[0], 2, 1)
+
+    def fc2_parts(hidden):
+        return dot(hidden, low_keep, TN).astype(BF16), over(0, dot(hidden, low_send, TN).astype(BF16))
+
+    fc2_own_pair, fc2_far_pair = fc2_parts(own_hidden), fc2_parts(far_hidden)
+    fc2_mine = reduce_x_first(fc2_own_pair, fc2_far_pair)
+
+    def pre_grad(fc2, slope):
+        return (dot(grad_low, fc2, NT) * slope.astype(F32)).astype(BF16)
+
+    own_pre = pre_grad(w_fc2, own_slope)
+    far_pre = pre_grad(far_fc2, far_slope)
+    grad_normed_two = dot(own_pre, w_fc1, NT) + dot(far_pre, far_fc1, NT)
+    two_keep, two_send = part(normed_two, bits[0], 2, 1), part(normed_two, 1 - bits[0], 2, 1)
+
+    def fc1_parts(pre):
+        return dot(two_keep, pre, TN).astype(BF16), over(0, dot(two_send, pre, TN).astype(BF16))
+
+    fc1_own_pair, fc1_far_pair = fc1_parts(own_pre), fc1_parts(far_pre)
+    fc1_mine = reduce_y_first(fc1_own_pair, fc1_far_pair)
+
+    mlp_branch = dot(own_hidden, w_fc2, NN) + dot(far_hidden, far_fc2, NN)
+    output = (middle + mlp_branch + fc2_bias.astype(F32)).astype(BF16)
+    output_recv = over_x(output[half_rows:])
+    block_output = joined(mp_at, output[None, :half_rows], output_recv[None])
+
+    grad_from_norm, gain_two_grad, shift_two_grad = normalise_back(
+        grad_normed_two, scaled_two, inverse_two, gain_two
+    )
+    grad_middle = grad_top + grad_from_norm
+    out_bias_grad = jnp.sum(grad_middle, axis=0)
+    fc2_bias_grad = jnp.sum(grad_top, axis=0)
+    grad_branch = grad_middle.astype(BF16)
+
+    own_grad_att = dot(grad_branch, w_out, NT).astype(BF16)
+    far_grad_att = dot(grad_branch, far_out, NT).astype(BF16)
+    branch_keep, branch_send = part(grad_branch, bits[0], 2, 1), part(grad_branch, 1 - bits[0], 2, 1)
+
+    def out_parts(att):
+        return dot(att, branch_keep, TN).astype(BF16), over(0, dot(att, branch_send, TN).astype(BF16))
+
+    out_mine = reduce_x_first(out_parts(own_attended), out_parts(far_attended))
+    far_dqkv = attend_back(far_heads, far_powers, far_inverse, far_attended, far_grad_att)
+    own_dqkv = attend_back(own_heads, own_powers, own_inverse, own_attended, own_grad_att)
+    one_keep, one_send = part(normed_one, bits[0], 2, 1), part(normed_one, 1 - bits[0], 2, 1)
+
+    def qkv_parts(dqkv):
+        def one(rows):
+            return jnp.einsum("td,ctf->cdf", rows, dqkv, preferred_element_type=F32).astype(BF16)
+
+        return one(one_keep), over(0, one(one_send))
+
+    far_qkv_pair = qkv_parts(far_dqkv)
+    own_qkv_pair = qkv_parts(own_dqkv)
+    qkv_mine = reduce_x_first(own_qkv_pair, far_qkv_pair)
+
+    def back_project(dqkv, weight):
+        return jnp.einsum("ctf,cdf->td", dqkv, weight, preferred_element_type=F32)
+
+    grad_normed_one = back_project(far_dqkv, far_qkv) + back_project(own_dqkv, own_qkv)
+    grad_in_one, gain_one_grad, shift_one_grad = normalise_back(
+        grad_normed_one, scaled_one, inverse_one, gain_one
+    )
+    grad_shifted = grad_middle + grad_in_one
+    grad_recv = over_x(grad_shifted[half_rows:].astype(BF16)).astype(F32)
+    input_grad = joined(mp_at, grad_shifted[None, :half_rows], grad_recv[None])
+
+    bucket_rows = jnp.arange(counts.shape[0], dtype=jnp.int32)[:, None] == bucket
+    lead_part = jnp.where(bucket_rows, jnp.sum(grad_shifted, axis=0)[None], 0.0)
+
+    def column_sums(value):
+        return jnp.sum(value.astype(F32), axis=-2)
+
+    own_bias, far_bias = column_sums(own_dqkv), column_sums(far_dqkv)
+    qv_bias_part = joined(mp_at, own_bias, far_bias, 1)
+    fc1_bias_part = joined(mp_at, column_sums(own_pre), column_sums(far_pre), 0)
+    vectors = jnp.concatenate(
+        [
+            lead_part,
+            jnp.stack(
+                [gain_one_grad, shift_one_grad, out_bias_grad, gain_two_grad, shift_two_grad, fc2_bias_grad]
+            ),
+            qv_bias_part[0::2],
+            fc1_bias_part.reshape(-1, width),
+        ]
+    )
+    vectors = vectors + over_x(vectors)
+    for level in range(levels):
+        vectors = vectors + over(level, vectors)
+    table = counts.shape[0]
+    lead_grad, singles, rest = vectors[:table], vectors[table : table + 6], vectors[table + 6 :]
+    qv_bias_grad = part(rest[:2], mp_at, 2, 1)
+    fc1_bias_grad = part(rest[2:].reshape(-1), mp_at, 2)
+
+    fc2_half, fc1_half, out_half, qkv_half = gather(fc2_mine), gather(fc1_mine), gather(out_mine), gather(qkv_mine)
+
+    def finish(half, axis):
+        return joined(bits[0], half, over(0, half), axis).astype(F32)
+
+    fc2_grad = finish(fc2_half, 1)
+    fc1_grad = finish(fc1_half, 0)
+    out_grad = finish(out_half, 1)
+    qkv_grad = jnp.transpose(finish(qkv_half, 1), (1, 0, 2))
+    return (
+        block_output,
+        input_grad,
+        lead_grad,
+        singles[0],
+        singles[1],
+        qkv_grad,
+        qv_bias_grad,
+        out_grad,
+        singles[2],
+        singles[3],
+        singles[4],
+        fc1_grad,
+        fc1_bias_grad,
+        fc2_grad,
+        singles[5],
+    )
+
+
 def solution(mesh):
     in_specs = (
         P("dp", "mp", None),
@@ -309,4 +742,10 @@
         P("mp", None),
         P(),
     )
-    return jax.shard_map(body, mesh=mesh, in_specs=in_specs, out_specs=out_specs, check_vma=False)
+    def local(*args):
+        replicas = lax.axis_size("dp")
+        one_each = args[0].shape[0] == 2 and lax.axis_size("mp") == 2
+        chosen = fast_body if one_each and replicas >= 4 and replicas & (replicas - 1) == 0 else body
+        return chosen(*args)
+
+    return jax.shard_map(local, mesh=mesh, in_specs=in_specs, out_specs=out_specs, check_vma=False)

time: 1250 us -> 683 us (0.55)
  matrix products: 375 us -> 133 us
  waiting for transfers between devices: 502 us -> 284 us
  other arithmetic: 188 us -> 79.6 us
  Pallas kernels: 0 us -> 97.3 us
  blocking collectives: 82.4 us -> 0 us
  starting transfers between devices: 0.36 us -> 49.4 us
  local copies, waits for them, and re-layouts: 72 us -> 25.3 us
    ppermute x0 -> x59, waiting for transfers between devices: none -> 284 us  [the longest x46 159 us: over(): lax.ppermute(value, 'dp', [(i, i ^ 1 << level) for i in range(replicas)])]
    dot_general x28 -> x30, matrix products: 375 us -> 133 us  [the longest x22 98.6 us: dot(): return lax.dot_general(left, right, dims, preferred_element_type=F32)]
    all_gather x4 -> x0, waiting for transfers between devices: 240 us -> none  [the longest x1 99.5 us: body(): lax.all_gather(w_fc1, 'mp', axis=1, tiled=True)]
    psum x1 -> x0, waiting for transfers between devices: 169 us -> none  [body(): lax.psum(qkv_grad.astype(jnp.bfloat16), 'dp').astype(jnp.float32)]
    convert_element_type x23 -> x33, other arithmetic: 132 us -> 33.6 us  [the longest x3 10.1 us: finish(): return joined(bits[0], half, over(0, half), axis).astype(F32)]
    pallas_call x0 -> x6, Pallas kernels: none -> 97.3 us  [the longest x2 43.9 us: attend_back(): pl.pallas_call(functools.partial(attention_backward_kernel, min(512, rows...]
    reduce_scatter x4 -> x0, waiting for transfers between devices: 92 us -> none  [the longest x1 92 us: body(): lax.psum_scatter(jnp.einsum('tsf,fd->tsd', picked, w_out, preferred_eleme...]
    psum x2 -> x0, blocking collectives: 72.9 us -> none  [the longest x1 39.2 us: body(): lead_grad, small_grads = lax.psum((lead_grad, small_grads), ('dp', 'mp'))]
  transfers between devices with their start and end apart: 9 -> 59, of which waited for: 5 -> 26; matrix products, arithmetic and copies ran while one was open for 34% -> 33% of each run, Pallas kernels for 0% -> 14%
where the time goes in v1:
time: 683 us; the launch traced here: 674 us
  waiting for transfers between devices  284 us (42%)
  matrix products  133 us (19%)
  Pallas kernels  97.3 us (14%)
  other arithmetic  79.6 us (12%)
  starting transfers between devices  49.4 us (7%)
  local copies, waits for them, and re-layouts  25.3 us (4%)
    ppermute x46, waiting for transfers between devices, over(): lax.ppermute(value, 'dp', [(i, i ^ 1 << level) for i in range(replicas)])  159 us
    ppermute x13, waiting for transfers between devices, over_x(): return lax.ppermute(value, 'mp', [(0, 1), (1, 0)])  125 us
    dot_general x22, matrix products, dot(): return lax.dot_general(left, right, dims, preferred_element_type=F32)  98.6 us
    pallas_call x2, Pallas kernels, attend_back(): pl.pallas_call(functools.partial(attention_backward_kernel, min(512, rows...  43.9 us
    pallas_call x2, Pallas kernels, attend(): pl.pallas_call(attention_forward_kernel, out_shape=(jax.ShapeDtypeStruct(...  35 us
    ppermute x46, starting transfers between devices, over(): lax.ppermute(value, 'dp', [(i, i ^ 1 << level) for i in range(replicas)])  32.6 us
    select_n x20, other arithmetic, joined(): jnp.where(bit == 0, jnp.concatenate([mine, theirs], axis), jnp.concatenat...  22.5 us
    pallas_call x2, Pallas kernels, hidden_layer(): pl.pallas_call(hidden_kernel, out_shape=(jax.ShapeDtypeStruct((rows, unit...  18.3 us
  transfers between devices with their start and end apart: 59, of which 26 were waited for; matrix products, arithmetic and copies ran while one was open for 33% of the time, Pallas kernels for 14%

profile of v1, /device:TPU:0, one launch (start us, length us, event | category | flops | bytes accessed | tf_op | source)
XLA Modules:
  0.0 674.0 jit_solution(7311773002383364499)
XLA Ops:
  2.4 2.7 dynamic-slice_bitcast_fusion.3
  6.2 2.9 collective-permute-start
  25.3 8.0 %collective-permute-done = bf16[528,1024]{1,0:T(8,128)(2,1)} collective-permute-done((bf16[528,1024]{1,0:T(8,128)(2,1)}, bf16[528,1024]{1,0:T(8,128)(2,1)}, u32[]{:S(2)}, u32[]{:S(2)}) %collective-permute-start) | collective-permute-done | bytes 1081376 | tf_op jit(solution)/shard_map/ppermute | solution.py:455
  40.4 28.6 %collective-permute-done.1 = bf16[1536,512]{1,0:T(8,128)(2,1)} collective-permute-done((bf16[1536,512]{1,0:T(8,128)(2,1)S(1)}, bf16[1536,512]{1,0:T(8,128)(2,1)}, u32[]{:S(2)}, u32[]{:S(2)}) %collective-permute-start.1) | collective-permute-done | bytes 1572896 | tf_op jit(solution)/shard_map/ppermute | solution.py:455
  69.0 3.7 fusion.7.qkv_ref
  74.3 17.4 %attention_forward.2 = (bf16[1024,512]{1,0:T(8,128)(2,1)S(1)}, bf16[8,1024,1024]{2,1,0:T(8,128)(2,1)}, f32[4,2,1024]{2,1,0:T(2,128)S(1)}) custom-call(bf16[3,1024,512]{2,1,0:T(8,128)(2,1)S(1)} %fusion.7.qkv_ref), custom_call_target="tpu_custom_call" | custom-call | flops 8589934592 | bytes 20971520 | tf_op jit(solution)/shard_map/attention_forward/pallas_call | solution.py:343
  93.1 4.5 fusion.89
  97.6 12.4 %collective-permute-done.3 = bf16[256,1024]{1,0:T(8,128)(2,1)} collective-permute-done((bf16[256,1024]{1,0:T(8,128)(2,1)S(1)}, bf16[256,1024]{1,0:T(8,128)(2,1)}, u32[]{:S(2)}, u32[]{:S(2)}) %collective-permute-start.3) | collective-permute-done | bytes 524320 | tf_op jit(solution)/shard_map/ppermute | solution.py:455
  113.9 3.3 maximum_select_fusion.5
  118.9 3.7 fusion.8.qkv_ref
  122.6 17.6 %attention_forward.3 = (bf16[1024,512]{1,0:T(8,128)(2,1)S(1)}, bf16[8,1024,1024]{2,1,0:T(8,128)(2,1)}, f32[4,2,1024]{2,1,0:T(2,128)S(1)}) custom-call(bf16[3,1024,512]{2,1,0:T(8,128)(2,1)S(1)} %fusion.8.qkv_ref), custom_call_target="tpu_custom_call" | custom-call | flops 8589934592 | bytes 20971520 | tf_op jit(solution)/shard_map/attention_forward/pallas_call | solution.py:343
  140.3 4.7 fusion.88
  147.0 9.2 %hidden_layer.2 = (bf16[1024,2048]{1,0:T(8,128)(2,1)S(1)}, bf16[1024,2048]{1,0:T(8,128)(2,1)S(1)}) custom-call(bf16[1024,1024]{1,0:T(8,128)(2,1)S(1)} %add_convert_fusion.5.normed_ref, bf16[1024,2048]{1,0:T(8,128)(2,1)S(1)} %copy-done.9, f32[1,2048]{1,0:T(1,128)S(1)} %bitcast.153), custom_call_target="tpu_custom_call" | custom-call | flops 4294967296 | bytes 14680064 | tf_op jit(solution)/shard_map/hidden_layer/pallas_call | solution.py:406
  156.2 6.0 fusion.90
  162.2 3.8 maximum_select_fusion.7
  167.2 9.0 %convert_reduce_fusion.1 = (f32[2048]{0:T(1024)S(1)}, bf16[1024,2048]{1,0:T(8,128)(2,1)}) fusion(bf16[1024,2048]{1,0:T(8,128)(2,1)S(1)} %get-tuple-element.39, bf16[1024,1024]{1,0:T(8,128)(2,1)S(1)} %fusion.3, bf16[2048,1024]{1,0:T(8,128)(2,1)} %param.32), kind=kOutput, calls=%fused_computation.1 | convolution fusion | flops 4305451008 | bytes 14688256 | tf_op jit(solution)/shard_map/dot_general | solution.py:287
  176.2 3.9 convolution_convert_fusion.2
  180.1 3.8 convolution_convert_fusion.5
  183.9 7.9 %collective-permute-done.9 = bf16[512,1024]{1,0:T(8,128)(2,1)S(1)} collective-permute-done((bf16[512,1024]{1,0:T(8,128)(2,1)}, bf16[512,1024]{1,0:T(8,128)(2,1)S(1)}, u32[]{:S(2)}, u32[]{:S(2)}) %collective-permute-start.9) | collective-permute-done | bytes 1048608 | tf_op jit(solution)/shard_map/ppermute | solution.py:455
  192.3 6.1 fusion.91
  198.4 18.1 %collective-permute-done.10 = bf16[512,1024]{1,0:T(8,128)(2,1)S(1)} collective-permute-done((bf16[512,1024]{1,0:T(8,128)(2,1)S(1)}, bf16[512,1024]{1,0:T(8,128)(2,1)S(1)}, u32[]{:S(2)}, u32[]{:S(2)}) %collective-permute-start.10) | collective-permute-done | bytes 1048608 | tf_op jit(solution)/shard_map/ppermute | solution.py:458
  218.9 3.7 fusion.14
  222.6 5.0 maximum_select_fusion.weight_ref
  227.6 9.2 %hidden_layer.3 = (bf16[1024,2048]{1,0:T(8,128)(2,1)S(1)}, bf16[1024,2048]{1,0:T(8,128)(2,1)S(1)}) custom-call(bf16[1024,1024]{1,0:T(8,128)(2,1)S(1)} %copy-done.7, bf16[1024,2048]{1,0:T(8,128)(2,1)S(1)} %maximum_select_fusion.weight_ref, f32[1,2048]{1,0:T(1,128)S(1)} %bitcast.154), custom_call_target="tpu_custom_call" | custom-call | flops 4294967296 | bytes 14680064 | tf_op jit(solution)/shard_map/hidden_layer/pallas_call | solution.py:406
  236.8 4.0 convolution_convert_fusion
  241.4 3.8 convolution_convert_fusion.1
  245.2 11.6 %convert_reduce_fusion = (f32[2048]{0:T(1024)S(1)}, bf16[1024,2048]{1,0:T(8,128)(2,1)}) fusion(bf16[1024,2048]{1,0:T(8,128)(2,1)} %copy-done.19, bf16[1024,1024]{1,0:T(8,128)(2,1)S(1)} %copy-done.48, bf16[1024,1024]{1,0:T(8,128)(2,1)} %collective-permute-done.11, bf16[1024,1024]{1,0:T(8,128)(2,1)} %maximum_select_fusion.8, pred[]{:T(512)S(6)} %eq.20), kind=kOutput, calls=%fused_computation | convolution fusion | flops 4324325376 | bytes 14688257 | tf_op jit(solution)/shard_map/dot_general | solution.py:287
  256.8 10.5 %multiply_reduce_fusion = (f32[1024]{0:T(1024)S(1)}, f32[1024]{0:T(1024)S(1)}, f32[1024]{0:T(1024)S(1)}, f32[1024]{0:T(1024)S(1)}, f32[1024,1024]{1,0:T(8,128)}) fusion(f32[1024,1024]{1,0:T(8,128)S(1)} %copy-done.23, f32[1024]{0:T(1024)S(1)} %add_rsqrt_fusion, f32[1024]{0:T(1024)S(1)} %broadcast_multiply_fusion.4, f32[1024]{0:T(1024)S(1)} %convert_element_type.431, ...), kind=kOutput, calls=%fused_computation.27 | convolution fusion | flops 4305448960 | bytes 21000192 | tf_op jit(solution)/shard_map/dot_general | solution.py:287
  267.3 4.5 fusion.83
  277.4 3.8 convolution_convert_fusion.4
  281.2 21.9 %attention_backward.3 = bf16[3,1024,512]{2,1,0:T(8,128)(2,1)S(1)} custom-call(bf16[3,1024,512]{2,1,0:T(8,128)(2,1)} %copy-done.20, bf16[8,1024,1024]{2,1,0:T(8,128)(2,1)} %get-tuple-element.43.power_ref, f32[4,2,1024]{2,1,0:T(2,128)S(1)} %get-tuple-element.44.inverse_ref, bf16[1024,512]{1,0:T(8,128)(2,1)S(1)} %copy-done.11, ...), custom_call_target="tpu_custom_call" | custom-call | flops 17179869184 | bytes 25165824 | tf_op jit(solution)/shard_map/attention_backward/pallas_call | solution.py:369
  303.1 5.5 fusion.10
  311.1 22.0 %attention_backward.2 = bf16[3,1024,512]{2,1,0:T(8,128)(2,1)S(1)} custom-call(bf16[3,1024,512]{2,1,0:T(8,128)(2,1)} %copy-done.21, bf16[8,1024,1024]{2,1,0:T(8,128)(2,1)} %get-tuple-element.41.power_ref, f32[4,2,1024]{2,1,0:T(2,128)S(1)} %get-tuple-element.42.inverse_ref, bf16[1024,512]{1,0:T(8,128)(2,1)S(1)} %copy-done.13, ...), custom_call_target="tpu_custom_call" | custom-call | flops 17179869184 | bytes 25165824 | tf_op jit(solution)/shard_map/attention_backward/pallas_call | solution.py:369
  333.2 5.4 fusion.33
  338.7 4.7 multiply_reduce_fusion.1
  344.1 3.9 fusion.84
  352.8 3.9 add_convert_fusion.2
  357.4 4.5 fusion.32
  368.3 10.1 %collective-permute-done.31 = bf16[512,512]{1,0:T(8,128)(2,1)S(1)} collective-permute-done((bf16[512,512]{1,0:T(8,128)(2,1)S(1)}, bf16[512,512]{1,0:T(8,128)(2,1)S(1)}, u32[]{:S(2)}, u32[]{:S(2)}) %collective-permute-start.31) | collective-permute-done | bytes 524320 | tf_op jit(solution)/shard_map/ppermute | solution.py:455
  380.1 4.5 fusion.9
  388.7 4.6 collective-permute-done.32
  401.6 25.5 %collective-permute-done.51 = bf16[2048,512]{1,0:T(8,128)(2,1)S(1)} collective-permute-done((bf16[2048,512]{1,0:T(8,128)(2,1)S(1)}, bf16[2048,512]{1,0:T(8,128)(2,1)S(1)}, u32[]{:S(2)}, u32[]{:S(2)}) %collective-permute-start.51) | collective-permute-done | bytes 2097184 | tf_op jit(solution)/shard_map/ppermute | solution.py:455
  431.6 28.7 %collective-permute-done.21 = bf16[3,512,512]{2,1,0:T(8,128)(2,1)S(1)} collective-permute-done((bf16[3,512,512]{2,1,0:T(8,128)(2,1)}, bf16[3,512,512]{2,1,0:T(8,128)(2,1)S(1)}, u32[]{:S(2)}, u32[]{:S(2)}) %collective-permute-start.21) | collective-permute-done | bytes 1572896 | tf_op jit(solution)/shard_map/ppermute | solution.py:455
  460.3 2.9 fusion.28
  466.8 7.9 %add_convert_fusion.4 = bf16[1024,1024]{1,0:T(8,128)(2,1)S(1)} fusion(f32[1024,1024]{1,0:T(8,128)S(1)} %copy-done.25, f32[1024,1024]{1,0:T(8,128)} %fusion.90, f32[1024]{0:T(1024)S(1)} %copy-done.71, bf16[1024,2048]{1,0:T(8,128)(2,1)S(1)} %copy-done.16, bf16[1024,1024]{1,0:T(8,128)(2,1)} %collective-permute-done.11, ...), kind=kOutput, calls=%fused_computation.36 | convolution fusion | flops 4318035968 | bytes 18878464 | tf_op jit(solution)/shard_map/dot_general | solution.py:287
  486.3 4.0 collective-permute-done.42
  498.1 13.3 %collective-permute-done.23 = bf16[3,128,512]{2,1,0:T(8,128)(2,1)S(1)} collective-permute-done((bf16[3,128,512]{2,1,0:T(8,128)(2,1)S(1)}, bf16[3,128,512]{2,1,0:T(8,128)(2,1)S(1)}, u32[]{:S(2)}, u32[]{:S(2)}) %collective-permute-start.23) | collective-permute-done | bytes 393248 | tf_op jit(solution)/shard_map/ppermute | solution.py:458
  511.6 9.5 %collective-permute-done.43 = bf16[128,2048]{1,0:T(8,128)(2,1)S(1)} collective-permute-done((bf16[128,2048]{1,0:T(8,128)(2,1)S(1)}, bf16[128,2048]{1,0:T(8,128)(2,1)S(1)}, u32[]{:S(2)}, u32[]{:S(2)}) %collective-permute-start.43) | collective-permute-done | bytes 524320 | tf_op jit(solution)/shard_map/ppermute | solution.py:458
  521.6 2.9 collective-permute-start.55
  524.5 16.8 %collective-permute-done.24 = bf16[3,64,512]{2,1,0:T(8,128)(2,1)S(1)} collective-permute-done((bf16[3,64,512]{2,1,0:T(8,128)(2,1)S(1)}, bf16[3,64,512]{2,1,0:T(8,128)(2,1)S(1)}, u32[]{:S(2)}, u32[]{:S(2)}) %collective-permute-start.24) | collective-permute-done | bytes 196640 | tf_op jit(solution)/shard_map/ppermute | solution.py:458
  541.4 11.1 %collective-permute-done.44 = bf16[64,2048]{1,0:T(8,128)(2,1)S(1)} collective-permute-done((bf16[64,2048]{1,0:T(8,128)(2,1)S(1)}, bf16[64,2048]{1,0:T(8,128)(2,1)S(1)}, u32[]{:S(2)}, u32[]{:S(2)}) %collective-permute-start.44) | collective-permute-done | bytes 262176 | tf_op jit(solution)/shard_map/ppermute | solution.py:458
  552.7 2.9 collective-permute-start.34
  555.6 6.2 collective-permute-done.55
  562.0 3.9 collective-permute-done.25
  566.1 4.6 collective-permute-done.45
  574.3 12.0 %collective-permute-done.56 = bf16[512,512]{1,0:T(8,128)(2,1)S(1)} collective-permute-done((bf16[512,512]{1,0:T(8,128)(2,1)S(1)}, bf16[512,512]{1,0:T(8,128)(2,1)S(1)}, u32[]{:S(2)}, u32[]{:S(2)}) %collective-permute-start.56) | collective-permute-done | bytes 524320 | tf_op jit(solution)/shard_map/ppermute | solution.py:458
  588.3 6.4 collective-permute-done.26
  596.6 7.9 %collective-permute-done.46 = bf16[128,2048]{1,0:T(8,128)(2,1)S(1)} collective-permute-done((bf16[128,2048]{1,0:T(8,128)(2,1)S(1)}, bf16[128,2048]{1,0:T(8,128)(2,1)S(1)}, u32[]{:S(2)}, u32[]{:S(2)}) %collective-permute-start.46) | collective-permute-done | bytes 524320 | tf_op jit(solution)/shard_map/ppermute | solution.py:458
  608.7 4.3 collective-permute-done.36
  615.7 14.0 %collective-permute-done.27 = bf16[3,256,512]{2,1,0:T(8,128)(2,1)S(1)} collective-permute-done((bf16[3,256,512]{2,1,0:T(8,128)(2,1)S(1)}, bf16[3,256,512]{2,1,0:T(8,128)(2,1)S(1)}, u32[]{:S(2)}, u32[]{:S(2)}) %collective-permute-start.27) | collective-permute-done | bytes 786464 | tf_op jit(solution)/shard_map/ppermute | solution.py:458
  630.3 20.9 %collective-permute-done.47 = bf16[256,2048]{1,0:T(8,128)(2,1)S(1)} collective-permute-done((bf16[256,2048]{1,0:T(8,128)(2,1)S(1)}, bf16[256,2048]{1,0:T(8,128)(2,1)S(1)}, u32[]{:S(2)}, u32[]{:S(2)}) %collective-permute-start.47) | collective-permute-done | bytes 1048608 | tf_op jit(solution)/shard_map/ppermute | solution.py:458
  662.0 3.1 convert_bitcast_fusion
  665.1 4.0 fusion.1
  669.1 4.4 fusion
  (390 shorter events, 126.7 us)
Async XLA Ops:
  6.2 27.1 %collective-permute-start = (bf16[528,1024]{1,0:T(8,128)(2,1)}, bf16[528,1024]{1,0:T(8,128)(2,1)}, u32[]{:S(2)}, u32[]{:S(2)}) collective-permute-start(bf16[528,1024]{1,0:T(8,128)(2,1)} %pad_maximum_fusion.2), channel_id=1, source_target_pairs={{0,1},{1,0},{2,3},{3,2},{4,5},{5,4},{6,7},{7,6},{8,9},{9,8},{10,11... | collective-permute-start | bytes 3244040 | tf_op jit(solution)/shard_map/ppermute | solution.py:455
  13.0 127.2 %copy-start.61 = (f32[1,1024]{1,0:T(1,128)}, f32[1,1024]{1,0:T(1,128)S(1)}, u32[]{:S(2)}) copy-start(f32[1,1024]{1,0:T(1,128)S(1)} %fusion.78) | copy-start | bytes 12292
  23.9 142.7 %copy-start.31 = (bf16[512,1024]{1,0:T(8,128)(2,1)}, bf16[512,1024]{1,0:T(8,128)(2,1)S(1)}, u32[]{:S(2)}) copy-start(bf16[512,1024]{1,0:T(8,128)(2,1)S(1)} %get-tuple-element.58) | copy-start | bytes 3145732
  33.3 35.7 %collective-permute-start.1 = (bf16[1536,512]{1,0:T(8,128)(2,1)S(1)}, bf16[1536,512]{1,0:T(8,128)(2,1)}, u32[]{:S(2)}, u32[]{:S(2)}) collective-permute-start(bf16[1536,512]{1,0:T(8,128)(2,1)S(1)} %constant_dynamic-slice_fusion.12), channel_id=1, source_target_pairs={{0,1},{1,0},{2,3},{3,2},{4,5},{5,4},{6,7},{7,6},{8,9},{9,8},{10,11... | collective-permute-start | bytes 4718600 | tf_op jit(solution)/shard_map/ppermute | solution.py:455
  37.1 103.2 %copy-start.28 = (bf16[512,1024]{1,0:T(8,128)(2,1)}, bf16[512,1024]{1,0:T(8,128)(2,1)S(1)}, u32[]{:S(2)}) copy-start(bf16[512,1024]{1,0:T(8,128)(2,1)S(1)} %slice.126) | copy-start | bytes 3145732
  69.0 44.9 %collective-permute-start.2 = (bf16[1536,512]{1,0:T(8,128)(2,1)}, bf16[1536,512]{1,0:T(8,128)(2,1)}, u32[]{:S(2)}, u32[]{:S(2)}) collective-permute-start(bf16[1536,512]{1,0:T(8,128)(2,1)} %collective-permute-done.1), channel_id=1, source_target_pairs={{0,2},{2,0},{4,6},{6,4},{8,10},{10,8},{12,14},{14,12},{16,18},{18,... | collective-permute-start | bytes 4718600 | tf_op jit(solution)/shard_map/ppermute | solution.py:458
  72.8 37.2 %collective-permute-start.5 = (bf16[256,2048]{1,0:T(8,128)(2,1)}, bf16[256,2048]{1,0:T(8,128)(2,1)S(1)}, u32[]{:S(2)}, u32[]{:S(2)}) collective-permute-start(bf16[256,2048]{1,0:T(8,128)(2,1)} %constant_dynamic-slice_fusion.10), channel_id=1, source_target_pairs={{0,1},{1,0},{2,3},{3,2},{4,5},{5,4},{6,7},{7,6},{8,9},{9,8},{10,11... | collective-permute-start | bytes 3145736 | tf_op jit(solution)/shard_map/ppermute | solution.py:455
  91.7 18.2 %collective-permute-start.3 = (bf16[256,1024]{1,0:T(8,128)(2,1)S(1)}, bf16[256,1024]{1,0:T(8,128)(2,1)}, u32[]{:S(2)}, u32[]{:S(2)}) collective-permute-start(bf16[256,1024]{1,0:T(8,128)(2,1)S(1)} %copy-done.58), channel_id=1, source_target_pairs={{0,1},{1,0},{2,3},{3,2},{4,5},{5,4},{6,7},{7,6},{8,9},{9,8},{10,11... | collective-permute-start | bytes 1572872 | tf_op jit(solution)/shard_map/ppermute | solution.py:455
  110.0 30.3 %collective-permute-start.4 = (bf16[256,1024]{1,0:T(8,128)(2,1)}, bf16[256,1024]{1,0:T(8,128)(2,1)S(1)}, u32[]{:S(2)}, u32[]{:S(2)}) collective-permute-start(bf16[256,1024]{1,0:T(8,128)(2,1)} %collective-permute-done.3), channel_id=1, source_target_pairs={{0,2},{2,0},{4,6},{6,4},{8,10},{10,8},{12,14},{14,12},{16,18},{18,... | collective-permute-start | bytes 1572872 | tf_op jit(solution)/shard_map/ppermute | solution.py:458
  110.9 55.1 %collective-permute-start.8 = (bf16[512,1024]{1,0:T(8,128)(2,1)}, bf16[512,1024]{1,0:T(8,128)(2,1)S(1)}, u32[]{:S(2)}, u32[]{:S(2)}) collective-permute-start(bf16[512,1024]{1,0:T(8,128)(2,1)} %get-tuple-element.37), channel_id=1, source_target_pairs={{0,1},{1,0},{2,3},{3,2},{4,5},{5,4},{6,7},{7,6},{8,9},{9,8},{10,11... | collective-permute-start | bytes 3145736 | tf_op jit(solution)/shard_map/ppermute | solution.py:455
  112.4 49.8 %collective-permute-start.6 = (bf16[256,2048]{1,0:T(8,128)(2,1)}, bf16[256,2048]{1,0:T(8,128)(2,1)}, u32[]{:S(2)}, u32[]{:S(2)}) collective-permute-start(bf16[256,2048]{1,0:T(8,128)(2,1)} %copy-done.54), channel_id=1, source_target_pairs={{0,4},{2,6},{4,0},{6,2},{8,12},{10,14},{12,8},{14,10},{16,20},{18,... | collective-permute-start | bytes 3145736 | tf_op jit(solution)/shard_map/ppermute | solution.py:458
  147.0 71.9 %copy-start.6 = (bf16[1024,1024]{1,0:T(8,128)(2,1)}, bf16[1024,1024]{1,0:T(8,128)(2,1)S(1)}, u32[]{:S(2)}) copy-start(bf16[1024,1024]{1,0:T(8,128)(2,1)S(1)} %add_convert_fusion.5.normed_ref) | copy-start | bytes 6291460
  166.0 56.6 %collective-permute-start.7 = (bf16[512,2048]{1,0:T(8,128)(2,1)}, bf16[512,2048]{1,0:T(8,128)(2,1)}, u32[]{:S(2)}, u32[]{:S(2)}) collective-permute-start(bf16[512,2048]{1,0:T(8,128)(2,1)} %maximum_select_fusion.7), channel_id=1, source_target_pairs={{0,2},{2,0},{4,6},{6,4},{8,10},{10,8},{12,14},{14,12},{16,18},{18,... | collective-permute-start | bytes 6291464 | tf_op jit(solution)/shard_map/ppermute | solution.py:458
  166.0 25.8 %collective-permute-start.9 = (bf16[512,1024]{1,0:T(8,128)(2,1)}, bf16[512,1024]{1,0:T(8,128)(2,1)S(1)}, u32[]{:S(2)}, u32[]{:S(2)}) collective-permute-start(bf16[512,1024]{1,0:T(8,128)(2,1)} %constant_dynamic-slice_fusion.9), channel_id=1, source_target_pairs={{0,1},{1,0},{2,3},{3,2},{4,5},{5,4},{6,7},{7,6},{8,9},{9,8},{10,11... | collective-permute-start | bytes 3145736 | tf_op jit(solution)/shard_map/ppermute | solution.py:455
  183.8 200.7 %collective-permute-start.39 = (bf16[512,2048]{1,0:T(8,128)(2,1)}, bf16[512,2048]{1,0:T(8,128)(2,1)}, u32[]{:S(2)}, u32[]{:S(2)}) collective-permute-start(bf16[512,2048]{1,0:T(8,128)(2,1)} %convolution_convert_fusion.5), channel_id=1, source_target_pairs={{0,2},{2,0},{4,6},{6,4},{8,10},{10,8},{12,14},{14,12},{16,18},{18,... | collective-permute-start | bytes 6291464 | tf_op jit(solution)/shard_map/ppermute | solution.py:458
  191.8 24.7 %collective-permute-start.10 = (bf16[512,1024]{1,0:T(8,128)(2,1)S(1)}, bf16[512,1024]{1,0:T(8,128)(2,1)S(1)}, u32[]{:S(2)}, u32[]{:S(2)}) collective-permute-start(bf16[512,1024]{1,0:T(8,128)(2,1)S(1)} %collective-permute-done.9), channel_id=1, source_target_pairs={{0,4},{2,6},{4,0},{6,2},{8,12},{10,14},{12,8},{14,10},{16,20},{18,... | collective-permute-start | bytes 3145736 | tf_op jit(solution)/shard_map/ppermute | solution.py:458
  218.9 26.3 %collective-permute-start.11 = (bf16[1024,1024]{1,0:T(8,128)(2,1)}, bf16[1024,1024]{1,0:T(8,128)(2,1)}, u32[]{:S(2)}, u32[]{:S(2)}) collective-permute-start(bf16[1024,1024]{1,0:T(8,128)(2,1)} %maximum_select_fusion.8), channel_id=1, source_target_pairs={{0,2},{2,0},{4,6},{6,4},{8,10},{10,8},{12,14},{14,12},{16,18},{18,... | collective-permute-start | bytes 6291464 | tf_op jit(solution)/shard_map/ppermute | solution.py:458
  240.8 111.3 %collective-permute-start.50 = (bf16[2048,512]{1,0:T(8,128)(2,1)}, bf16[2048,512]{1,0:T(8,128)(2,1)}, u32[]{:S(2)}, u32[]{:S(2)}) collective-permute-start(bf16[2048,512]{1,0:T(8,128)(2,1)} %convolution_convert_fusion), channel_id=1, source_target_pairs={{0,2},{2,0},{4,6},{6,4},{8,10},{10,8},{12,14},{14,12},{16,18},{18,... | collective-permute-start | bytes 6291464 | tf_op jit(solution)/shard_map/ppermute | solution.py:458
  343.4 35.1 %collective-permute-start.20 = (bf16[3,512,512]{2,1,0:T(8,128)(2,1)}, bf16[3,512,512]{2,1,0:T(8,128)(2,1)}, u32[]{:S(2)}, u32[]{:S(2)}) collective-permute-start(bf16[3,512,512]{2,1,0:T(8,128)(2,1)} %fusion.33), channel_id=1, source_target_pairs={{0,2},{2,0},{4,6},{6,4},{8,10},{10,8},{12,14},{14,12},{16,18},{18,... | collective-permute-start | bytes 4718600 | tf_op jit(solution)/shard_map/ppermute | solution.py:458
  343.5 18.5 %collective-permute-start.30 = (bf16[512,512]{1,0:T(8,128)(2,1)}, bf16[512,512]{1,0:T(8,128)(2,1)}, u32[]{:S(2)}, u32[]{:S(2)}) collective-permute-start(bf16[512,512]{1,0:T(8,128)(2,1)} %convolution_convert_fusion.14), channel_id=1, source_target_pairs={{0,2},{2,0},{4,6},{6,4},{8,10},{10,8},{12,14},{14,12},{16,18},{18,... | collective-permute-start | bytes 1572872 | tf_op jit(solution)/shard_map/ppermute | solution.py:458
  344.0 40.8 %collective-permute-start.40 = (bf16[512,2048]{1,0:T(8,128)(2,1)}, bf16[512,2048]{1,0:T(8,128)(2,1)}, u32[]{:S(2)}, u32[]{:S(2)}) collective-permute-start(bf16[512,2048]{1,0:T(8,128)(2,1)} %convolution_convert_fusion.4), channel_id=1, source_target_pairs={{0,2},{2,0},{4,6},{6,4},{8,10},{10,8},{12,14},{14,12},{16,18},{18,... | collective-permute-start | bytes 6291464 | tf_op jit(solution)/shard_map/ppermute | solution.py:458
  356.8 7.2 %collective-permute-start.14 = (f32[20,1024]{1,0:T(8,128)S(1)}, f32[20,1024]{1,0:T(8,128)S(1)}, u32[]{:S(2)}, u32[]{:S(2)}) collective-permute-start(f32[20,1024]{1,0:T(8,128)S(1)} %concatenate.203), channel_id=1, source_target_pairs={{0,1},{1,0},{2,3},{3,2},{4,5},{5,4},{6,7},{7,6},{8,9},{9,8},{10,11... | collective-permute-start | bytes 245768 | tf_op jit(solution)/shard_map/ppermute | solution.py:455
  362.0 6.1 collective-permute-start.29
  364.1 14.3 %collective-permute-start.31 = (bf16[512,512]{1,0:T(8,128)(2,1)S(1)}, bf16[512,512]{1,0:T(8,128)(2,1)S(1)}, u32[]{:S(2)}, u32[]{:S(2)}) collective-permute-start(bf16[512,512]{1,0:T(8,128)(2,1)S(1)} %fusion.36), channel_id=1, source_target_pairs={{0,1},{1,0},{2,3},{3,2},{4,5},{5,4},{6,7},{7,6},{8,9},{9,8},{10,11... | collective-permute-start | bytes 1572872 | tf_op jit(solution)/shard_map/ppermute | solution.py:455
  368.1 31.9 %collective-permute-start.49 = (bf16[2048,512]{1,0:T(8,128)(2,1)S(1)}, bf16[2048,512]{1,0:T(8,128)(2,1)S(1)}, u32[]{:S(2)}, u32[]{:S(2)}) collective-permute-start(bf16[2048,512]{1,0:T(8,128)(2,1)S(1)} %copy-done.79), channel_id=1, source_target_pairs={{0,2},{2,0},{4,6},{6,4},{8,10},{10,8},{12,14},{14,12},{16,18},{18,... | collective-permute-start | bytes 6291464 | tf_op jit(solution)/shard_map/ppermute | solution.py:458
  378.4 52.7 %collective-permute-start.19 = (bf16[3,512,512]{2,1,0:T(8,128)(2,1)}, bf16[3,512,512]{2,1,0:T(8,128)(2,1)}, u32[]{:S(2)}, u32[]{:S(2)}) collective-permute-start(bf16[3,512,512]{2,1,0:T(8,128)(2,1)} %fusion.32), channel_id=1, source_target_pairs={{0,2},{2,0},{4,6},{6,4},{8,10},{10,8},{12,14},{14,12},{16,18},{18,... | collective-permute-start | bytes 4718600 | tf_op jit(solution)/shard_map/ppermute | solution.py:458
  378.5 48.5 %collective-permute-start.51 = (bf16[2048,512]{1,0:T(8,128)(2,1)S(1)}, bf16[2048,512]{1,0:T(8,128)(2,1)S(1)}, u32[]{:S(2)}, u32[]{:S(2)}) collective-permute-start(bf16[2048,512]{1,0:T(8,128)(2,1)S(1)} %copy-done.38), channel_id=1, source_target_pairs={{0,1},{1,0},{2,3},{3,2},{4,5},{5,4},{6,7},{7,6},{8,9},{9,8},{10,11... | collective-permute-start | bytes 6291464 | tf_op jit(solution)/shard_map/ppermute | solution.py:455
  384.6 3.2 collective-permute-start.15
  384.8 8.5 %collective-permute-start.32 = (bf16[256,512]{1,0:T(8,128)(2,1)S(1)}, bf16[256,512]{1,0:T(8,128)(2,1)S(1)}, u32[]{:S(2)}, u32[]{:S(2)}) collective-permute-start(bf16[256,512]{1,0:T(8,128)(2,1)S(1)} %add_convert_fusion.16), channel_id=1, source_target_pairs={{0,4},{2,6},{4,0},{6,2},{8,12},{10,14},{12,8},{14,10},{16,20},{18,... | collective-permute-start | bytes 786440 | tf_op jit(solution)/shard_map/ppermute | solution.py:458
  387.8 72.5 %collective-permute-start.21 = (bf16[3,512,512]{2,1,0:T(8,128)(2,1)}, bf16[3,512,512]{2,1,0:T(8,128)(2,1)S(1)}, u32[]{:S(2)}, u32[]{:S(2)}) collective-permute-start(bf16[3,512,512]{2,1,0:T(8,128)(2,1)} %fusion.9), channel_id=1, source_target_pairs={{0,1},{1,0},{2,3},{3,2},{4,5},{5,4},{6,7},{7,6},{8,9},{9,8},{10,11... | collective-permute-start | bytes 4718600 | tf_op jit(solution)/shard_map/ppermute | solution.py:455
  393.3 70.5 %collective-permute-start.41 = (bf16[2,256,2048]{2,1,0:T(8,128)(2,1)S(1)}, bf16[2,256,2048]{2,1,0:T(8,128)(2,1)S(1)}, u32[]{:S(2)}, u32[]{:S(2)}) collective-permute-start(bf16[2,256,2048]{2,1,0:T(8,128)(2,1)S(1)} %add_convert_fusion.3), channel_id=1, source_target_pairs={{0,4},{2,6},{4,0},{6,2},{8,12},{10,14},{12,8},{14,10},{16,20},{18,... | collective-permute-start | bytes 6291464 | tf_op jit(solution)/shard_map/ppermute | solution.py:458
  398.4 61.9 %copy-start.52 = (bf16[3,512,512]{1,2,0:T(8,128)(2,1)}, bf16[3,512,512]{1,2,0:T(8,128)(2,1)S(1)}, u32[]{:S(2)}) copy-start(bf16[3,512,512]{1,2,0:T(8,128)(2,1)S(1)} %convolution_convert_fusion.11) | copy-start | bytes 4718596
  400.0 74.6 %collective-permute-start.16 = (f32[20,1024]{1,0:T(8,128)}, f32[20,1024]{1,0:T(8,128)}, u32[]{:S(2)}, u32[]{:S(2)}) collective-permute-start(f32[20,1024]{1,0:T(8,128)} %add.370), channel_id=1, source_target_pairs={{0,4},{2,6},{4,0},{6,2},{8,12},{10,14},{12,8},{14,10},{16,20},{18,... | collective-permute-start | bytes 245768 | tf_op jit(solution)/shard_map/ppermute | solution.py:458
  427.0 50.2 %collective-permute-start.33 = (bf16[128,512]{1,0:T(8,128)(2,1)}, bf16[128,512]{1,0:T(8,128)(2,1)}, u32[]{:S(2)}, u32[]{:S(2)}) collective-permute-start(bf16[128,512]{1,0:T(8,128)(2,1)} %constant_dynamic-slice_fusion.5), channel_id=1, source_target_pairs={{0,8},{2,10},{4,12},{6,14},{8,0},{10,2},{12,4},{14,6},{16,24},{18,... | collective-permute-start | bytes 393224 | tf_op jit(solution)/shard_map/ppermute | solution.py:458
  431.1 47.2 %collective-permute-start.52 = (bf16[1024,512]{1,0:T(8,128)(2,1)S(1)}, bf16[1024,512]{1,0:T(8,128)(2,1)}, u32[]{:S(2)}, u32[]{:S(2)}) collective-permute-start(bf16[1024,512]{1,0:T(8,128)(2,1)S(1)} %add_convert_fusion.8), channel_id=1, source_target_pairs={{0,4},{2,6},{4,0},{6,2},{8,12},{10,14},{12,8},{14,10},{16,20},{18,... | collective-permute-start | bytes 3145736 | tf_op jit(solution)/shard_map/ppermute | solution.py:458
  463.2 19.6 %collective-permute-start.22 = (bf16[3,256,512]{2,1,0:T(8,128)(2,1)}, bf16[3,256,512]{2,1,0:T(8,128)(2,1)}, u32[]{:S(2)}, u32[]{:S(2)}) collective-permute-start(bf16[3,256,512]{2,1,0:T(8,128)(2,1)} %fusion.28), channel_id=1, source_target_pairs={{0,4},{2,6},{4,0},{6,2},{8,12},{10,14},{12,8},{14,10},{16,20},{18,... | collective-permute-start | bytes 2359304 | tf_op jit(solution)/shard_map/ppermute | solution.py:458
  465.4 24.9 %collective-permute-start.42 = (bf16[256,2048]{1,0:T(8,128)(2,1)}, bf16[256,2048]{1,0:T(8,128)(2,1)}, u32[]{:S(2)}, u32[]{:S(2)}) collective-permute-start(bf16[256,2048]{1,0:T(8,128)(2,1)} %fusion.37), channel_id=1, source_target_pairs={{0,1},{1,0},{2,3},{3,2},{4,5},{5,4},{6,7},{7,6},{8,9},{9,8},{10,11... | collective-permute-start | bytes 3145736 | tf_op jit(solution)/shard_map/ppermute | solution.py:455
  475.6 95.6 %collective-permute-start.17 = (f32[20,1024]{1,0:T(8,128)S(1)}, f32[20,1024]{1,0:T(8,128)S(1)}, u32[]{:S(2)}, u32[]{:S(2)}) collective-permute-start(f32[20,1024]{1,0:T(8,128)S(1)} %add.371), channel_id=1, source_target_pairs={{0,8},{2,10},{4,12},{6,14},{8,0},{10,2},{12,4},{14,6},{16,24},{18,... | collective-permute-start | bytes 245768 | tf_op jit(solution)/shard_map/ppermute | solution.py:458
  480.3 14.9 %collective-permute-start.53 = (bf16[512,512]{1,0:T(8,128)(2,1)S(1)}, bf16[512,512]{1,0:T(8,128)(2,1)S(1)}, u32[]{:S(2)}, u32[]{:S(2)}) collective-permute-start(bf16[512,512]{1,0:T(8,128)(2,1)S(1)} %constant_dynamic-slice_fusion), channel_id=1, source_target_pairs={{0,8},{2,10},{4,12},{6,14},{8,0},{10,2},{12,4},{14,6},{16,24},{18,... | collective-permute-start | bytes 1572872 | tf_op jit(solution)/shard_map/ppermute | solution.py:458
  484.7 26.7 %collective-permute-start.23 = (bf16[3,128,512]{2,1,0:T(8,128)(2,1)S(1)}, bf16[3,128,512]{2,1,0:T(8,128)(2,1)S(1)}, u32[]{:S(2)}, u32[]{:S(2)}) collective-permute-start(bf16[3,128,512]{2,1,0:T(8,128)(2,1)S(1)} %constant_dynamic-slice_fusion.8), channel_id=1, source_target_pairs={{0,8},{2,10},{4,12},{6,14},{8,0},{10,2},{12,4},{14,6},{16,24},{18,... | collective-permute-start | bytes 1179656 | tf_op jit(solution)/shard_map/ppermute | solution.py:458
  492.3 28.8 %collective-permute-start.43 = (bf16[128,2048]{1,0:T(8,128)(2,1)S(1)}, bf16[128,2048]{1,0:T(8,128)(2,1)S(1)}, u32[]{:S(2)}, u32[]{:S(2)}) collective-permute-start(bf16[128,2048]{1,0:T(8,128)(2,1)S(1)} %constant_dynamic-slice_fusion.2), channel_id=1, source_target_pairs={{0,8},{2,10},{4,12},{6,14},{8,0},{10,2},{12,4},{14,6},{16,24},{18,... | collective-permute-start | bytes 1572872 | tf_op jit(solution)/shard_map/ppermute | solution.py:458
  495.4 26.1 %collective-permute-start.54 = (bf16[256,512]{1,0:T(8,128)(2,1)S(1)}, bf16[256,512]{1,0:T(8,128)(2,1)S(1)}, u32[]{:S(2)}, u32[]{:S(2)}) collective-permute-start(bf16[256,512]{1,0:T(8,128)(2,1)S(1)} %constant_dynamic-slice_fusion.3), channel_id=1, source_target_pairs={{0,16},{2,18},{4,20},{6,22},{8,24},{10,26},{12,28},{14,30},{16,0},... | collective-permute-start | bytes 786440 | tf_op jit(solution)/shard_map/ppermute | solution.py:458
  511.5 29.7 %collective-permute-start.24 = (bf16[3,64,512]{2,1,0:T(8,128)(2,1)S(1)}, bf16[3,64,512]{2,1,0:T(8,128)(2,1)S(1)}, u32[]{:S(2)}, u32[]{:S(2)}) collective-permute-start(bf16[3,64,512]{2,1,0:T(8,128)(2,1)S(1)} %constant_dynamic-slice_fusion.7), channel_id=1, source_target_pairs={{0,16},{2,18},{4,20},{6,22},{8,24},{10,26},{12,28},{14,30},{16,0},... | collective-permute-start | bytes 589832 | tf_op jit(solution)/shard_map/ppermute | solution.py:458
  521.3 31.2 %collective-permute-start.44 = (bf16[64,2048]{1,0:T(8,128)(2,1)S(1)}, bf16[64,2048]{1,0:T(8,128)(2,1)S(1)}, u32[]{:S(2)}, u32[]{:S(2)}) collective-permute-start(bf16[64,2048]{1,0:T(8,128)(2,1)S(1)} %constant_dynamic-slice_fusion.1), channel_id=1, source_target_pairs={{0,16},{2,18},{4,20},{6,22},{8,24},{10,26},{12,28},{14,30},{16,0},... | collective-permute-start | bytes 786440 | tf_op jit(solution)/shard_map/ppermute | solution.py:458
  521.6 40.1 %collective-permute-start.55 = (bf16[256,512]{1,0:T(8,128)(2,1)S(1)}, bf16[256,512]{1,0:T(8,128)(2,1)S(1)}, u32[]{:S(2)}, u32[]{:S(2)}) collective-permute-start(bf16[256,512]{1,0:T(8,128)(2,1)S(1)} %add_convert_fusion.13), channel_id=1, source_target_pairs={{0,16},{2,18},{4,20},{6,22},{8,24},{10,26},{12,28},{14,30},{16,0},... | collective-permute-start | bytes 786440 | tf_op jit(solution)/shard_map/ppermute | solution.py:458
  541.3 24.6 %collective-permute-start.25 = (bf16[3,64,512]{2,1,0:T(8,128)(2,1)S(1)}, bf16[3,64,512]{2,1,0:T(8,128)(2,1)S(1)}, u32[]{:S(2)}, u32[]{:S(2)}) collective-permute-start(bf16[3,64,512]{2,1,0:T(8,128)(2,1)S(1)} %add_convert_fusion.17), channel_id=1, source_target_pairs={{0,16},{2,18},{4,20},{6,22},{8,24},{10,26},{12,28},{14,30},{16,0},... | collective-permute-start | bytes 589832 | tf_op jit(solution)/shard_map/ppermute | solution.py:458
  552.6 18.2 %collective-permute-start.45 = (bf16[64,2048]{1,0:T(8,128)(2,1)S(1)}, bf16[64,2048]{1,0:T(8,128)(2,1)S(1)}, u32[]{:S(2)}, u32[]{:S(2)}) collective-permute-start(bf16[64,2048]{1,0:T(8,128)(2,1)S(1)} %add_convert_fusion.14), channel_id=1, source_target_pairs={{0,16},{2,18},{4,20},{6,22},{8,24},{10,26},{12,28},{14,30},{16,0},... | collective-permute-start | bytes 786440 | tf_op jit(solution)/shard_map/ppermute | solution.py:458
  552.7 19.8 %collective-permute-start.34 = (bf16[64,512]{1,0:T(8,128)(2,1)S(1)}, bf16[64,512]{1,0:T(8,128)(2,1)S(1)}, u32[]{:S(2)}, u32[]{:S(2)}) collective-permute-start(bf16[64,512]{1,0:T(8,128)(2,1)S(1)} %constant_dynamic-slice_fusion.4), channel_id=1, source_target_pairs={{0,16},{2,18},{4,20},{6,22},{8,24},{10,26},{12,28},{14,30},{16,0},... | collective-permute-start | bytes 196616 | tf_op jit(solution)/shard_map/ppermute | solution.py:458
  561.9 24.3 %collective-permute-start.56 = (bf16[512,512]{1,0:T(8,128)(2,1)S(1)}, bf16[512,512]{1,0:T(8,128)(2,1)S(1)}, u32[]{:S(2)}, u32[]{:S(2)}) collective-permute-start(bf16[512,512]{1,0:T(8,128)(2,1)S(1)} %maximum_select_fusion.22), channel_id=1, source_target_pairs={{0,8},{2,10},{4,12},{6,14},{8,0},{10,2},{12,4},{14,6},{16,24},{18,... | collective-permute-start | bytes 1572872 | tf_op jit(solution)/shard_map/ppermute | solution.py:458
  566.1 28.6 %collective-permute-start.26 = (bf16[3,128,512]{2,1,0:T(8,128)(2,1)S(1)}, bf16[3,128,512]{2,1,0:T(8,128)(2,1)S(1)}, u32[]{:S(2)}, u32[]{:S(2)}) collective-permute-start(bf16[3,128,512]{2,1,0:T(8,128)(2,1)S(1)} %maximum_select_fusion.23), channel_id=1, source_target_pairs={{0,8},{2,10},{4,12},{6,14},{8,0},{10,2},{12,4},{14,6},{16,24},{18,... | collective-permute-start | bytes 1179656 | tf_op jit(solution)/shard_map/ppermute | solution.py:458
  570.8 33.6 %collective-permute-start.46 = (bf16[128,2048]{1,0:T(8,128)(2,1)S(1)}, bf16[128,2048]{1,0:T(8,128)(2,1)S(1)}, u32[]{:S(2)}, u32[]{:S(2)}) collective-permute-start(bf16[128,2048]{1,0:T(8,128)(2,1)S(1)} %maximum_select_fusion.21), channel_id=1, source_target_pairs={{0,8},{2,10},{4,12},{6,14},{8,0},{10,2},{12,4},{14,6},{16,24},{18,... | collective-permute-start | bytes 1572872 | tf_op jit(solution)/shard_map/ppermute | solution.py:458
  571.2 35.4 %collective-permute-start.18 = (f32[20,1024]{1,0:T(8,128)S(1)}, f32[20,1024]{1,0:T(8,128)S(1)}, u32[]{:S(2)}, u32[]{:S(2)}) collective-permute-start(f32[20,1024]{1,0:T(8,128)S(1)} %add.372), channel_id=1, source_target_pairs={{0,16},{2,18},{4,20},{6,22},{8,24},{10,26},{12,28},{14,30},{16,0},... | collective-permute-start | bytes 245768 | tf_op jit(solution)/shard_map/ppermute | solution.py:458
  572.5 35.4 %collective-permute-start.35 = (bf16[64,512]{1,0:T(8,128)(2,1)S(1)}, bf16[64,512]{1,0:T(8,128)(2,1)S(1)}, u32[]{:S(2)}, u32[]{:S(2)}) collective-permute-start(bf16[64,512]{1,0:T(8,128)(2,1)S(1)} %add_convert_fusion.19), channel_id=1, source_target_pairs={{0,16},{2,18},{4,20},{6,22},{8,24},{10,26},{12,28},{14,30},{16,0},... | collective-permute-start | bytes 196616 | tf_op jit(solution)/shard_map/ppermute | solution.py:458
  586.7 27.8 %collective-permute-start.57 = (bf16[1024,512]{1,0:T(8,128)(2,1)S(1)}, bf16[1024,512]{1,0:T(8,128)(2,1)S(1)}, u32[]{:S(2)}, u32[]{:S(2)}) collective-permute-start(bf16[1024,512]{1,0:T(8,128)(2,1)S(1)} %maximum_select_fusion.16), channel_id=1, source_target_pairs={{0,4},{2,6},{4,0},{6,2},{8,12},{10,14},{12,8},{14,10},{16,20},{18,... | collective-permute-start | bytes 3145736 | tf_op jit(solution)/shard_map/ppermute | solution.py:458
  595.0 34.7 %collective-permute-start.27 = (bf16[3,256,512]{2,1,0:T(8,128)(2,1)S(1)}, bf16[3,256,512]{2,1,0:T(8,128)(2,1)S(1)}, u32[]{:S(2)}, u32[]{:S(2)}) collective-permute-start(bf16[3,256,512]{2,1,0:T(8,128)(2,1)S(1)} %maximum_select_fusion.17), channel_id=1, source_target_pairs={{0,4},{2,6},{4,0},{6,2},{8,12},{10,14},{12,8},{14,10},{16,20},{18,... | collective-permute-start | bytes 2359304 | tf_op jit(solution)/shard_map/ppermute | solution.py:458
  604.7 46.5 %collective-permute-start.47 = (bf16[256,2048]{1,0:T(8,128)(2,1)S(1)}, bf16[256,2048]{1,0:T(8,128)(2,1)S(1)}, u32[]{:S(2)}, u32[]{:S(2)}) collective-permute-start(bf16[256,2048]{1,0:T(8,128)(2,1)S(1)} %maximum_select_fusion.15), channel_id=1, source_target_pairs={{0,4},{2,6},{4,0},{6,2},{8,12},{10,14},{12,8},{14,10},{16,20},{18,... | collective-permute-start | bytes 3145736 | tf_op jit(solution)/shard_map/ppermute | solution.py:458
  606.7 48.8 %collective-permute-start.12 = (bf16[512,1024]{1,0:T(8,128)(2,1)S(1)}, bf16[512,1024]{1,0:T(8,128)(2,1)S(1)}, u32[]{:S(2)}, u32[]{:S(2)}) collective-permute-start(bf16[512,1024]{1,0:T(8,128)(2,1)S(1)} %get-tuple-element.61), channel_id=1, source_target_pairs={{0,1},{1,0},{2,3},{3,2},{4,5},{5,4},{6,7},{7,6},{8,9},{9,8},{10,11... | collective-permute-start | bytes 3145736 | tf_op jit(solution)/shard_map/ppermute | solution.py:455
  608.0 5.0 collective-permute-start.36
  613.0 44.6 %collective-permute-start.13 = (bf16[512,1024]{1,0:T(8,128)(2,1)S(1)}, bf16[512,1024]{1,0:T(8,128)(2,1)S(1)}, u32[]{:S(2)}, u32[]{:S(2)}) collective-permute-start(bf16[512,1024]{1,0:T(8,128)(2,1)S(1)} %slice.164), channel_id=1, source_target_pairs={{0,1},{1,0},{2,3},{3,2},{4,5},{5,4},{6,7},{7,6},{8,9},{9,8},{10,11... | collective-permute-start | bytes 3145736 | tf_op jit(solution)/shard_map/ppermute | solution.py:455
  614.5 39.4 %collective-permute-start.37 = (bf16[256,512]{1,0:T(8,128)(2,1)S(1)}, bf16[256,512]{1,0:T(8,128)(2,1)S(1)}, u32[]{:S(2)}, u32[]{:S(2)}) collective-permute-start(bf16[256,512]{1,0:T(8,128)(2,1)S(1)} %maximum_select_fusion.24), channel_id=1, source_target_pairs={{0,4},{2,6},{4,0},{6,2},{8,12},{10,14},{12,8},{14,10},{16,20},{18,... | collective-permute-start | bytes 786440 | tf_op jit(solution)/shard_map/ppermute | solution.py:458
  629.7 35.4 %collective-permute-start.58 = (bf16[2048,512]{1,0:T(8,128)(2,1)S(1)}, bf16[2048,512]{1,0:T(8,128)(2,1)S(1)}, u32[]{:S(2)}, u32[]{:S(2)}) collective-permute-start(bf16[2048,512]{1,0:T(8,128)(2,1)S(1)} %maximum_select_fusion.11), channel_id=1, source_target_pairs={{0,2},{2,0},{4,6},{6,4},{8,10},{10,8},{12,14},{14,12},{16,18},{18,... | collective-permute-start | bytes 6291464 | tf_op jit(solution)/shard_map/ppermute | solution.py:458
  651.2 10.8 %collective-permute-start.28 = (bf16[3,512,512]{2,1,0:T(8,128)(2,1)S(1)}, bf16[3,512,512]{2,1,0:T(8,128)(2,1)S(1)}, u32[]{:S(2)}, u32[]{:S(2)}) collective-permute-start(bf16[3,512,512]{2,1,0:T(8,128)(2,1)S(1)} %maximum_select_fusion.12), channel_id=1, source_target_pairs={{0,2},{2,0},{4,6},{6,4},{8,10},{10,8},{12,14},{14,12},{16,18},{18,... | collective-permute-start | bytes 4718600 | tf_op jit(solution)/shard_map/ppermute | solution.py:458
  654.0 15.2 %collective-permute-start.48 = (bf16[512,2048]{1,0:T(8,128)(2,1)S(1)}, bf16[512,2048]{1,0:T(8,128)(2,1)S(1)}, u32[]{:S(2)}, u32[]{:S(2)}) collective-permute-start(bf16[512,2048]{1,0:T(8,128)(2,1)S(1)} %maximum_select_fusion.10), channel_id=1, source_target_pairs={{0,2},{2,0},{4,6},{6,4},{8,10},{10,8},{12,14},{14,12},{16,18},{18,... | collective-permute-start | bytes 6291464 | tf_op jit(solution)/shard_map/ppermute | solution.py:458
  655.4 4.9 collective-permute-start.38
  (84 other events, 924.3 us)

commit v2 on v0

--- a/solution.py
+++ b/solution.py
@@ -1,6 +1,10 @@
+import functools
+
 import jax
 import jax.numpy as jnp
 from jax import lax
+from jax.experimental import pallas as pl
+from jax.experimental.pallas import tpu as pltpu
 from jax.sharding import PartitionSpec as P
 
 HD = 64
@@ -272,6 +276,810 @@
     )
 
 
+F32 = jnp.float32
+BF16 = jnp.bfloat16
+NN = (((1,), (0,)), ((), ()))
+NT = (((1,), (1,)), ((), ()))
+TN = (((0,), (0,)), ((), ()))
+MIB = 1 << 20
+
+
+def dot(left, right, dims):
+    return lax.dot_general(left, right, dims, preferred_element_type=F32)
+
+
+def whole(array):
+    return pl.BlockSpec(array.shape, lambda *_: (0,) * array.ndim)
+
+
+def kernel_call(body, name, grid, scalars, ins, outs, scratch=(), vmem=40):
+    spec = pltpu.PrefetchScalarGridSpec(
+        num_scalar_prefetch=len(scalars),
+        grid=grid,
+        in_specs=[spec for _, spec in ins],
+        out_specs=[spec for _, spec in outs],
+        scratch_shapes=list(scratch),
+    )
+    return pl.pallas_call(
+        body,
+        out_shape=[shape for shape, _ in outs],
+        grid_spec=spec,
+        compiler_params=pltpu.CompilerParams(vmem_limit_bytes=vmem * MIB),
+        cost_estimate=pl.CostEstimate(flops=MIB, transcendentals=0, bytes_accessed=MIB),
+        name=name,
+    )(*scalars, *[array for array, _ in ins])
+
+
+def struct(shape, dtype=BF16):
+    return jax.ShapeDtypeStruct(shape, dtype)
+
+
+def centred(values):
+    center = values - jnp.mean(values, axis=-1, keepdims=True)
+    inverse = lax.rsqrt(jnp.mean(center * center, axis=-1, keepdims=True) + EPS)
+    return center * inverse, inverse
+
+
+def norm_input_grad(grad_out, scaled, inverse, gain):
+    grad_scaled = grad_out * gain
+    grad_mean = jnp.mean(grad_scaled, axis=-1, keepdims=True)
+    cross_mean = jnp.mean(grad_scaled * scaled, axis=-1, keepdims=True)
+    return inverse * (grad_scaled - grad_mean - scaled * cross_mean)
+
+
+def column_sum(values):
+    return jnp.sum(values, axis=0, keepdims=True)
+
+
+def chunk_of(nat_ref, index, size):
+    return pl.ds(pl.multiple_of(nat_ref[index] * size, size), size)
+
+
+def attention_forward_kernel(qkv_ref, out_ref, power_ref, inverse_ref):
+    outs = []
+    for head in range(2):
+        lanes = slice(HD * head, HD * head + HD)
+        query = qkv_ref[0, :, lanes] * BF16(0.125)
+        scores = dot(qkv_ref[1, :, lanes], query, NT)
+        powers = jnp.exp(scores - jnp.max(scores, axis=0, keepdims=True))
+        inverse = 1.0 / jnp.sum(powers, axis=0, keepdims=True)
+        power_low = powers.astype(BF16)
+        power_ref[head] = power_low
+        inverse_ref[0, head : head + 1, :] = inverse
+        outs.append(dot(qkv_ref[2, :, lanes], power_low, TN) * inverse)
+    out_ref[...] = jnp.concatenate(outs, axis=0).T.astype(BF16)
+
+
+def attend(qkv):
+    _, rows, width = qkv.shape
+    pairs = width // (2 * HD)
+    return kernel_call(
+        attention_forward_kernel,
+        "attention_forward",
+        (pairs,),
+        [],
+        [(qkv, pl.BlockSpec((3, rows, 2 * HD), lambda j: (0, 0, j)))],
+        [
+            (struct((rows, width)), pl.BlockSpec((rows, 2 * HD), lambda j: (0, j))),
+            (struct((2 * pairs, rows, rows)), pl.BlockSpec((2, rows, rows), lambda j: (j, 0, 0))),
+            (struct((pairs, 2, rows), F32), pl.BlockSpec((1, 2, rows), lambda j: (j, 0, 0))),
+        ],
+    )
+
+
+def attention_backward_kernel(block, qkv_ref, power_ref, inverse_ref, out_ref, grad_ref, dqkv_ref, sums_ref):
+    rows_all = qkv_ref.shape[1]
+    out_t = out_ref[...].astype(F32).T
+    grad_t = grad_ref[...].astype(F32).T
+    for head in range(2):
+        lanes = slice(HD * head, HD * head + HD)
+        inverse = inverse_ref[0, head : head + 1, :]
+        grad_head = grad_t[lanes]
+        inner = jnp.sum(grad_head * out_t[lanes], axis=0, keepdims=True) * inverse
+        grad_scaled = grad_head * inverse
+        grad_low_t = grad_scaled.astype(BF16)
+        grad_low = grad_scaled.T.astype(BF16)
+        query = qkv_ref[0, :, lanes] * BF16(0.125)
+        key = qkv_ref[1, :, lanes]
+        value = qkv_ref[2, :, lanes]
+        key_t = key.T
+        key_grad = value_grad = None
+        query_grads = []
+        for start in range(0, rows_all, block):
+            rows = slice(start, start + block)
+            power = power_ref[head, :, rows]
+            grad_power = dot(value, grad_low_t[:, rows], NN) - inner[:, rows]
+            grad_scores = (power.astype(F32) * grad_power).astype(BF16)
+            key_part = dot(grad_scores, query[rows], NN)
+            value_part = dot(power, grad_low[rows], NN)
+            key_grad = key_part if key_grad is None else key_grad + key_part
+            value_grad = value_part if value_grad is None else value_grad + value_part
+            query_grads.append(dot(key_t, grad_scores, NN))
+        sums_ref[0, :, lanes] = jnp.concatenate(query_grads, axis=1).T * 0.125
+        sums_ref[1, :, lanes] = key_grad
+        sums_ref[2, :, lanes] = value_grad
+    dqkv_ref[...] = sums_ref[...].astype(BF16)
+
+
+def attend_back(first, count, qkv, powers, inverse, attended, grad_attended):
+    _, rows, width = qkv.shape
+    block = (3, rows, 2 * HD)
+    flat = pl.BlockSpec((rows, 2 * HD), lambda j: (0, j + first))
+    return kernel_call(
+        functools.partial(attention_backward_kernel, min(512, rows)),
+        "attention_backward",
+        (count,),
+        [],
+        [
+            (qkv, pl.BlockSpec(block, lambda j: (0, 0, j + first))),
+            (powers, pl.BlockSpec((2, rows, rows), lambda j: (j + first, 0, 0))),
+            (inverse, pl.BlockSpec((1, 2, rows), lambda j: (j + first, 0, 0))),
+            (attended, flat),
+            (grad_attended, flat),
+        ],
+        [(struct((3, rows, 2 * HD * count)), pl.BlockSpec(block, lambda j: (0, 0, j)))],
+        [pltpu.VMEM(block, F32)],
+    )[0]
+
+
+def project_own_kernel(at_ref, tokens_ref, recv_ref, lead_ref, gain_ref, shift_ref, weight_ref, bias_ref, rows_ref, normed_ref, heads_ref):
+    own = pl.program_id(0) < pl.num_programs(0) // 2
+    tokens = jnp.where(own, tokens_ref[0].astype(F32), recv_ref[...].astype(F32))
+    rows_ref[...] = tokens.astype(BF16)
+    scaled, _ = centred(tokens + lead_ref[...])
+    normed = (scaled * gain_ref[...] + shift_ref[...]).astype(BF16)
+    normed_ref[...] = normed
+    for c in range(3):
+        heads_ref[c] = (dot(normed, weight_ref[c], NN) + bias_ref[c : c + 1]).astype(BF16)
+
+
+def project_own(at, tokens, recv, lead, gain, shift, weight, bias, chunk):
+    half, width = tokens.shape[1:]
+    heads = weight.shape[2]
+    steps = half // chunk
+    row = pl.BlockSpec((chunk, width), lambda j, at: (j, 0))
+    return kernel_call(
+        project_own_kernel,
+        "project_own",
+        (2 * steps,),
+        [at],
+        [
+            (tokens, pl.BlockSpec((1, chunk, width), lambda j, at: (at[0], jnp.minimum(j, steps - 1), 0))),
+            (recv, pl.BlockSpec((chunk, width), lambda j, at: (jnp.maximum(j - steps, 0), 0))),
+            *[(v, whole(v)) for v in (lead, gain, shift, weight, bias)],
+        ],
+        [
+            (struct((2 * half, width)), row),
+            (struct((2 * half, width)), row),
+            (struct((3, 2 * half, heads)), pl.BlockSpec((3, chunk, heads), lambda j, at: (0, j, 0))),
+        ],
+    )
+
+
+def project_far_kernel(nat_ref, normed_ref, bias_ref, *refs):
+    *pieces, heads_ref = refs
+    size = pieces[0].shape[1]
+    total = bias_ref[0]
+    for k, piece in enumerate(pieces):
+        total = total + dot(normed_ref[:, chunk_of(nat_ref, k, size)], piece[0], NN)
+    heads_ref[0] = total.astype(BF16)
+
+
+def project_far(nat, normed, bias, pieces):
+    rows = normed.shape[0]
+    heads = pieces[0].shape[2]
+    first = lambda j, nat: (j, 0, 0)
+    return kernel_call(
+        project_far_kernel,
+        "project_far",
+        (3,),
+        [nat],
+        [
+            (normed, whole(normed)),
+            (bias[:, None], pl.BlockSpec((1, 1, heads), first)),
+            *[(p, pl.BlockSpec((1, *p.shape[1:]), first)) for p in pieces],
+        ],
+        [(struct((3, rows, heads)), pl.BlockSpec((1, rows, heads), first))],
+    )[0]
+
+
+def middle_kernel(nat_ref, own_ref, far_ref, weight_ref, rows_ref, lead_ref, bias_ref, gain_ref, shift_ref, *refs):
+    *pieces, middle_ref, normed_ref = refs
+    total = dot(own_ref[...], weight_ref[...], NN)
+    for k, piece in enumerate(pieces):
+        total = total + dot(far_ref[:, chunk_of(nat_ref, k, piece.shape[0])], piece[...], NN)
+    middle = rows_ref[...].astype(F32) + lead_ref[...] + total + bias_ref[...]
+    middle_ref[...] = middle
+    scaled, _ = centred(middle)
+    normed_ref[...] = (scaled * gain_ref[...] + shift_ref[...]).astype(BF16)
+
+
+def middle_layer(nat, own, far, weight, pieces, rows, lead, bias, gain, shift, chunk):
+    count, width = rows.shape
+    row = pl.BlockSpec((chunk, width), lambda j, nat: (j, 0))
+    heads = pl.BlockSpec((chunk, own.shape[1]), lambda j, nat: (j, 0))
+    return kernel_call(
+        middle_kernel,
+        "middle_layer",
+        (count // chunk,),
+        [nat],
+        [(own, heads), (far, heads), (weight, whole(weight)), (rows, row)]
+        + [(v, whole(v)) for v in (lead, bias, gain, shift, *pieces)],
+        [(struct((count, width), F32), row), (struct((count, width)), row)],
+    )
+
+
+def gelu_store(pre_act, rows, hidden_ref, slope_ref):
+    cdf = 0.5 * (1.0 + lax.erf(pre_act * 0.7071067811865476))
+    hidden_ref[rows] = (pre_act * cdf).astype(BF16)
+    density = jnp.exp(-0.5 * pre_act * pre_act) * 0.3989422804014327
+    slope_ref[rows] = (cdf + pre_act * density).astype(BF16)
+
+
+def hidden_kernel(block, nat_ref, normed_ref, bias_ref, *refs):
+    *pieces, hidden_ref, slope_ref = refs
+    size = pieces[0].shape[0]
+    for start in range(0, normed_ref.shape[0], block):
+        rows = slice(start, start + block)
+        pre_act = bias_ref[...]
+        for k, piece in enumerate(pieces):
+            lanes = slice(None) if len(pieces) == 1 else chunk_of(nat_ref, k, size)
+            pre_act = pre_act + dot(normed_ref[rows, lanes], piece[...], NN)
+        gelu_store(pre_act, rows, hidden_ref, slope_ref)
+
+
+def hidden_layer(nat, normed, bias, pieces, chunk):
+    rows = normed.shape[0]
+    units = pieces[0].shape[1]
+    tile = min(512, units)
+    column = lambda j, nat: (0, j)
+    return kernel_call(
+        functools.partial(hidden_kernel, chunk),
+        "hidden_layer",
+        (units // tile,),
+        [nat],
+        [(normed, whole(normed)), (bias, pl.BlockSpec((1, tile), column))]
+        + [(p, pl.BlockSpec((p.shape[0], tile), column)) for p in pieces],
+        [(struct((rows, units)), pl.BlockSpec((rows, tile), column))] * 2,
+    )
+
+
+def product_kernel(_, left_ref, right_ref, out_ref):
+    if len(right_ref.shape) == 3:
+        out_ref[0] = dot(left_ref[...], right_ref[0], TN).astype(BF16)
+    else:
+        out_ref[...] = dot(left_ref[...], right_ref[...], TN).astype(BF16)
+
+
+def grad_right_half(half, left, right):
+    rows, columns = left.shape
+    kept = right.shape[1] // 2
+    tile = min(1024, columns)
+    return kernel_call(
+        product_kernel,
+        "grad_right_half",
+        (columns // tile,),
+        [half],
+        [
+            (left, pl.BlockSpec((rows, tile), lambda j, half: (0, j))),
+            (right, pl.BlockSpec((rows, kept), lambda j, half: (0, half[0]))),
+        ],
+        [(struct((columns, kept)), pl.BlockSpec((tile, kept), lambda j, half: (j, 0)))],
+    )[0]
+
+
+def grad_left_half(half, left, right):
+    rows = left.shape[0]
+    kept = left.shape[1] // 2
+    columns = right.shape[-1]
+    tile = min(1024, columns)
+    left_spec = pl.BlockSpec((rows, kept), lambda j, half: (0, half[0]))
+    if right.ndim == 3:
+        grid, out_shape = (right.shape[0],), (right.shape[0], kept, columns)
+        right_spec = pl.BlockSpec((1, rows, columns), lambda j, half: (j, 0, 0))
+        out_spec = pl.BlockSpec((1, kept, columns), lambda j, half: (j, 0, 0))
+    else:
+        grid, out_shape = (columns // tile,), (kept, columns)
+        right_spec = pl.BlockSpec((rows, tile), lambda j, half: (0, j))
+        out_spec = pl.BlockSpec((kept, tile), lambda j, half: (0, j))
+    return kernel_call(
+        product_kernel,
+        "grad_left_half",
+        grid,
+        [half],
+        [(left, left_spec), (right, right_spec)],
+        [(struct(out_shape), out_spec)],
+    )[0]
+
+
+def pre_grad_store(grad, slope_ref, pre_ref, sum_ref):
+    pre = (grad * slope_ref[...].astype(F32)).astype(BF16)
+    pre_ref[...] = pre
+    sum_ref[...] = column_sum(pre.astype(F32))
+
+
+def pre_grad_own_kernel(low_ref, weight_ref, slope_ref, pre_ref, sum_ref):
+    pre_grad_store(dot(low_ref[...], weight_ref[...], NT), slope_ref, pre_ref, sum_ref)
+
+
+def pre_grad_own(low, weight, slope):
+    rows, width = low.shape
+    units = weight.shape[0]
+    tile = min(512, units)
+    column = lambda j: (0, j)
+    return kernel_call(
+        pre_grad_own_kernel,
+        "pre_grad_own",
+        (units // tile,),
+        [],
+        [
+            (low, whole(low)),
+            (weight, pl.BlockSpec((tile, width), lambda j: (j, 0))),
+            (slope, pl.BlockSpec((rows, tile), column)),
+        ],
+        [
+            (struct((rows, units)), pl.BlockSpec((rows, tile), column)),
+            (struct((1, units), F32), pl.BlockSpec((1, tile), column)),
+        ],
+    )
+
+
+def pre_grad_far_kernel(nat_ref, low_ref, slope_ref, *refs):
+    *pieces, pre_ref, sum_ref = refs
+    for k, piece in enumerate(pieces):
+
+        @pl.when(pl.program_id(0) == k)
+        def _(piece=piece):
+            pre_grad_store(dot(low_ref[...], piece[...], NT), slope_ref, pre_ref, sum_ref)
+
+
+def pre_grad_far(nat, low, pieces, slope):
+    rows = low.shape[0]
+    tile = pieces[0].shape[0]
+    units = tile * len(pieces)
+    column = lambda j, nat: (0, nat[j])
+    return kernel_call(
+        pre_grad_far_kernel,
+        "pre_grad_far",
+        (len(pieces),),
+        [nat],
+        [(low, whole(low)), (slope, pl.BlockSpec((rows, tile), column))] + [(p, whole(p)) for p in pieces],
+        [
+            (struct((rows, units)), pl.BlockSpec((rows, tile), column)),
+            (struct((1, units), F32), pl.BlockSpec((1, tile), column)),
+        ],
+    )
+
+
+def add_sums(sums_ref, rows):
+    @pl.when(pl.program_id(0) == 0)
+    def _():
+        sums_ref[...] = jnp.zeros_like(sums_ref)
+
+    for k, row in enumerate(rows):
+        sums_ref[k : k + 1, :] += row
+
+
+def middle_grad_kernel(nat_ref, own_ref, far_ref, weight_ref, middle_ref, cot_ref, loss_ref, gain_ref, *refs):
+    *pieces, grad_ref, low_ref, sums_ref, total_ref = refs
+    total_ref[...] = dot(own_ref[...], weight_ref[...], NT)
+    for k, piece in enumerate(pieces):
+        total_ref[:, chunk_of(nat_ref, k, piece.shape[0])] += dot(far_ref[...], piece[...], NT)
+    grad = total_ref[...]
+    scaled, inverse = centred(middle_ref[...])
+    top = cot_ref[...].astype(F32) * loss_ref[...]
+    grad_middle = top + norm_input_grad(grad, scaled, inverse, gain_ref[...])
+    grad_ref[...] = grad_middle
+    low_ref[...] = grad_middle.astype(BF16)
+    add_sums(
+        sums_ref,
+        [column_sum(grad * scaled), column_sum(grad), column_sum(grad_middle), column_sum(top)],
+    )
+
+
+def middle_grad(nat, own, far, weight, pieces, middle, cot, loss, gain, chunk):
+    count, width = middle.shape
+    row = pl.BlockSpec((chunk, width), lambda j, nat: (j, 0))
+    units = pl.BlockSpec((chunk, own.shape[1]), lambda j, nat: (j, 0))
+    return kernel_call(
+        middle_grad_kernel,
+        "middle_grad",
+        (count // chunk,),
+        [nat],
+        [(own, units), (far, units), (weight, whole(weight)), (middle, row), (cot, row)]
+        + [(v, whole(v)) for v in (loss, gain, *pieces)],
+        [
+            (struct((count, width), F32), row),
+            (struct((count, width)), row),
+            (struct((8, width), F32), pl.BlockSpec((8, width), lambda j, nat: (0, 0))),
+        ],
+        [pltpu.VMEM((chunk, width), F32)],
+    )
+
+
+def attended_grad_kernel(nat_ref, low_ref, weight_ref, *refs):
+    *pieces, own_ref, far_ref = refs
+    own_ref[...] = dot(low_ref[...], weight_ref[...], NT).astype(BF16)
+    for k, piece in enumerate(pieces):
+        far_ref[:, chunk_of(nat_ref, k, piece.shape[0])] = dot(low_ref[...], piece[...], NT).astype(BF16)
+
+
+def attended_grad(nat, low, weight, pieces, chunk):
+    count, width = low.shape
+    heads = weight.shape[0]
+    out = (struct((count, heads)), pl.BlockSpec((chunk, heads), lambda j, nat: (j, 0)))
+    return kernel_call(
+        attended_grad_kernel,
+        "attended_grad",
+        (count // chunk,),
+        [nat],
+        [(low, pl.BlockSpec((chunk, width), lambda j, nat: (j, 0)))] + [(v, whole(v)) for v in (weight, *pieces)],
+        [out, out],
+    )
+
+
+def output_kernel(nat_ref, own_ref, far_ref, weight_ref, middle_ref, bias_ref, *refs):
+    *pieces, out_ref = refs
+    total = dot(own_ref[...], weight_ref[...], NN)
+    for k, piece in enumerate(pieces):
+        total = total + dot(far_ref[:, chunk_of(nat_ref, k, piece.shape[0])], piece[...], NN)
+    out_ref[...] = (middle_ref[...] + total + bias_ref[...]).astype(BF16)
+
+
+def output_layer(nat, own, far, weight, pieces, middle, bias, chunk):
+    count, width = middle.shape
+    row = pl.BlockSpec((chunk, width), lambda j, nat: (j, 0))
+    units = pl.BlockSpec((chunk, own.shape[1]), lambda j, nat: (j, 0))
+    return kernel_call(
+        output_kernel,
+        "output_layer",
+        (count // chunk,),
+        [nat],
+        [(own, units), (far, units), (weight, whole(weight)), (middle, row)]
+        + [(v, whole(v)) for v in (bias, *pieces)],
+        [(struct((count, width)), row)],
+    )[0]
+
+
+def input_grad_kernel(own_count, nat_ref, far_ref, weight_ref, rows_ref, lead_ref, grad_ref, gain_ref, *refs):
+    owns, refs = refs[:own_count], refs[own_count:]
+    *pieces, out_ref, low_ref, sums_ref, total_ref = refs
+    total = None
+    at = 0
+    for own in owns:
+        size = own.shape[2]
+        for c in range(3):
+            part = dot(own[c], weight_ref[c, :, at : at + size], NT)
+            total = part if total is None else total + part
+        at += size
+    total_ref[...] = total
+    for k, piece in enumerate(pieces):
+        part = dot(far_ref[0], piece[0], NT) + dot(far_ref[1], piece[1], NT) + dot(far_ref[2], piece[2], NT)
+        total_ref[:, chunk_of(nat_ref, k, piece.shape[1])] += part
+    grad = total_ref[...]
+    scaled, inverse = centred(rows_ref[...].astype(F32) + lead_ref[...])
+    grad_shifted = grad_ref[...] + norm_input_grad(grad, scaled, inverse, gain_ref[...])
+    out_ref[...] = grad_shifted
+    low_ref[...] = grad_shifted.astype(BF16)
+    bias_rows = [
+        jnp.concatenate([column_sum(d[c].astype(F32)) for d in (*owns, far_ref)], axis=1) for c in (0, 2)
+    ]
+    add_sums(
+        sums_ref, [column_sum(grad * scaled), column_sum(grad), column_sum(grad_shifted), *bias_rows]
+    )
+
+
+def input_grads(nat, owns, far, weight, pieces, rows, lead, grad_middle, gain, chunk):
+    count, width = rows.shape
+    row = pl.BlockSpec((chunk, width), lambda j, nat: (j, 0))
+    heads = lambda d: pl.BlockSpec((3, chunk, d.shape[2]), lambda j, nat: (0, j, 0))
+    steps = count // chunk
+    half = pl.BlockSpec((chunk, width), lambda j, nat: (jnp.maximum(j - steps // 2, 0), 0))
+    return kernel_call(
+        functools.partial(input_grad_kernel, len(owns)),
+        "input_grads",
+        (steps,),
+        [nat],
+        [
+            (far, heads(far)),
+            (weight, whole(weight)),
+            (rows, row),
+            (lead, whole(lead)),
+            (grad_middle, row),
+            (gain, whole(gain)),
+        ]
+        + [(d, heads(d)) for d in owns]
+        + [(p, whole(p)) for p in pieces],
+        [
+            (struct((count, width), F32), row),
+            (struct((count // 2, width)), half),
+            (struct((8, width), F32), pl.BlockSpec((8, width), lambda j, nat: (0, 0))),
+        ],
+        [pltpu.VMEM((chunk, width), F32)],
+    )
+
+
+def hold(*values):
+    return lax.optimization_barrier(values)
+
+
+def fast_body(
+    tokens,
+    cotangent,
+    buckets,
+    counts,
+    lead_table,
+    norm1_gain,
+    norm1_shift,
+    w_qkv,
+    qv_bias,
+    w_out,
+    out_bias,
+    norm2_gain,
+    norm2_shift,
+    w_fc1,
+    fc1_bias,
+    w_fc2,
+    fc2_bias,
+):
+    replicas = lax.axis_size("dp")
+    levels = replicas.bit_length() - 1
+    dp_at, mp_at = lax.axis_index("dp"), lax.axis_index("mp")
+    bits = [(dp_at >> level) & 1 for level in range(levels)]
+
+    def over_x(value):
+        return lax.ppermute(value, "mp", [(0, 1), (1, 0)])
+
+    def over(level, value):
+        return lax.ppermute(value, "dp", [(i, i ^ (1 << level)) for i in range(replicas)])
+
+    def joined(bit, mine, theirs, axis=0):
+        return jnp.where(
+            bit == 0,
+            jnp.concatenate([mine, theirs], axis),
+            jnp.concatenate([theirs, mine], axis),
+        )
+
+    def part(value, index, count, axis=0):
+        size = value.shape[axis] // count
+        return lax.dynamic_slice_in_dim(value, index * size, size, axis)
+
+    half_rows, width = tokens.shape[1:]
+    heads_width = w_qkv.shape[2]
+    units = w_fc1.shape[1]
+    chunk = 256
+    core, side = bits[0], bits[1]
+    at = jnp.stack([mp_at, core, 1 - core]).astype(jnp.int32)
+    keep_half, send_half = at[1:2], at[2:3]
+    mine = core * 2 + side
+    shared_nat = jnp.stack([mine, mine ^ 1, mine ^ 2, mine ^ 3]).astype(jnp.int32)
+    direct_nat = jnp.stack([core * 2, core * 2 + 1, 2 - core * 2, 3 - core * 2]).astype(jnp.int32)
+    pair_nat = at[1:3]
+
+    def row_of(vector):
+        return vector.astype(F32)[None]
+
+    small = jnp.concatenate([qv_bias.reshape(-1), fc1_bias])
+    small_rows = -(-small.shape[0] // width)
+    small_rows_padded = -(-small_rows // 16) * 16
+    small = jnp.pad(small, (0, small_rows_padded * width - small.shape[0])).reshape(-1, width)
+    token_recv = over_x(jnp.concatenate([part(tokens, 1 - mp_at, 2)[0], small]))
+
+    bucket = lax.dynamic_index_in_dim(buckets, mp_at, 0, keepdims=False)
+    count_f = counts.astype(F32)
+    loss_weight = jnp.mean(count_f) / lax.dynamic_index_in_dim(count_f, bucket, 0, keepdims=False)
+    loss_row = jnp.broadcast_to(loss_weight, (1, width))
+    lead = lax.dynamic_index_in_dim(lead_table, bucket, 0).astype(F32)
+    own_qkv = jnp.transpose(w_qkv, (1, 0, 2))
+
+    token_recv, qkv_send = hold(token_recv, part(own_qkv, mine, 4, 1))
+    far_small = token_recv[half_rows:].reshape(-1)
+
+    def bias_three(bias):
+        bias_f = bias.astype(F32)
+        return jnp.stack([bias_f[0], jnp.zeros_like(bias_f[0]), bias_f[1]])
+
+    far_bias = bias_three(far_small[: 2 * heads_width].reshape(2, heads_width))
+    far_fc1_bias = row_of(far_small[2 * heads_width : 2 * heads_width + units])
+
+    qkv_x = over_x(qkv_send)
+    gain_one, gain_two = row_of(norm1_gain), row_of(norm2_gain)
+    rows, normed_one, own_heads = project_own(
+        at[:1], tokens, token_recv, lead, gain_one, row_of(norm1_shift), own_qkv, bias_three(qv_bias), chunk
+    )
+    own_heads, qkv_x, out_send, fc1_send = hold(own_heads, qkv_x, part(w_out, core, 2), part(w_fc1, mine, 4))
+
+    qkv_y = over(1, qkv_x)
+    out_x = over_x(out_send)
+    fc1_x = over_x(fc1_send)
+    own_attended, own_powers, own_inverse = attend(own_heads)
+    own_attended, qkv_x, qkv_y, out_x = hold(own_attended, qkv_x, qkv_y, out_x)
+
+    far_qkv = [qkv_x, qkv_y, over(0, qkv_x), over(0, qkv_y)]
+    far_out = [out_x, over(0, out_x)]
+    far_heads = project_far(shared_nat, normed_one, far_bias, far_qkv)
+    far_heads, fc1_x, cot_send = hold(far_heads, fc1_x, part(cotangent, 1 - mp_at, 2)[0])
+
+    fc1_y = over(1, fc1_x)
+    cot_recv = over_x(cot_send)
+    far_attended, far_powers, far_inverse = attend(far_heads)
+    middle, normed_two = middle_layer(
+        pair_nat, own_attended, far_attended, w_out, far_out, rows, lead,
+        row_of(out_bias), gain_two, row_of(norm2_shift), chunk,
+    )
+    normed_two, fc1_x, fc1_y, cot_recv, fc2_send = hold(
+        normed_two, fc1_x, fc1_y, cot_recv, part(w_fc2, core * 2, 4)
+    )
+
+    fc2_first = over_x(fc2_send)
+    far_fc1 = [fc1_x, fc1_y, over(0, fc1_x), over(0, fc1_y)]
+    cot_rows = jnp.concatenate([part(cotangent, mp_at, 2)[0], cot_recv])
+    grad_low = (cot_rows.astype(F32) * loss_weight).astype(BF16)
+    own_hidden, own_slope = hidden_layer(shared_nat, normed_two, row_of(fc1_bias), [w_fc1], chunk)
+    far_hidden, far_slope = hidden_layer(shared_nat, normed_two, far_fc1_bias, far_fc1, chunk)
+    far_hidden, own_hidden, fc2_first, grad_low, fc2_send = hold(
+        far_hidden, own_hidden, fc2_first, grad_low, part(w_fc2, core * 2 + 1, 4)
+    )
+
+    def total(values):
+        return sum(v.astype(F32) for v in values)
+
+    def low(values):
+        return total(values).astype(BF16)
+
+    def halves(values, level):
+        axis = values[0].ndim - 2
+        bit = bits[level]
+        return [part(v, bit, 2, axis) for v in values], [part(v, 1 - bit, 2, axis) for v in values]
+
+    def spread(values, level):
+        kept, sent = halves(values, level)
+        return kept, over(level, low(sent))
+
+    def collect(value, level):
+        return joined(bits[level], value, over(level, value), value.ndim - 2)
+
+    fc2_second = over_x(fc2_send)
+    far_recv = over(0, grad_right_half(send_half, far_hidden, grad_low))
+    own_recv = over(0, grad_right_half(send_half, own_hidden, grad_low))
+    far_keep = grad_right_half(keep_half, far_hidden, grad_low)
+    own_keep = grad_right_half(keep_half, own_hidden, grad_low)
+    own_keep, far_keep, far_recv, own_recv, fc2_second, grad_low = hold(
+        own_keep, far_keep, far_recv, own_recv, fc2_second, grad_low
+    )
+
+    fc2_recv = over_x(low([far_keep, far_recv]))
+    far_fc2 = [fc2_first, fc2_second, over(0, fc2_first), over(0, fc2_second)]
+    own_pre, own_fc1_bias = pre_grad_own(grad_low, w_fc2, own_slope)
+    far_pre, far_fc1_bias_sum = pre_grad_far(direct_nat, grad_low, far_fc2, far_slope)
+    fc1_far_recv = over(0, grad_left_half(send_half, normed_two, far_pre))
+    fc1_far_keep = grad_left_half(keep_half, normed_two, far_pre)
+    fc1_own_recv = over(0, grad_left_half(send_half, normed_two, own_pre))
+    fc1_own_keep = grad_left_half(keep_half, normed_two, own_pre)
+    own_pre, far_pre, fc1_far_keep, fc1_far_recv, fc1_own_keep, fc1_own_recv = hold(
+        own_pre, far_pre, fc1_far_keep, fc1_far_recv, fc1_own_keep, fc1_own_recv
+    )
+
+    fc1_recv = over_x(low([fc1_far_keep, fc1_far_recv]))
+    grad_middle, grad_branch, sums_two = middle_grad(
+        shared_nat, own_pre, far_pre, w_fc1, far_fc1, middle, cot_rows, loss_row, gain_two, chunk
+    )
+    own_grad_att, far_grad_att = attended_grad(pair_nat, grad_branch, w_out, far_out, chunk)
+    far_grad_att, own_grad_att, fc2_recv = hold(far_grad_att, own_grad_att, fc2_recv)
+
+    fc2_terms = [own_keep, own_recv, fc2_recv]
+    fc2_kept, fc2_recv = spread(fc2_terms, 1)
+    out_far_recv = over(0, grad_left_half(send_half, grad_branch, far_attended))
+    out_far_keep = grad_left_half(keep_half, grad_branch, far_attended)
+    out_own_recv = over(0, grad_left_half(send_half, grad_branch, own_attended))
+    out_own_keep = grad_left_half(keep_half, grad_branch, own_attended)
+    pairs = heads_width // (2 * HD)
+    far_dqkv = attend_back(0, pairs, far_heads, far_powers, far_inverse, far_attended, far_grad_att)
+    far_dqkv, fc2_recv, out_far_keep, out_far_recv, own_grad_att = hold(
+        far_dqkv, fc2_recv, out_far_keep, out_far_recv, own_grad_att
+    )
+
+    fc2_kept, fc2_recv = spread([*fc2_kept, fc2_recv], 2)
+    out_recv = over_x(low([out_far_keep, out_far_recv]))
+    qkv_far_recv = over(0, grad_left_half(send_half, normed_one, far_dqkv))
+    qkv_far_keep = grad_left_half(keep_half, normed_one, far_dqkv)
+    own_a = attend_back(0, pairs // 2, own_heads, own_powers, own_inverse, own_attended, own_grad_att)
+    own_a, fc2_recv, out_recv, fc1_recv, qkv_far_keep, qkv_far_recv, own_grad_att = hold(
+        own_a, fc2_recv, out_recv, fc1_recv, qkv_far_keep, qkv_far_recv, own_grad_att
+    )
+
+    fc1_terms = [
+        jnp.concatenate(pair, 1)
+        for pair in ((fc1_own_keep, out_own_keep), (fc1_own_recv, out_own_recv), (fc1_recv, out_recv))
+    ]
+    fc1_kept, fc1_recv = spread(fc1_terms, 1)
+    qkv_recv = over_x(low([qkv_far_keep, qkv_far_recv]))
+    for level in range(3, levels):
+        fc2_kept, fc2_recv = spread([*fc2_kept, fc2_recv], level)
+    own_b = attend_back(pairs // 2, pairs - pairs // 2, own_heads, own_powers, own_inverse, own_attended, own_grad_att)
+    own_b, fc2_recv = hold(own_b, fc2_recv)
+
+    fc2_mine = collect(low([*fc2_kept, fc2_recv]), levels - 1)
+
+    def own_grads(half):
+        return jnp.concatenate([grad_left_half(half, normed_one, own_a), grad_left_half(half, normed_one, own_b)], 2)
+
+    qkv_own_recv = over(0, own_grads(send_half))
+    qkv_own_keep = own_grads(keep_half)
+    grad_shifted, grad_send, sums_one = input_grads(
+        shared_nat, [own_a, own_b], far_dqkv, own_qkv, far_qkv, rows, lead, grad_middle, gain_one, chunk
+    )
+    grad_shifted, fc2_mine, fc1_recv, qkv_own_keep, qkv_own_recv, qkv_recv = hold(
+        grad_shifted, fc2_mine, fc1_recv, qkv_own_keep, qkv_own_recv, qkv_recv
+    )
+
+    output = output_layer(direct_nat, own_hidden, far_hidden, w_fc2, far_fc2, middle, row_of(fc2_bias), chunk)
+    qkv_kept, qkv_recv = spread([qkv_own_keep, qkv_own_recv, qkv_recv], 1)
+    fc1_kept, fc1_recv = spread([*fc1_kept, fc1_recv], 2)
+    for level in range(levels - 2, 1, -1):
+        fc2_mine = collect(fc2_mine, level)
+    bucket_rows = jnp.arange(counts.shape[0], dtype=jnp.int32)[:, None] == bucket
+    bias_sums = jnp.concatenate([own_fc1_bias, far_fc1_bias_sum], 0)
+    vectors = jnp.concatenate(
+        [
+            jnp.where(bucket_rows, sums_one[2:3], 0.0),
+            sums_one[:2],
+            sums_two[:4],
+            jnp.where(mp_at == 0, sums_one[3:5], jnp.roll(sums_one[3:5], heads_width, 1)),
+            jnp.where(mp_at == 0, bias_sums, bias_sums[::-1]).reshape(-1, width),
+        ]
+    )
+    vectors = vectors + over_x(vectors)
+    vectors = vectors + over(0, vectors)
+    qkv_recv, fc1_recv, fc2_mine, output, vectors = hold(qkv_recv, fc1_recv, fc2_mine, output, vectors)
+
+    output_recv = over_x(output[half_rows:])
+    grad_recv = over_x(grad_send)
+    fc2_mine = collect(fc2_mine, 1)
+    for level in range(1, levels):
+        vectors = vectors + over(level, vectors)
+    for level in range(2, levels):
+        qkv_kept, qkv_recv = spread([*qkv_kept, qkv_recv], level)
+    for level in range(3, levels):
+        fc1_kept, fc1_recv = spread([*fc1_kept, fc1_recv], level)
+    qkv_mine, fc1_mine = low([*qkv_kept, qkv_recv]), low([*fc1_kept, fc1_recv])
+    for level in range(levels - 1, 0, -1):
+        fc1_mine = collect(fc1_mine, level)
+        qkv_mine = collect(qkv_mine, level)
+    block_output = joined(mp_at, output[None, :half_rows], output_recv[None])
+    input_grad = joined(mp_at, grad_shifted[None, :half_rows], grad_recv[None].astype(F32))
+
+    table = counts.shape[0]
+    lead_grad, singles, rest = vectors[:table], vectors[table : table + 6], vectors[table + 6 :]
+    qv_bias_grad = part(rest[:2], mp_at, 2, 1)
+    fc1_bias_grad = part(rest[2:].reshape(-1), mp_at, 2)
+
+    def finish(half, axis):
+        return joined(core, half, over(0, half), axis).astype(F32)
+
+    fc2_grad = finish(fc2_mine, 1)
+    fc1_grad = finish(fc1_mine[:, :units], 0)
+    out_grad = finish(fc1_mine[:, units:], 0).T
+    qkv_grad = jnp.transpose(finish(qkv_mine, 1), (1, 0, 2))
+    return (
+        block_output,
+        input_grad,
+        lead_grad,
+        singles[0],
+        singles[1],
+        qkv_grad,
+        qv_bias_grad,
+        out_grad,
+        singles[4],
+        singles[2],
+        singles[3],
+        fc1_grad,
+        fc1_bias_grad,
+        fc2_grad,
+        singles[5],
+    )
+
+
 def solution(mesh):
     in_specs = (
         P("dp", "mp", None),
@@ -309,4 +1117,12 @@
         P("mp", None),
         P(),
     )
-    return jax.shard_map(body, mesh=mesh, in_specs=in_specs, out_specs=out_specs, check_vma=False)
+    def local(*args):
+        replicas = lax.axis_size("dp")
+        samples, half_rows, width = args[0].shape
+        heads_width, units = args[7].shape[2], args[13].shape[1]
+        fits = samples == 2 and lax.axis_size("mp") == 2 and replicas >= 16 and replicas & (replicas - 1) == 0
+        even = half_rows % 256 == 0 and width == 2 * heads_width == 1024 and units == 2 * width
+        return (fast_body if fits and even else body)(*args)
+
+    return jax.shard_map(local, mesh=mesh, in_specs=in_specs, out_specs=out_specs, check_vma=False)

time: 1250 us -> 584 us (0.47)
  matrix products: 375 us -> 0 us
  waiting for transfers between devices: 502 us -> 146 us
  Pallas kernels: 0 us -> 231 us
  other arithmetic: 188 us -> 81.8 us
  blocking collectives: 82.4 us -> 0 us
  starting transfers between devices: 0.36 us -> 39.7 us
    dot_general x28 -> x0, matrix products: 375 us -> none  [the longest x4 71.4 us: one_block(): jnp.einsum('qshd,kshd->shqk', query_block, key_all, preferred_element_typ...]
    all_gather x4 -> x0, waiting for transfers between devices: 240 us -> none  [the longest x1 99.5 us: body(): lax.all_gather(w_fc1, 'mp', axis=1, tiled=True)]
    pallas_call x0 -> x34, Pallas kernels: none -> 231 us  [kernel_call(): pl.pallas_call(body, out_shape=[shape for shape, _ in outs], grid_spec=sp...]
    psum x1 -> x0, waiting for transfers between devices: 169 us -> none  [body(): lax.psum(qkv_grad.astype(jnp.bfloat16), 'dp').astype(jnp.float32)]
    ppermute x0 -> x57, waiting for transfers between devices: none -> 146 us  [the longest x43 90 us: over(): lax.ppermute(value, 'dp', [(i, i ^ 1 << level) for i in range(replicas)])]
    reduce_scatter x4 -> x0, waiting for transfers between devices: 92 us -> none  [the longest x1 92 us: body(): lax.psum_scatter(jnp.einsum('tsf,fd->tsd', picked, w_out, preferred_eleme...]
    convert_element_type x23, other arithmetic: 132 us -> 51.2 us  [the longest x16 32.7 us: low(): return total(values).astype(BF16)]
    psum x2 -> x0, blocking collectives: 72.9 us -> none  [the longest x1 39.2 us: body(): lead_grad, small_grads = lax.psum((lead_grad, small_grads), ('dp', 'mp'))]
  transfers between devices with their start and end apart: 9 -> 57, of which waited for: 5 -> 15; matrix products, arithmetic and copies ran while one was open for 34% -> 16% of each run, Pallas kernels for 0% -> 39%
where the time goes in v2:
time: 584 us; the launch traced here: 574 us
  Pallas kernels  231 us (40%)
  waiting for transfers between devices  146 us (25%)
  other arithmetic  81.8 us (14%)
  local copies, waits for them, and re-layouts  69.9 us (12%)
  starting transfers between devices  39.7 us (7%)
    pallas_call x34, Pallas kernels, kernel_call(): pl.pallas_call(body, out_shape=[shape for shape, _ in outs], grid_spec=sp...  231 us
    ppermute x43, waiting for transfers between devices, over(): lax.ppermute(value, 'dp', [(i, i ^ 1 << level) for i in range(replicas)])  90 us
    ppermute x14, waiting for transfers between devices, over_x(): return lax.ppermute(value, 'mp', [(0, 1), (1, 0)])  55.7 us
    unnamed x183, local copies, waits for them, and re-layouts  49.4 us
    convert_element_type x16, other arithmetic, low(): return total(values).astype(BF16)  32.7 us
    ppermute x43, starting transfers between devices, over(): lax.ppermute(value, 'dp', [(i, i ^ 1 << level) for i in range(replicas)])  23.1 us
    ppermute x14, starting transfers between devices, over_x(): return lax.ppermute(value, 'mp', [(0, 1), (1, 0)])  16.6 us
    select_n x11, other arithmetic, joined(): jnp.where(bit == 0, jnp.concatenate([mine, theirs], axis), jnp.concatenat...  16.4 us
  transfers between devices with their start and end apart: 57, of which 15 were waited for; matrix products, arithmetic and copies ran while one was open for 16% of the time, Pallas kernels for 39%

profile of v2, /device:TPU:0, one launch (start us, length us, event | category | flops | bytes accessed | tf_op | source)
XLA Modules:
  0.0 574.3 jit_solution(7579028266151432940)
XLA Ops:
  4.5 2.9 collective-permute-start
  12.3 2.3 constant_dynamic-slice_fusion.3
  14.6 16.9 %collective-permute-done.recv_ref = bf16[528,1024]{1,0:T(8,128)(2,1)S(1)} collective-permute-done((bf16[528,1024]{1,0:T(8,128)(2,1)}, bf16[528,1024]{1,0:T(8,128)(2,1)S(1)}, u32[]{:S(2)}, u32[]{:S(2)}) %collective-permute-start) | collective-permute-done | bytes 1081376 | tf_op jit(solution)/shard_map/ppermute | solution.py:831
  38.3 5.5 project_own.1
  43.9 6.7 %collective-permute-done.1.refs_0_.refs_2_ = bf16[3,256,512]{2,1,0:T(8,128)(2,1)} collective-permute-done((bf16[3,256,512]{2,1,0:T(8,128)(2,1)}, bf16[3,256,512]{2,1,0:T(8,128)(2,1)}, u32[]{:S(2)}, u32[]{:S(2)}) %collective-permute-start.1) | collective-permute-done | bytes 786464 | tf_op jit(solution)/shard_map/ppermute | solution.py:831
  54.1 17.4 %attention_forward.2 = (bf16[1024,512]{1,0:T(8,128)(2,1)S(1)}, bf16[8,1024,1024]{2,1,0:T(8,128)(2,1)}, f32[4,2,1024]{2,1,0:T(2,128)S(1)}) custom-call(bf16[3,1024,512]{2,1,0:T(8,128)(2,1)S(1)} %get-tuple-element.109.qkv_ref), custom_call_target="tpu_custom_call" | custom-call | flops 1048576 | bytes 1048576 | tf_op jit(solution)/shard_map/attention_forward/pallas_call | solution.py:303
  73.8 3.0 dynamic-slice_bitcast_fusion
  76.9 5.5 project_far.1.qkv_ref
  84.1 2.1 collective-permute-done.6.refs_0_
  88.4 3.2 constant_dynamic-slice_fusion.1
  91.6 17.4 %attention_forward.3 = (bf16[1024,512]{1,0:T(8,128)(2,1)S(1)}, bf16[8,1024,1024]{2,1,0:T(8,128)(2,1)}, f32[4,2,1024]{2,1,0:T(2,128)S(1)}) custom-call(bf16[3,1024,512]{2,1,0:T(8,128)(2,1)S(1)} %copy-done.24), custom_call_target="tpu_custom_call" | custom-call | flops 1048576 | bytes 1048576 | tf_op jit(solution)/shard_map/attention_forward/pallas_call | solution.py:303
  109.0 5.8 %middle_layer.1 = (f32[1024,1024]{1,0:T(8,128)S(1)}, bf16[1024,1024]{1,0:T(8,128)(2,1)S(1)}) custom-call(s32[2]{0:T(128)S(1)} %pad_add_fusion.1.nat_ref, bf16[1024,512]{1,0:T(8,128)(2,1)S(1)} %get-tuple-element.120.own_ref.out_ref.right_ref, bf16[1024,512]{1,0:T(8,128)(2,1)S(1)} %get-tuple-element.119.far_ref.out_ref.right_ref, ...), custom_call_target="tpu_custom_call" | custom-call | flops 1048576 | bytes 1048576 | tf_op jit(solution)/shard_map/middle_layer/pallas_call | solution.py:303
  124.6 10.6 %hidden_layer.3 = (bf16[1024,2048]{1,0:T(8,128)(2,1)S(1)}, bf16[1024,2048]{1,0:T(8,128)(2,1)S(1)}) custom-call(s32[4]{0:T(128)S(1)} %pad_add_fusion.nat_ref, bf16[1024,1024]{1,0:T(8,128)(2,1)S(1)} %copy-done.4, f32[1,2048]{1,0:T(1,128)S(1)} %bitcast.66, bf16[1024,2048]{1,0:T(8,128)(2,1)} %weight_ref.7), custom_call_target="tpu_custom_call" | custom-call | flops 1048576 | bytes 1048576 | tf_op jit(solution)/shard_map/hidden_layer/pallas_call | solution.py:303
  137.1 2.5 multiply_convert_fusion.right_ref.low_ref
  139.7 11.2 %hidden_layer.2 = (bf16[1024,2048]{1,0:T(8,128)(2,1)S(1)}, bf16[1024,2048]{1,0:T(8,128)(2,1)}) custom-call(s32[4]{0:T(128)S(1)} %pad_add_fusion.nat_ref, bf16[1024,1024]{1,0:T(8,128)(2,1)S(1)} %copy-done.4, f32[1,2048]{1,0:T(1,128)S(1)} %bitcast.67, bf16[256,2048]{1,0:T(8,128)(2,1)} %collective-permute-done.6.refs_0_, ...), custom_call_target="tpu_custom_call" | custom-call | flops 1048576 | bytes 1048576 | tf_op jit(solution)/shard_map/hidden_layer/pallas_call | solution.py:303
  150.9 3.0 grad_right_half.7
  153.9 3.0 grad_right_half.6
  158.6 3.0 grad_right_half.4
  161.6 3.0 grad_right_half.5
  166.0 17.1 %collective-permute-done.15.refs_1_ = bf16[512,1024]{1,0:T(8,128)(2,1)} collective-permute-done((bf16[512,1024]{1,0:T(8,128)(2,1)}, bf16[512,1024]{1,0:T(8,128)(2,1)}, u32[]{:S(2)}, u32[]{:S(2)}) %collective-permute-start.15) | collective-permute-done | bytes 1048608 | tf_op jit(solution)/shard_map/ppermute | solution.py:831
  187.4 2.2 copy-done.28
  189.6 7.2 %pre_grad_own.1 = (bf16[1024,2048]{1,0:T(8,128)(2,1)S(1)}, f32[1,2048]{1,0:T(1,128)S(1)}) custom-call(bf16[1024,1024]{1,0:T(8,128)(2,1)S(1)} %copy-done.1, bf16[2048,1024]{1,0:T(8,128)(2,1)S(1)} %copy-done.28, bf16[1024,2048]{1,0:T(8,128)(2,1)} %copy-done.56), custom_call_target="tpu_custom_call" | custom-call | flops 1048576 | bytes 1048576 | tf_op jit(solution)/shard_map/pre_grad_own/pallas_call | solution.py:303
  196.8 4.0 grad_left_half.17
  201.3 9.3 %pre_grad_far.1 = (bf16[1024,2048]{1,0:T(8,128)(2,1)S(1)}, f32[1,2048]{1,0:T(1,128)S(1)}) custom-call(s32[4]{0:T(128)S(1)} %pad_add_fusion.2.nat_ref, bf16[1024,1024]{1,0:T(8,128)(2,1)S(1)} %copy-done.2, bf16[1024,2048]{1,0:T(8,128)(2,1)} %get-tuple-element.140.slope_ref, bf16[512,1024]{1,0:T(8,128)(2,1)} %collective-permute-done.12.refs_0_, ...), custom_call_target="tpu_custom_call" | custom-call | flops 1048576 | bytes 1048576 | tf_op jit(solution)/shard_map/pre_grad_far/pallas_call | solution.py:303
  210.7 4.0 grad_left_half.15
  220.4 2.2 copy-done.20
  222.6 3.1 grad_left_half.16
  225.7 3.1 grad_left_half.14
  228.8 18.6 %middle_grad.1 = (f32[1024,1024]{1,0:T(8,128)S(1)}, bf16[1024,1024]{1,0:T(8,128)(2,1)S(1)}, f32[8,1024]{1,0:T(8,128)S(1)}) custom-call(s32[4]{0:T(128)S(1)} %pad_add_fusion.nat_ref, bf16[1024,2048]{1,0:T(8,128)(2,1)} %copy-done.19, bf16[1024,2048]{1,0:T(8,128)(2,1)} %copy-done.21, bf16[1024,2048]{1,0:T(8,128)(2,1)} %weight_ref.7, f32[1024,1024]{1,0:T(8,128)} %copy-done.36, ...), custom_call_target="tpu_custom_call" | custom-call | flops 1048576 | bytes 1048576 | tf_op jit(solution)/shard_map/middle_grad/pallas_call | solution.py:303
  251.4 4.8 attended_grad.1
  256.2 8.8 %collective-permute-done.20 = bf16[2048,512]{1,0:T(8,128)(2,1)} collective-permute-done((bf16[2048,512]{1,0:T(8,128)(2,1)}, bf16[2048,512]{1,0:T(8,128)(2,1)}, u32[]{:S(2)}, u32[]{:S(2)}) %collective-permute-start.20) | collective-permute-done | bytes 2097184 | tf_op jit(solution)/shard_map/ppermute | solution.py:831
  268.0 3.8 add_convert_fusion
  274.8 22.1 %attention_backward.3.right_ref.far_ref = bf16[3,1024,512]{2,1,0:T(8,128)(2,1)S(1)} custom-call(bf16[3,1024,512]{2,1,0:T(8,128)(2,1)S(1)} %copy-done.25, bf16[8,1024,1024]{2,1,0:T(8,128)(2,1)} %get-tuple-element.117.power_ref, f32[4,2,1024]{2,1,0:T(2,128)S(1)} %get-tuple-element.118.inverse_ref, bf16[1024,512]{1,0:T(8,128)(2,1)S(1)} %copy-done.35, ...), custom_call_target="tpu_custom_call" | custom-call | flops 1048576 | bytes 1048576 | tf_op jit(solution)/shard_map/attention_backward/pallas_call | solution.py:303
  296.9 3.7 grad_left_half.21
  304.3 2.6 add_convert_fusion.8
  316.1 2.3 grad_left_half.20
  319.2 12.1 %attention_backward.4.refs_0_.right_ref = bf16[3,1024,256]{2,1,0:T(8,128)(2,1)S(1)} custom-call(bf16[3,1024,512]{2,1,0:T(8,128)(2,1)S(1)} %copy-done.27, bf16[8,1024,1024]{2,1,0:T(8,128)(2,1)} %get-tuple-element.159.power_ref, f32[4,2,1024]{2,1,0:T(2,128)S(1)} %get-tuple-element.160.inverse_ref, ...), custom_call_target="tpu_custom_call" | custom-call | flops 1048576 | bytes 1048576 | tf_op jit(solution)/shard_map/attention_backward/pallas_call | solution.py:303
  331.4 2.1 add_convert_fusion.13
  333.5 2.6 collective-permute-start.27
  336.2 3.0 add_convert_fusion.2
  342.5 12.0 %attention_backward.5.refs_1_.right_ref = bf16[3,1024,256]{2,1,0:T(8,128)(2,1)S(1)} custom-call(bf16[3,1024,512]{2,1,0:T(8,128)(2,1)S(1)} %copy-done.27, bf16[8,1024,1024]{2,1,0:T(8,128)(2,1)} %get-tuple-element.159.power_ref, f32[4,2,1024]{2,1,0:T(2,128)S(1)} %get-tuple-element.160.inverse_ref, ...), custom_call_target="tpu_custom_call" | custom-call | flops 1048576 | bytes 1048576 | tf_op jit(solution)/shard_map/attention_backward/pallas_call | solution.py:303
  371.3 2.1 copy-done.15
  373.4 15.2 %input_grads.1 = (f32[1024,1024]{1,0:T(8,128)}, bf16[512,1024]{1,0:T(8,128)(2,1)S(1)}, f32[8,1024]{1,0:T(8,128)S(1)}) custom-call(s32[4]{0:T(128)S(1)} %pad_add_fusion.nat_ref, bf16[3,1024,512]{2,1,0:T(8,128)(2,1)S(1)} %copy-done.15, bf16[3,1024,512]{2,1,0:T(8,128)(2,1)} %bitcast.60, bf16[1024,1024]{1,0:T(8,128)(2,1)S(1)} %copy-done.42, ...), custom_call_target="tpu_custom_call" | custom-call | flops 1048576 | bytes 1048576 | tf_op jit(solution)/shard_map/input_grads/pallas_call | solution.py:303
  389.9 3.2 collective-permute-done.30
  393.6 2.6 add_convert_fusion.5
  396.6 3.0 add_convert_fusion.6
  401.8 4.1 collective-permute-done.36
  406.1 2.2 copy-done.17
  408.2 14.2 %output_layer.1 = bf16[1024,1024]{1,0:T(8,128)(2,1)S(1)} custom-call(s32[4]{0:T(128)S(1)} %pad_add_fusion.2.nat_ref, bf16[1024,2048]{1,0:T(8,128)(2,1)S(1)} %copy-done.17, bf16[1024,2048]{1,0:T(8,128)(2,1)} %copy-done.18, bf16[2048,1024]{1,0:T(8,128)(2,1)} %weight_ref.9, f32[1024,1024]{1,0:T(8,128)} %copy-done.36, f32[1,1024]{1,0:T(1,128)S(1)} %bitcast.71, ...), custom_call_target="tpu_custom_call" | custom-call | flops 1048576 | bytes 1048576 | tf_op jit(solution)/shard_map/output_layer/pallas_call | solution.py:303
  422.5 3.3 maximum_select_fusion.9
  428.3 17.2 %collective-permute-done.49 = bf16[64,2560]{1,0:T(8,128)(2,1)S(1)} collective-permute-done((bf16[64,2560]{1,0:T(8,128)(2,1)S(1)}, bf16[64,2560]{1,0:T(8,128)(2,1)S(1)}, u32[]{:S(2)}, u32[]{:S(2)}) %collective-permute-start.49) | collective-permute-done | bytes 327712 | tf_op jit(solution)/shard_map/ppermute | solution.py:834
  447.3 15.2 %collective-permute-done.50 = bf16[64,2560]{1,0:T(8,128)(2,1)S(1)} collective-permute-done((bf16[64,2560]{1,0:T(8,128)(2,1)S(1)}, bf16[64,2560]{1,0:T(8,128)(2,1)S(1)}, u32[]{:S(2)}, u32[]{:S(2)}) %collective-permute-start.50) | collective-permute-done | bytes 327712 | tf_op jit(solution)/shard_map/ppermute | solution.py:834
  468.2 19.7 %collective-permute-done.43 = bf16[3,128,512]{2,1,0:T(8,128)(2,1)S(1)} collective-permute-done((bf16[3,128,512]{2,1,0:T(8,128)(2,1)S(1)}, bf16[3,128,512]{2,1,0:T(8,128)(2,1)S(1)}, u32[]{:S(2)}, u32[]{:S(2)}) %collective-permute-start.43) | collective-permute-done | bytes 393248 | tf_op jit(solution)/shard_map/ppermute | solution.py:834
  491.1 9.4 %collective-permute-done.44 = bf16[3,64,512]{2,1,0:T(8,128)(2,1)S(1)} collective-permute-done((bf16[3,64,512]{2,1,0:T(8,128)(2,1)S(1)}, bf16[3,64,512]{2,1,0:T(8,128)(2,1)S(1)}, u32[]{:S(2)}, u32[]{:S(2)}) %collective-permute-start.44) | collective-permute-done | bytes 196640 | tf_op jit(solution)/shard_map/ppermute | solution.py:834
  502.0 9.3 %collective-permute-done.45 = bf16[3,64,512]{2,1,0:T(8,128)(2,1)S(1)} collective-permute-done((bf16[3,64,512]{2,1,0:T(8,128)(2,1)S(1)}, bf16[3,64,512]{2,1,0:T(8,128)(2,1)S(1)}, u32[]{:S(2)}, u32[]{:S(2)}) %collective-permute-start.45) | collective-permute-done | bytes 196640 | tf_op jit(solution)/shard_map/ppermute | solution.py:834
  513.5 4.2 maximum_select_fusion.6
  517.7 4.8 collective-permute-done.46
  524.5 2.1 maximum_select_fusion.4
  530.6 10.9 %collective-permute-done.47 = bf16[3,256,512]{2,1,0:T(8,128)(2,1)S(1)} collective-permute-done((bf16[3,256,512]{2,1,0:T(8,128)(2,1)S(1)}, bf16[3,256,512]{2,1,0:T(8,128)(2,1)S(1)}, u32[]{:S(2)}, u32[]{:S(2)}) %collective-permute-start.47) | collective-permute-done | bytes 786464 | tf_op jit(solution)/shard_map/ppermute | solution.py:834
  543.3 2.5 maximum_select_fusion
  552.1 2.9 copy.32
  555.0 7.7 %fusion.1 = f32[2048,1024]{1,0:T(8,128)} fusion(bf16[2048,512]{1,0:T(8,128)(2,1)} %collective-permute-done.56, bf16[2048,512]{1,0:T(8,128)(2,1)} %maximum_select_fusion.6, pred[]{:T(512)S(6)} %eq.43), kind=kLoop, calls=%fused_computation.9 | loop fusion | flops 20971520 | bytes 12582913 | tf_op jit(solution)/shard_map/convert_element_type | solution.py:1058
  562.7 5.1 convert_bitcast_fusion
  567.8 6.0 %fusion = f32[1024,2048]{1,0:T(8,128)} fusion(bf16[512,2048]{1,0:T(8,128)(2,1)} %collective-permute-done.54, bf16[512,2048]{1,0:T(8,128)(2,1)S(1)} %slice.138, pred[]{:T(512)S(6)} %eq.43), kind=kLoop, calls=%fused_computation.7 | loop fusion | flops 20971520 | bytes 12582913 | tf_op jit(solution)/shard_map/convert_element_type | solution.py:1058
  (361 shorter events, 125.9 us)
Async XLA Ops:
  4.5 27.0 %collective-permute-start = (bf16[528,1024]{1,0:T(8,128)(2,1)}, bf16[528,1024]{1,0:T(8,128)(2,1)S(1)}, u32[]{:S(2)}, u32[]{:S(2)}) collective-permute-start(bf16[528,1024]{1,0:T(8,128)(2,1)} %pad_maximum_fusion.3), channel_id=1, source_target_pairs={{0,1},{1,0},{2,3},{3,2},{4,5},{5,4},{6,7},{7,6},{8,9},{9,8},{10,11... | collective-permute-start | bytes 3244040 | tf_op jit(solution)/shard_map/ppermute | solution.py:831
  10.3 24.5 %copy-start.78 = (bf16[2,512]{1,0:T(2,128)(2,1)S(1)}, bf16[2,512]{1,0:T(2,128)(2,1)}, u32[]{:S(2)}) copy-start(bf16[2,512]{1,0:T(2,128)(2,1)} %param.25) | copy-start | bytes 6148
  31.6 19.0 %collective-permute-start.1 = (bf16[3,256,512]{2,1,0:T(8,128)(2,1)}, bf16[3,256,512]{2,1,0:T(8,128)(2,1)}, u32[]{:S(2)}, u32[]{:S(2)}) collective-permute-start(bf16[3,256,512]{2,1,0:T(8,128)(2,1)} %dynamic-slice_bitcast_fusion.3), channel_id=1, source_target_pairs={{0,1},{1,0},{2,3},{3,2},{4,5},{5,4},{6,7},{7,6},{8,9},{9,8},{10,11... | collective-permute-start | bytes 2359304 | tf_op jit(solution)/shard_map/ppermute | solution.py:831
  43.9 27.6 %copy-start.40 = (bf16[1024,1024]{1,0:T(8,128)(2,1)}, bf16[1024,1024]{1,0:T(8,128)(2,1)S(1)}, u32[]{:S(2)}) copy-start(bf16[1024,1024]{1,0:T(8,128)(2,1)S(1)} %get-tuple-element.121.rows_ref) | copy-start | bytes 6291460
  50.6 22.6 %collective-permute-start.2 = (bf16[3,256,512]{2,1,0:T(8,128)(2,1)}, bf16[3,256,512]{2,1,0:T(8,128)(2,1)}, u32[]{:S(2)}, u32[]{:S(2)}) collective-permute-start(bf16[3,256,512]{2,1,0:T(8,128)(2,1)} %collective-permute-done.1.refs_0_.refs_2_), channel_id=1, source_target_pairs={{0,4},{2,6},{4,0},{6,2},{8,12},{10,14},{12,8},{14,10},{16,20},{18,... | collective-permute-start | bytes 2359304 | tf_op jit(solution)/shard_map/ppermute | solution.py:834
  52.1 21.1 %collective-permute-start.3 = (bf16[256,1024]{1,0:T(8,128)(2,1)S(1)}, bf16[256,1024]{1,0:T(8,128)(2,1)}, u32[]{:S(2)}, u32[]{:S(2)}) collective-permute-start(bf16[256,1024]{1,0:T(8,128)(2,1)S(1)} %copy-done.76), channel_id=1, source_target_pairs={{0,1},{1,0},{2,3},{3,2},{4,5},{5,4},{6,7},{7,6},{8,9},{9,8},{10,11... | collective-permute-start | bytes 1572872 | tf_op jit(solution)/shard_map/ppermute | solution.py:831
  53.5 32.7 %collective-permute-start.6 = (bf16[256,2048]{1,0:T(8,128)(2,1)}, bf16[256,2048]{1,0:T(8,128)(2,1)}, u32[]{:S(2)}, u32[]{:S(2)}) collective-permute-start(bf16[256,2048]{1,0:T(8,128)(2,1)} %constant_dynamic-slice_fusion.3), channel_id=1, source_target_pairs={{0,1},{1,0},{2,3},{3,2},{4,5},{5,4},{6,7},{7,6},{8,9},{9,8},{10,11... | collective-permute-start | bytes 3145736 | tf_op jit(solution)/shard_map/ppermute | solution.py:831
  73.2 3.6 collective-permute-start.4
  73.2 3.7 collective-permute-start.5
  86.2 32.0 %collective-permute-start.9 = (bf16[512,1024]{1,0:T(8,128)(2,1)}, bf16[512,1024]{1,0:T(8,128)(2,1)}, u32[]{:S(2)}, u32[]{:S(2)}) collective-permute-start(bf16[512,1024]{1,0:T(8,128)(2,1)} %get-tuple-element.125), channel_id=1, source_target_pairs={{0,1},{1,0},{2,3},{3,2},{4,5},{5,4},{6,7},{7,6},{8,9},{9,8},{10,11... | collective-permute-start | bytes 3145736 | tf_op jit(solution)/shard_map/ppermute | solution.py:831
  87.7 30.5 %collective-permute-start.8 = (bf16[256,2048]{1,0:T(8,128)(2,1)}, bf16[256,2048]{1,0:T(8,128)(2,1)}, u32[]{:S(2)}, u32[]{:S(2)}) collective-permute-start(bf16[256,2048]{1,0:T(8,128)(2,1)} %collective-permute-done.6.refs_0_), channel_id=1, source_target_pairs={{0,4},{2,6},{4,0},{6,2},{8,12},{10,14},{12,8},{14,10},{16,20},{18,... | collective-permute-start | bytes 3145736 | tf_op jit(solution)/shard_map/ppermute | solution.py:834
  88.2 20.8 %collective-permute-start.7 = (bf16[256,1024]{1,0:T(8,128)(2,1)}, bf16[256,1024]{1,0:T(8,128)(2,1)}, u32[]{:S(2)}, u32[]{:S(2)}) collective-permute-start(bf16[256,1024]{1,0:T(8,128)(2,1)} %collective-permute-done.3.refs_0_), channel_id=1, source_target_pairs={{0,2},{2,0},{4,6},{6,4},{8,10},{10,8},{12,14},{14,12},{16,18},{18,... | collective-permute-start | bytes 1572872 | tf_op jit(solution)/shard_map/ppermute | solution.py:834
  118.2 21.4 %collective-permute-start.10 = (bf16[256,2048]{1,0:T(8,128)(2,1)}, bf16[256,2048]{1,0:T(8,128)(2,1)}, u32[]{:S(2)}, u32[]{:S(2)}) collective-permute-start(bf16[256,2048]{1,0:T(8,128)(2,1)} %collective-permute-done.6.refs_0_), channel_id=1, source_target_pairs={{0,2},{2,0},{4,6},{6,4},{8,10},{10,8},{12,14},{14,12},{16,18},{18,... | collective-permute-start | bytes 3145736 | tf_op jit(solution)/shard_map/ppermute | solution.py:834
  118.7 21.0 %collective-permute-start.11 = (bf16[256,2048]{1,0:T(8,128)(2,1)}, bf16[256,2048]{1,0:T(8,128)(2,1)}, u32[]{:S(2)}, u32[]{:S(2)}) collective-permute-start(bf16[256,2048]{1,0:T(8,128)(2,1)} %collective-permute-done.8.refs_1_), channel_id=1, source_target_pairs={{0,2},{2,0},{4,6},{6,4},{8,10},{10,8},{12,14},{14,12},{16,18},{18,... | collective-permute-start | bytes 3145736 | tf_op jit(solution)/shard_map/ppermute | solution.py:834
  118.8 32.1 %collective-permute-start.12 = (bf16[512,1024]{1,0:T(8,128)(2,1)}, bf16[512,1024]{1,0:T(8,128)(2,1)}, u32[]{:S(2)}, u32[]{:S(2)}) collective-permute-start(bf16[512,1024]{1,0:T(8,128)(2,1)} %get-tuple-element.131), channel_id=1, source_target_pairs={{0,1},{1,0},{2,3},{3,2},{4,5},{5,4},{6,7},{7,6},{8,9},{9,8},{10,11... | collective-permute-start | bytes 3145736 | tf_op jit(solution)/shard_map/ppermute | solution.py:831
  156.9 26.1 %collective-permute-start.13 = (bf16[2048,512]{1,0:T(8,128)(2,1)S(1)}, bf16[2048,512]{1,0:T(8,128)(2,1)S(1)}, u32[]{:S(2)}, u32[]{:S(2)}) collective-permute-start(bf16[2048,512]{1,0:T(8,128)(2,1)S(1)} %grad_right_half.6), channel_id=1, source_target_pairs={{0,2},{2,0},{4,6},{6,4},{8,10},{10,8},{12,14},{14,12},{16,18},{18,... | collective-permute-start | bytes 6291464 | tf_op jit(solution)/shard_map/ppermute | solution.py:834
  157.1 25.9 %collective-permute-start.14 = (bf16[2048,512]{1,0:T(8,128)(2,1)S(1)}, bf16[2048,512]{1,0:T(8,128)(2,1)S(1)}, u32[]{:S(2)}, u32[]{:S(2)}) collective-permute-start(bf16[2048,512]{1,0:T(8,128)(2,1)S(1)} %grad_right_half.7), channel_id=1, source_target_pairs={{0,2},{2,0},{4,6},{6,4},{8,10},{10,8},{12,14},{14,12},{16,18},{18,... | collective-permute-start | bytes 6291464 | tf_op jit(solution)/shard_map/ppermute | solution.py:834
  157.5 25.5 %collective-permute-start.15 = (bf16[512,1024]{1,0:T(8,128)(2,1)}, bf16[512,1024]{1,0:T(8,128)(2,1)}, u32[]{:S(2)}, u32[]{:S(2)}) collective-permute-start(bf16[512,1024]{1,0:T(8,128)(2,1)} %get-tuple-element.136), channel_id=1, source_target_pairs={{0,1},{1,0},{2,3},{3,2},{4,5},{5,4},{6,7},{7,6},{8,9},{9,8},{10,11... | collective-permute-start | bytes 3145736 | tf_op jit(solution)/shard_map/ppermute | solution.py:831
  158.6 42.7 %collective-permute-start.16 = (bf16[512,1024]{1,0:T(8,128)(2,1)}, bf16[512,1024]{1,0:T(8,128)(2,1)}, u32[]{:S(2)}, u32[]{:S(2)}) collective-permute-start(bf16[512,1024]{1,0:T(8,128)(2,1)} %collective-permute-done.12.refs_0_), channel_id=1, source_target_pairs={{0,2},{2,0},{4,6},{6,4},{8,10},{10,8},{12,14},{14,12},{16,18},{18,... | collective-permute-start | bytes 3145736 | tf_op jit(solution)/shard_map/ppermute | solution.py:834
  185.7 15.6 %collective-permute-start.17 = (bf16[512,1024]{1,0:T(8,128)(2,1)}, bf16[512,1024]{1,0:T(8,128)(2,1)}, u32[]{:S(2)}, u32[]{:S(2)}) collective-permute-start(bf16[512,1024]{1,0:T(8,128)(2,1)} %collective-permute-done.15.refs_1_), channel_id=1, source_target_pairs={{0,2},{2,0},{4,6},{6,4},{8,10},{10,8},{12,14},{14,12},{16,18},{18,... | collective-permute-start | bytes 3145736 | tf_op jit(solution)/shard_map/ppermute | solution.py:834
  200.8 28.0 %collective-permute-start.19 = (bf16[512,2048]{1,0:T(8,128)(2,1)}, bf16[512,2048]{1,0:T(8,128)(2,1)}, u32[]{:S(2)}, u32[]{:S(2)}) collective-permute-start(bf16[512,2048]{1,0:T(8,128)(2,1)} %grad_left_half.17), channel_id=1, source_target_pairs={{0,2},{2,0},{4,6},{6,4},{8,10},{10,8},{12,14},{14,12},{16,18},{18,... | collective-permute-start | bytes 6291464 | tf_op jit(solution)/shard_map/ppermute | solution.py:834
  214.6 14.1 %collective-permute-start.18 = (bf16[512,2048]{1,0:T(8,128)(2,1)}, bf16[512,2048]{1,0:T(8,128)(2,1)}, u32[]{:S(2)}, u32[]{:S(2)}) collective-permute-start(bf16[512,2048]{1,0:T(8,128)(2,1)} %grad_left_half.15), channel_id=1, source_target_pairs={{0,2},{2,0},{4,6},{6,4},{8,10},{10,8},{12,14},{14,12},{16,18},{18,... | collective-permute-start | bytes 6291464 | tf_op jit(solution)/shard_map/ppermute | solution.py:834
  217.0 48.0 %collective-permute-start.20 = (bf16[2048,512]{1,0:T(8,128)(2,1)}, bf16[2048,512]{1,0:T(8,128)(2,1)}, u32[]{:S(2)}, u32[]{:S(2)}) collective-permute-start(bf16[2048,512]{1,0:T(8,128)(2,1)} %add_convert_fusion.1), channel_id=1, source_target_pairs={{0,1},{1,0},{2,3},{3,2},{4,5},{5,4},{6,7},{7,6},{8,9},{9,8},{10,11... | collective-permute-start | bytes 6291464 | tf_op jit(solution)/shard_map/ppermute | solution.py:831
  249.4 23.8 %copy-start.7 = (bf16[1024,1024]{1,0:T(8,128)(2,1)}, bf16[1024,1024]{1,0:T(8,128)(2,1)S(1)}, u32[]{:S(2)}) copy-start(bf16[1024,1024]{1,0:T(8,128)(2,1)S(1)} %get-tuple-element.147.low_ref.left_ref) | copy-start | bytes 6291460
  250.2 46.7 %collective-permute-start.22 = (bf16[512,512]{1,0:T(8,128)(2,1)S(1)}, bf16[512,512]{1,0:T(8,128)(2,1)S(1)}, u32[]{:S(2)}, u32[]{:S(2)}) collective-permute-start(bf16[512,512]{1,0:T(8,128)(2,1)S(1)} %grad_left_half.19), channel_id=1, source_target_pairs={{0,2},{2,0},{4,6},{6,4},{8,10},{10,8},{12,14},{14,12},{16,18},{18,... | collective-permute-start | bytes 1572872 | tf_op jit(solution)/shard_map/ppermute | solution.py:834
  266.7 30.2 %collective-permute-start.21 = (bf16[1024,512]{1,0:T(8,128)(2,1)S(1)}, bf16[1024,512]{1,0:T(8,128)(2,1)S(1)}, u32[]{:S(2)}, u32[]{:S(2)}) collective-permute-start(bf16[1024,512]{1,0:T(8,128)(2,1)S(1)} %add_convert_fusion.4), channel_id=1, source_target_pairs={{0,4},{2,6},{4,0},{6,2},{8,12},{10,14},{12,8},{14,10},{16,20},{18,... | collective-permute-start | bytes 3145736 | tf_op jit(solution)/shard_map/ppermute | solution.py:834
  271.8 59.6 %collective-permute-start.25 = (bf16[512,2048]{1,0:T(8,128)(2,1)}, bf16[512,2048]{1,0:T(8,128)(2,1)}, u32[]{:S(2)}, u32[]{:S(2)}) collective-permute-start(bf16[512,2048]{1,0:T(8,128)(2,1)} %add_convert_fusion), channel_id=1, source_target_pairs={{0,1},{1,0},{2,3},{3,2},{4,5},{5,4},{6,7},{7,6},{8,9},{9,8},{10,11... | collective-permute-start | bytes 6291464 | tf_op jit(solution)/shard_map/ppermute | solution.py:831
  300.6 30.8 %collective-permute-start.26 = (bf16[3,512,512]{2,1,0:T(8,128)(2,1)}, bf16[3,512,512]{2,1,0:T(8,128)(2,1)}, u32[]{:S(2)}, u32[]{:S(2)}) collective-permute-start(bf16[3,512,512]{2,1,0:T(8,128)(2,1)} %grad_left_half.21), channel_id=1, source_target_pairs={{0,2},{2,0},{4,6},{6,4},{8,10},{10,8},{12,14},{14,12},{16,18},{18,... | collective-permute-start | bytes 4718600 | tf_op jit(solution)/shard_map/ppermute | solution.py:834
  303.9 11.2 %collective-permute-start.29 = (bf16[512,512]{1,0:T(8,128)(2,1)}, bf16[512,512]{1,0:T(8,128)(2,1)}, u32[]{:S(2)}, u32[]{:S(2)}) collective-permute-start(bf16[512,512]{1,0:T(8,128)(2,1)} %grad_left_half.23), channel_id=1, source_target_pairs={{0,2},{2,0},{4,6},{6,4},{8,10},{10,8},{12,14},{14,12},{16,18},{18,... | collective-permute-start | bytes 1572872 | tf_op jit(solution)/shard_map/ppermute | solution.py:834
  307.0 24.4 %collective-permute-start.23 = (bf16[512,512]{1,0:T(8,128)(2,1)}, bf16[512,512]{1,0:T(8,128)(2,1)}, u32[]{:S(2)}, u32[]{:S(2)}) collective-permute-start(bf16[512,512]{1,0:T(8,128)(2,1)} %add_convert_fusion.8), channel_id=1, source_target_pairs={{0,8},{2,10},{4,12},{6,14},{8,0},{10,2},{12,4},{14,6},{16,24},{18,... | collective-permute-start | bytes 1572872 | tf_op jit(solution)/shard_map/ppermute | solution.py:834
  309.5 21.9 %collective-permute-start.24 = (bf16[512,512]{1,0:T(8,128)(2,1)}, bf16[512,512]{1,0:T(8,128)(2,1)}, u32[]{:S(2)}, u32[]{:S(2)}) collective-permute-start(bf16[512,512]{1,0:T(8,128)(2,1)} %add_convert_fusion.7), channel_id=1, source_target_pairs={{0,1},{1,0},{2,3},{3,2},{4,5},{5,4},{6,7},{7,6},{8,9},{9,8},{10,11... | collective-permute-start | bytes 1572872 | tf_op jit(solution)/shard_map/ppermute | solution.py:831
  313.0 47.1 %copy-start.38 = (bf16[512,512]{1,0:T(8,128)(2,1)}, bf16[512,512]{1,0:T(8,128)(2,1)S(1)}, u32[]{:S(2)}) copy-start(bf16[512,512]{1,0:T(8,128)(2,1)S(1)} %grad_left_half.22) | copy-start | bytes 1572868
  316.1 44.0 %copy-start.64 = (bf16[512,2560]{1,0:T(8,128)(2,1)}, bf16[512,2560]{1,0:T(8,128)(2,1)S(1)}, u32[]{:S(2)}) copy-start(bf16[512,2560]{1,0:T(8,128)(2,1)S(1)} %constant_dynamic-update-slice_fusion) | copy-start | bytes 7864324
  331.4 23.1 %copy-start.29 = (bf16[3,1024,256]{2,1,0:T(8,128)(2,1)}, bf16[3,1024,256]{2,1,0:T(8,128)(2,1)S(1)}, u32[]{:S(2)}) copy-start(bf16[3,1024,256]{2,1,0:T(8,128)(2,1)S(1)} %attention_backward.4.refs_0_.right_ref) | copy-start | bytes 4718596
  333.5 23.6 %collective-permute-start.27 = (bf16[256,512]{1,0:T(8,128)(2,1)S(1)}, bf16[256,512]{1,0:T(8,128)(2,1)S(1)}, u32[]{:S(2)}, u32[]{:S(2)}) collective-permute-start(bf16[256,512]{1,0:T(8,128)(2,1)S(1)} %add_convert_fusion.13), channel_id=1, source_target_pairs={{0,16},{2,18},{4,20},{6,22},{8,24},{10,26},{12,28},{14,30},{16,0},... | collective-permute-start | bytes 786440 | tf_op jit(solution)/shard_map/ppermute | solution.py:834
  339.2 54.0 %collective-permute-start.32 = (bf16[3,512,512]{2,1,0:T(8,128)(2,1)}, bf16[3,512,512]{2,1,0:T(8,128)(2,1)}, u32[]{:S(2)}, u32[]{:S(2)}) collective-permute-start(bf16[3,512,512]{2,1,0:T(8,128)(2,1)} %add_convert_fusion.2), channel_id=1, source_target_pairs={{0,1},{1,0},{2,3},{3,2},{4,5},{5,4},{6,7},{7,6},{8,9},{9,8},{10,11... | collective-permute-start | bytes 4718600 | tf_op jit(solution)/shard_map/ppermute | solution.py:831
  360.1 33.1 %collective-permute-start.31 = (bf16[3,512,512]{2,1,0:T(8,128)(2,1)}, bf16[3,512,512]{2,1,0:T(8,128)(2,1)}, u32[]{:S(2)}, u32[]{:S(2)}) collective-permute-start(bf16[3,512,512]{2,1,0:T(8,128)(2,1)} %pad_maximum_fusion.2), channel_id=1, source_target_pairs={{0,2},{2,0},{4,6},{6,4},{8,10},{10,8},{12,14},{14,12},{16,18},{18,... | collective-permute-start | bytes 4718600 | tf_op jit(solution)/shard_map/ppermute | solution.py:834
  362.5 30.6 %collective-permute-start.30 = (bf16[256,2560]{1,0:T(8,128)(2,1)}, bf16[256,2560]{1,0:T(8,128)(2,1)}, u32[]{:S(2)}, u32[]{:S(2)}) collective-permute-start(bf16[256,2560]{1,0:T(8,128)(2,1)} %add_convert_fusion.3), channel_id=1, source_target_pairs={{0,4},{2,6},{4,0},{6,2},{8,12},{10,14},{12,8},{14,10},{16,20},{18,... | collective-permute-start | bytes 3932168 | tf_op jit(solution)/shard_map/ppermute | solution.py:834
  368.9 20.9 %collective-permute-start.28 = (bf16[256,512]{1,0:T(8,128)(2,1)S(1)}, bf16[256,512]{1,0:T(8,128)(2,1)S(1)}, u32[]{:S(2)}, u32[]{:S(2)}) collective-permute-start(bf16[256,512]{1,0:T(8,128)(2,1)S(1)} %add_convert_fusion.12), channel_id=1, source_target_pairs={{0,16},{2,18},{4,20},{6,22},{8,24},{10,26},{12,28},{14,30},{16,0},... | collective-permute-start | bytes 786440 | tf_op jit(solution)/shard_map/ppermute | solution.py:834
  393.2 29.4 %collective-permute-start.35 = (bf16[512,512]{1,0:T(8,128)(2,1)S(1)}, bf16[512,512]{1,0:T(8,128)(2,1)}, u32[]{:S(2)}, u32[]{:S(2)}) collective-permute-start(bf16[512,512]{1,0:T(8,128)(2,1)S(1)} %maximum_select_fusion.13), channel_id=1, source_target_pairs={{0,8},{2,10},{4,12},{6,14},{8,0},{10,2},{12,4},{14,6},{16,24},{18,... | collective-permute-start | bytes 1572872 | tf_op jit(solution)/shard_map/ppermute | solution.py:834
  396.2 29.6 %collective-permute-start.33 = (bf16[3,256,512]{2,1,0:T(8,128)(2,1)}, bf16[3,256,512]{2,1,0:T(8,128)(2,1)}, u32[]{:S(2)}, u32[]{:S(2)}) collective-permute-start(bf16[3,256,512]{2,1,0:T(8,128)(2,1)} %add_convert_fusion.5), channel_id=1, source_target_pairs={{0,4},{2,6},{4,0},{6,2},{8,12},{10,14},{12,8},{14,10},{16,20},{18,... | collective-permute-start | bytes 2359304 | tf_op jit(solution)/shard_map/ppermute | solution.py:834
  399.6 26.3 %collective-permute-start.34 = (bf16[128,2560]{1,0:T(8,128)(2,1)}, bf16[128,2560]{1,0:T(8,128)(2,1)}, u32[]{:S(2)}, u32[]{:S(2)}) collective-permute-start(bf16[128,2560]{1,0:T(8,128)(2,1)} %add_convert_fusion.6), channel_id=1, source_target_pairs={{0,8},{2,10},{4,12},{6,14},{8,0},{10,2},{12,4},{14,6},{16,24},{18,... | collective-permute-start | bytes 1966088 | tf_op jit(solution)/shard_map/ppermute | solution.py:834
  401.2 4.7 collective-permute-start.36
  405.9 16.6 %collective-permute-start.37 = (f32[20,1024]{1,0:T(8,128)S(1)}, f32[20,1024]{1,0:T(8,128)S(1)}, u32[]{:S(2)}, u32[]{:S(2)}) collective-permute-start(f32[20,1024]{1,0:T(8,128)S(1)} %add.434), channel_id=1, source_target_pairs={{0,2},{2,0},{4,6},{6,4},{8,10},{10,8},{12,14},{14,12},{16,18},{18,... | collective-permute-start | bytes 245768 | tf_op jit(solution)/shard_map/ppermute | solution.py:834
  427.5 17.9 %collective-permute-start.49 = (bf16[64,2560]{1,0:T(8,128)(2,1)S(1)}, bf16[64,2560]{1,0:T(8,128)(2,1)S(1)}, u32[]{:S(2)}, u32[]{:S(2)}) collective-permute-start(bf16[64,2560]{1,0:T(8,128)(2,1)S(1)} %add_convert_fusion.11), channel_id=1, source_target_pairs={{0,16},{2,18},{4,20},{6,22},{8,24},{10,26},{12,28},{14,30},{16,0},... | collective-permute-start | bytes 983048 | tf_op jit(solution)/shard_map/ppermute | solution.py:834
  428.2 34.5 %copy-start.66 = (bf16[3,512,512]{2,1,0:T(8,128)(2,1)S(1)}, bf16[3,512,512]{2,1,0:T(8,128)(2,1)}, u32[]{:S(2)}) copy-start(bf16[3,512,512]{2,1,0:T(8,128)(2,1)} %copy-done.65) | copy-start | bytes 4718596
  447.2 15.3 %collective-permute-start.50 = (bf16[64,2560]{1,0:T(8,128)(2,1)S(1)}, bf16[64,2560]{1,0:T(8,128)(2,1)S(1)}, u32[]{:S(2)}, u32[]{:S(2)}) collective-permute-start(bf16[64,2560]{1,0:T(8,128)(2,1)S(1)} %add_convert_fusion.10), channel_id=1, source_target_pairs={{0,16},{2,18},{4,20},{6,22},{8,24},{10,26},{12,28},{14,30},{16,0},... | collective-permute-start | bytes 983048 | tf_op jit(solution)/shard_map/ppermute | solution.py:834
  462.7 27.1 %collective-permute-start.51 = (bf16[128,2560]{1,0:T(8,128)(2,1)S(1)}, bf16[128,2560]{1,0:T(8,128)(2,1)S(1)}, u32[]{:S(2)}, u32[]{:S(2)}) collective-permute-start(bf16[128,2560]{1,0:T(8,128)(2,1)S(1)} %maximum_select_fusion.12), channel_id=1, source_target_pairs={{0,8},{2,10},{4,12},{6,14},{8,0},{10,2},{12,4},{14,6},{16,24},{18,... | collective-permute-start | bytes 1966088 | tf_op jit(solution)/shard_map/ppermute | solution.py:834
  464.4 23.4 %collective-permute-start.43 = (bf16[3,128,512]{2,1,0:T(8,128)(2,1)S(1)}, bf16[3,128,512]{2,1,0:T(8,128)(2,1)S(1)}, u32[]{:S(2)}, u32[]{:S(2)}) collective-permute-start(bf16[3,128,512]{2,1,0:T(8,128)(2,1)S(1)} %add_convert_fusion.9), channel_id=1, source_target_pairs={{0,8},{2,10},{4,12},{6,14},{8,0},{10,2},{12,4},{14,6},{16,24},{18,... | collective-permute-start | bytes 1179656 | tf_op jit(solution)/shard_map/ppermute | solution.py:834
  466.4 45.1 %collective-permute-start.39 = (bf16[512,1024]{1,0:T(8,128)(2,1)S(1)}, bf16[512,1024]{1,0:T(8,128)(2,1)}, u32[]{:S(2)}, u32[]{:S(2)}) collective-permute-start(bf16[512,1024]{1,0:T(8,128)(2,1)S(1)} %copy-done.61), channel_id=1, source_target_pairs={{0,1},{1,0},{2,3},{3,2},{4,5},{5,4},{6,7},{7,6},{8,9},{9,8},{10,11... | collective-permute-start | bytes 3145736 | tf_op jit(solution)/shard_map/ppermute | solution.py:831
  467.0 46.6 %collective-permute-start.55 = (bf16[1024,512]{1,0:T(8,128)(2,1)}, bf16[1024,512]{1,0:T(8,128)(2,1)}, u32[]{:S(2)}, u32[]{:S(2)}) collective-permute-start(bf16[1024,512]{1,0:T(8,128)(2,1)} %maximum_select_fusion.9), channel_id=1, source_target_pairs={{0,4},{2,6},{4,0},{6,2},{8,12},{10,14},{12,8},{14,10},{16,20},{18,... | collective-permute-start | bytes 3145736 | tf_op jit(solution)/shard_map/ppermute | solution.py:834
  489.2 11.3 %collective-permute-start.44 = (bf16[3,64,512]{2,1,0:T(8,128)(2,1)S(1)}, bf16[3,64,512]{2,1,0:T(8,128)(2,1)S(1)}, u32[]{:S(2)}, u32[]{:S(2)}) collective-permute-start(bf16[3,64,512]{2,1,0:T(8,128)(2,1)S(1)} %add_convert_fusion.15), channel_id=1, source_target_pairs={{0,16},{2,18},{4,20},{6,22},{8,24},{10,26},{12,28},{14,30},{16,0},... | collective-permute-start | bytes 589832 | tf_op jit(solution)/shard_map/ppermute | solution.py:834
  490.1 34.5 %collective-permute-start.52 = (bf16[256,2560]{1,0:T(8,128)(2,1)S(1)}, bf16[256,2560]{1,0:T(8,128)(2,1)}, u32[]{:S(2)}, u32[]{:S(2)}) collective-permute-start(bf16[256,2560]{1,0:T(8,128)(2,1)S(1)} %maximum_select_fusion.8), channel_id=1, source_target_pairs={{0,4},{2,6},{4,0},{6,2},{8,12},{10,14},{12,8},{14,10},{16,20},{18,... | collective-permute-start | bytes 3932168 | tf_op jit(solution)/shard_map/ppermute | solution.py:834
  501.9 9.4 %collective-permute-start.45 = (bf16[3,64,512]{2,1,0:T(8,128)(2,1)S(1)}, bf16[3,64,512]{2,1,0:T(8,128)(2,1)S(1)}, u32[]{:S(2)}, u32[]{:S(2)}) collective-permute-start(bf16[3,64,512]{2,1,0:T(8,128)(2,1)S(1)} %add_convert_fusion.14), channel_id=1, source_target_pairs={{0,16},{2,18},{4,20},{6,22},{8,24},{10,26},{12,28},{14,30},{16,0},... | collective-permute-start | bytes 589832 | tf_op jit(solution)/shard_map/ppermute | solution.py:834
  511.4 11.1 %collective-permute-start.46 = (bf16[3,128,512]{2,1,0:T(8,128)(2,1)S(1)}, bf16[3,128,512]{2,1,0:T(8,128)(2,1)S(1)}, u32[]{:S(2)}, u32[]{:S(2)}) collective-permute-start(bf16[3,128,512]{2,1,0:T(8,128)(2,1)S(1)} %maximum_select_fusion.14), channel_id=1, source_target_pairs={{0,8},{2,10},{4,12},{6,14},{8,0},{10,2},{12,4},{14,6},{16,24},{18,... | collective-permute-start | bytes 1179656 | tf_op jit(solution)/shard_map/ppermute | solution.py:834
  513.0 11.2 %collective-permute-start.40 = (f32[20,1024]{1,0:T(8,128)S(1)}, f32[20,1024]{1,0:T(8,128)S(1)}, u32[]{:S(2)}, u32[]{:S(2)}) collective-permute-start(f32[20,1024]{1,0:T(8,128)S(1)} %add.435), channel_id=1, source_target_pairs={{0,4},{2,6},{4,0},{6,2},{8,12},{10,14},{12,8},{14,10},{16,20},{18,... | collective-permute-start | bytes 245768 | tf_op jit(solution)/shard_map/ppermute | solution.py:834
  517.7 37.3 %collective-permute-start.56 = (bf16[2048,512]{1,0:T(8,128)(2,1)}, bf16[2048,512]{1,0:T(8,128)(2,1)}, u32[]{:S(2)}, u32[]{:S(2)}) collective-permute-start(bf16[2048,512]{1,0:T(8,128)(2,1)} %maximum_select_fusion.6), channel_id=1, source_target_pairs={{0,2},{2,0},{4,6},{6,4},{8,10},{10,8},{12,14},{14,12},{16,18},{18,... | collective-permute-start | bytes 6291464 | tf_op jit(solution)/shard_map/ppermute | solution.py:834
  522.9 18.7 %collective-permute-start.47 = (bf16[3,256,512]{2,1,0:T(8,128)(2,1)S(1)}, bf16[3,256,512]{2,1,0:T(8,128)(2,1)S(1)}, u32[]{:S(2)}, u32[]{:S(2)}) collective-permute-start(bf16[3,256,512]{2,1,0:T(8,128)(2,1)S(1)} %maximum_select_fusion.11), channel_id=1, source_target_pairs={{0,4},{2,6},{4,0},{6,2},{8,12},{10,14},{12,8},{14,10},{16,20},{18,... | collective-permute-start | bytes 2359304 | tf_op jit(solution)/shard_map/ppermute | solution.py:834
  523.6 25.2 %collective-permute-start.38 = (bf16[512,1024]{1,0:T(8,128)(2,1)S(1)}, bf16[512,1024]{1,0:T(8,128)(2,1)S(1)}, u32[]{:S(2)}, u32[]{:S(2)}) collective-permute-start(bf16[512,1024]{1,0:T(8,128)(2,1)S(1)} %get-tuple-element.213), channel_id=1, source_target_pairs={{0,1},{1,0},{2,3},{3,2},{4,5},{5,4},{6,7},{7,6},{8,9},{9,8},{10,11... | collective-permute-start | bytes 3145736 | tf_op jit(solution)/shard_map/ppermute | solution.py:831
  524.2 4.8 collective-permute-start.41
  527.0 40.9 %collective-permute-start.54 = (bf16[512,2048]{1,0:T(8,128)(2,1)S(1)}, bf16[512,2048]{1,0:T(8,128)(2,1)}, u32[]{:S(2)}, u32[]{:S(2)}) collective-permute-start(bf16[512,2048]{1,0:T(8,128)(2,1)S(1)} %slice.138), channel_id=1, source_target_pairs={{0,2},{2,0},{4,6},{6,4},{8,10},{10,8},{12,14},{14,12},{16,18},{18,... | collective-permute-start | bytes 6291464 | tf_op jit(solution)/shard_map/ppermute | solution.py:834
  529.0 16.7 %collective-permute-start.42 = (f32[20,1024]{1,0:T(8,128)S(1)}, f32[20,1024]{1,0:T(8,128)S(1)}, u32[]{:S(2)}, u32[]{:S(2)}) collective-permute-start(f32[20,1024]{1,0:T(8,128)S(1)} %add.437), channel_id=1, source_target_pairs={{0,16},{2,18},{4,20},{6,22},{8,24},{10,26},{12,28},{14,30},{16,0},... | collective-permute-start | bytes 245768 | tf_op jit(solution)/shard_map/ppermute | solution.py:834
  543.3 19.5 %collective-permute-start.48 = (bf16[3,512,512]{2,1,0:T(8,128)(2,1)}, bf16[3,512,512]{2,1,0:T(8,128)(2,1)}, u32[]{:S(2)}, u32[]{:S(2)}) collective-permute-start(bf16[3,512,512]{2,1,0:T(8,128)(2,1)} %maximum_select_fusion.7), channel_id=1, source_target_pairs={{0,2},{2,0},{4,6},{6,4},{8,10},{10,8},{12,14},{14,12},{16,18},{18,... | collective-permute-start | bytes 4718600 | tf_op jit(solution)/shard_map/ppermute | solution.py:834
  547.0 3.4 collective-permute-start.53
  (81 other events, 496.6 us)
